TPU v7x, 32 devices: a whole 2x2x4 slice. The times are simulated.
32 devices in a mesh: dp: 4 (over z), row: 4 (over y, x), col: 2 (over core).
Axes of the slice: x: 2, y: 2, z: 4, core: 2. Of those that a mesh axis runs over, the one named last changes fastest.
Arguments:
- grad_parts: bfloat16 [4, 1, 4, 512, 10240], P('dp', None, 'row', None, 'col'), may hold values from -6 to 6
- params: float32 [1, 4, 512, 10240], P(None, 'row', 'dp', 'col'), may hold values from -6 to 6
- row_second: float32 [1, 4, 512], P(None, 'row'), may hold values from 0.1 to 90
- col_second: float32 [1, 10240], P(None, 'col'), may hold values from 0.02 to 100
Outputs:
- new_params: float32 [1, 4, 512, 10240], P(None, 'row', 'dp', 'col')
- new_row: float32 [1, 4, 512], P(None, 'row', 'dp')
- new_col: float32 [1, 10240], P(None, 'col')
All inputs are finite; a program needn't handle non-finite values.
Results may differ from a plain program's by a relative error of at most 0.0003.
Values sent between devices are 32-bit elements; how exact they have to be, the bound alone decides.
No kernel may reach another device: no remote copies, remote signals or barrier semaphores. Data moves between devices by JAX's collectives and lax.ppermute only.
A program may use at most 64 MiB of HBM per device.

v0:
```python
import jax
import jax.numpy as jnp
from jax import lax
from jax.sharding import PartitionSpec as P

beta_two = 1.0 - 8.0 ** (-0.8)
step_rate = 0.5
tiny_add = 1e-30


def shards(grad_parts, params, row_second, col_second):
    owned_rows = params.shape[2]
    local_cols = params.shape[3]
    slab_rows = row_second.shape[2]
    hidden_width = local_cols * lax.axis_size("col")
    matrix_rows = slab_rows * lax.axis_size("row")
    first_row = lax.axis_index("dp") * owned_rows
    old_owned = lax.dynamic_slice_in_dim(row_second, first_row, owned_rows, 2)
    grad_local = grad_parts[0].astype(jnp.float32)
    gradient = lax.psum_scatter(grad_local, "dp", scatter_dimension=2, tiled=True)
    squares = gradient * gradient + tiny_add
    row_part = jnp.sum(squares, axis=3)
    col_part = jnp.sum(squares, axis=(1, 2))
    row_sum = lax.psum(row_part, "col")
    col_sum = lax.psum(col_part, ("dp", "row"))
    new_row = beta_two * old_owned + (1.0 - beta_two) * (row_sum / hidden_width)
    new_col = beta_two * col_second + (1.0 - beta_two) * (col_sum / matrix_rows)
    row_total = lax.psum(jnp.sum(new_row, axis=(1, 2)), ("dp", "row"))
    row_mean = row_total / matrix_rows
    denominator = new_row[:, :, :, None] * new_col[:, None, None, :] / row_mean[:, None, None, None]
    update = gradient * lax.rsqrt(denominator)
    update_total = lax.psum(jnp.sum(update * update, axis=(1, 2, 3)), ("dp", "row", "col"))
    clip_ratio = jnp.sqrt(update_total / (matrix_rows * hidden_width))
    new_params = params - step_rate * update / jnp.maximum(1.0, clip_ratio)[:, None, None, None]
    return (new_params, new_row, new_col)


def solution(mesh):
    return jax.shard_map(
        shards,
        mesh=mesh,
        in_specs=(
            P("dp", None, "row", None, "col"),
            P(None, "row", "dp", "col"),
            P(None, "row", None),
            P(None, "col"),
        ),
        out_specs=(P(None, "row", "dp", "col"), P(None, "row", "dp"), P(None, "col")),
        check_vma=False,
    )
```

profile of v0, /device:TPU:16, one launch (start us, length us, event | category | flops | bytes accessed | tf_op | source)
XLA Modules:
  0.0 328.3 jit_solution(5967783589630943489)
XLA Ops:
  7.2 0.0 reduce-scatter.2.cloned.1.call-start
  7.2 7.8 %bitcast_convert_fusion = f32[1,1,512,5120]{3,2,1,0:T(8,128)} fusion(bf16[1,1,1,512,5120]{4,3,2,1,0:T(8,128)(2,1)} %param.4), kind=kLoop, calls=%fused_computation | loop fusion | flops 2621440 | bytes 15728640 | tf_op jit(solution)/shard_map/convert_element_type | solution.py:19
  15.0 0.0 reduce-scatter.2.cloned.1.call-update
  15.1 0.0 copy-start.2
  15.1 180.3 %reduce-scatter.2.cloned.1.call-done = f32[1,1,128,5120]{3,2,1,0:T(8,128)} async-done(((f32[1,1,512,5120]{3,2,1,0:T(8,128)}), f32[1,1,128,5120]{3,2,1,0:T(8,128)}) %reduce-scatter.2.cloned.1.call-update) | async-done | bytes 2621456 | tf_op jit(solution)/shard_map/reduce_scatter | solution.py:20
  195.3 0.0 copy-start
  195.3 2.3 fusion
  197.7 2.5 psum.28
  200.1 1.3 fusion.2
  201.4 0.0 copy-start.3
  201.4 63.1 %all-reduce = (f32[1]{0:T(128)}, f32[1,5120]{1,0:T(1,128)S(1)}) all-reduce(f32[1]{0:T(128)} %bitcast.5, f32[1,5120]{1,0:T(1,128)S(1)} %bitcast.13), channel_id=1, replica_groups=mesh['dp'=4,'row'=4,'col'=2] {'dp','row'}, use_global_device_ids=true, to_apply=%region_6.0 | all-reduce | flops 5121 | bytes 40968 | tf_op jit(solution)/shard_map/psum | solution.py:28
  265.1 0.0 copy-done.2
  265.2 0.0 copy-start.1
  265.2 0.0 copy-done
  265.2 1.4 multiply_reduce_fusion
  266.6 50.2 %psum.31 = f32[1]{0:T(128)} all-reduce(f32[1]{0:T(128)} %bitcast.7), channel_id=1, replica_groups=mesh['dp'=4,'row'=4,'col'=2] {'dp','row','col'}, use_global_device_ids=true, to_apply=%region_8.0 | all-reduce | flops 1 | bytes 8 | tf_op jit(solution)/shard_map/psum | solution.py:32
  317.5 3.9 %divide_subtract_fusion = f32[1,1,128,5120]{3,2,1,0:T(8,128)} fusion(f32[1,1,128,5120]{3,2,1,0:T(8,128)} %param.5, f32[]{:T(128)} %bitcast.8, f32[1,1,128,5120]{3,2,1,0:T(8,128)S(1)} %copy-done, f32[]{:T(128)} %bitcast.6, f32[5120]{0:T(1024)S(1)} %bitcast.12, f32[128]{0:T(128)S(1)} %bitcast.15), kind=kLoop, calls=%fused_computation.1 | loop fusion | flops 3932160 | bytes 7885320 | tf_op jit(solution)/shard_map/sub | solution.py:34
  321.4 0.0 copy-done.3
  321.4 0.0 copy-done.1
  (1 shorter events, 0.0 us)
Async XLA Ops:
  7.2 188.2 %reduce-scatter.2.cloned.1.call-start = ((), (), s32[]{:S(2)}) async-start(), calls=%async_computation.1 | async-start | bytes 13107200 | tf_op jit(solution)/shard_map/reduce_scatter | solution.py:20
  15.1 250.1 %copy-start.2 = (f32[1,5120]{1,0:T(1,128)S(1)}, f32[1,5120]{1,0:T(1,128)}, u32[]{:S(2)}) copy-start(f32[1,5120]{1,0:T(1,128)} %param.7) | copy-start | bytes 61444
  195.3 69.9 %copy-start = (f32[1,1,128,5120]{3,2,1,0:T(8,128)S(1)}, f32[1,1,128,5120]{3,2,1,0:T(8,128)}, u32[]{:S(2)}) copy-start(f32[1,1,128,5120]{3,2,1,0:T(8,128)} %reduce-scatter.2.cloned.1.call-done) | copy-start | bytes 7864324
  201.4 120.0 %copy-start.3 = (f32[1,1,128]{2,1,0:T(1,128)}, f32[1,1,128]{2,1,0:T(1,128)S(1)}, u32[]{:S(2)}) copy-start(f32[1,1,128]{2,1,0:T(1,128)S(1)} %get-tuple-element.8) | copy-start | bytes 1540
  265.2 56.2 %copy-start.1 = (f32[1,5120]{1,0:T(1,128)}, f32[1,5120]{1,0:T(1,128)S(1)}, u32[]{:S(2)}) copy-start(f32[1,5120]{1,0:T(1,128)S(1)} %multiply_add_fusion.1) | copy-start | bytes 61444
Sparse Core Ops, SparseCore 0:
  15.2 180.1 reduce-scatter.1
where the time goes:
time: 331 us; the launch traced here: 328 us
  waiting for transfers between devices  180 us (54%)
  blocking collectives  116 us (35%)
  other arithmetic  16.8 us (5%)
  between operations  15.4 us (5%)
    reduce_scatter x1, waiting for transfers between devices, shards(): lax.psum_scatter(grad_local, 'dp', scatter_dimension=2, tiled=True)  180 us
    psum x1, blocking collectives, shards(): row_total = lax.psum(jnp.sum(new_row, axis=(1, 2)), ('dp', 'row'))  63.1 us
    psum x1, blocking collectives, shards(): lax.psum(jnp.sum(update * update, axis=(1, 2, 3)), ('dp', 'row', 'col'))  50.2 us
    convert_element_type x1, other arithmetic, shards(): grad_local = grad_parts[0].astype(jnp.float32)  7.83 us
  transfers between devices with their start and end apart: 1, of which 1 were waited for; matrix products, arithmetic and copies ran while one was open for 0% of the time, Pallas kernels for 0%

commit v1 on v0

v1 whole, which is shorter than its diff:
```python
import jax
import jax.numpy as jnp
from jax import lax
from jax.sharding import PartitionSpec as P

beta_two = 1.0 - 8.0 ** (-0.8)
step_rate = 0.5
tiny_add = 1e-30
pieces = 4


def axis_sum(values, axis):
    size = lax.axis_size(axis)
    hop = 1
    while hop < size:
        pairs = [(i, i ^ hop) for i in range(size)]
        values = values + lax.ppermute(values, axis, pairs)
        hop *= 2
    return values


def shards(grad_parts, params, row_second, col_second):
    owned_rows = params.shape[2]
    local_cols = params.shape[3]
    slab_rows = row_second.shape[2]
    hidden_width = local_cols * lax.axis_size("col")
    matrix_rows = slab_rows * lax.axis_size("row")
    replicas = lax.axis_size("dp")
    place = lax.axis_index("dp")
    piece_rows = owned_rows // pieces
    grad_local = grad_parts.reshape(slab_rows, local_cols)
    weights = params.reshape(owned_rows, local_cols)
    old_rows = lax.dynamic_slice_in_dim(row_second.reshape(slab_rows, 1), place * owned_rows, owned_rows, 0)
    old_cols = col_second.reshape(1, local_cols)

    def own(owner, piece):
        start = jnp.clip(owner, 0, replicas - 1) * owned_rows + piece * piece_rows
        return lax.dynamic_slice_in_dim(grad_local, start, piece_rows, 0).astype(jnp.float32)

    from_left = [None] * pieces
    from_right = [None] * pieces
    for step in range(replicas - 1):
        to_right = [(i, i + 1) for i in range(step + 1)]
        to_left = [(replicas - 1 - i, replicas - 2 - i) for i in range(step + 1)]
        for piece in range(pieces):
            right = own(replicas - 1 - step + place, piece)
            left = own(step - (replicas - 1) + place, piece)
            if step > 0:
                right = right + from_left[piece]
                left = left + from_right[piece]
            from_left[piece] = lax.ppermute(right, "dp", to_right)
            from_right[piece] = lax.ppermute(left, "dp", to_left)

    gradient = []
    new_row = []
    col_part = 0.0
    scaled_part = 0.0
    for piece in range(pieces):
        grad_piece = own(place, piece) + from_left[piece] + from_right[piece]
        squares = grad_piece * grad_piece + tiny_add
        row_sum = axis_sum(jnp.sum(squares, axis=1, keepdims=True), "col")
        old_piece = old_rows[piece * piece_rows : (piece + 1) * piece_rows]
        row_piece = beta_two * old_piece + (1.0 - beta_two) * (row_sum / hidden_width)
        col_part = col_part + jnp.sum(squares, axis=0, keepdims=True)
        scaled_part = scaled_part + jnp.sum(grad_piece * grad_piece / row_piece, axis=0, keepdims=True)
        gradient.append(grad_piece)
        new_row.append(row_piece)
    new_row = jnp.concatenate(new_row, axis=0)
    row_part = jnp.broadcast_to(jnp.sum(new_row), (1, 128))
    packed = jnp.concatenate([col_part, scaled_part, row_part], axis=1)
    packed = axis_sum(axis_sum(packed, "row"), "dp")
    col_sum = packed[:, :local_cols]
    scaled_sum = packed[:, local_cols : 2 * local_cols]
    row_mean = packed[0, 2 * local_cols] / matrix_rows
    new_col = beta_two * old_cols + (1.0 - beta_two) * (col_sum / matrix_rows)
    update_part = jnp.broadcast_to(jnp.sum(scaled_sum / new_col), (1, 128))
    update_total = axis_sum(update_part, "col")[0, 0] * row_mean
    clip_ratio = jnp.sqrt(update_total / (matrix_rows * hidden_width))
    factor = step_rate * jnp.sqrt(row_mean) / jnp.maximum(1.0, clip_ratio)
    row_scale = lax.rsqrt(new_row)
    col_scale = factor * lax.rsqrt(new_col)
    new_params = weights - jnp.concatenate(gradient, axis=0) * row_scale * col_scale
    return (new_params.reshape(params.shape), new_row.reshape(1, 1, owned_rows), new_col)


def solution(mesh):
    return jax.shard_map(
        shards,
        mesh=mesh,
        in_specs=(
            P("dp", None, "row", None, "col"),
            P(None, "row", "dp", "col"),
            P(None, "row", None),
            P(None, "col"),
        ),
        out_specs=(P(None, "row", "dp", "col"), P(None, "row", "dp"), P(None, "col")),
        check_vma=False,
    )
```

time: 331 us -> 249 us (0.75)
  blocking collectives: 116 us -> 0 us
  starting transfers between devices: 0.04 us -> 59.1 us
  waiting for transfers between devices: 180 us -> 151 us
  other arithmetic: 16.8 us -> 29.6 us
  between operations: 15.4 us -> 4.59 us
    reduce_scatter x1 -> x0, waiting for transfers between devices: 180 us -> none  [shards(): lax.psum_scatter(grad_local, 'dp', scatter_dimension=2, tiled=True)]
    ppermute x0 -> x33, waiting for transfers between devices: none -> 151 us  [the longest x12 85.1 us: shards(): from_right[piece] = lax.ppermute(left, 'dp', to_left)]
    psum x3 -> x0, blocking collectives: 116 us -> none  [the longest x1 63.1 us: shards(): row_total = lax.psum(jnp.sum(new_row, axis=(1, 2)), ('dp', 'row'))]
    ppermute x0 -> x33, starting transfers between devices: none -> 59.1 us  [the longest x12 28.3 us: shards(): from_right[piece] = lax.ppermute(left, 'dp', to_left)]
    add x1 -> x11, other arithmetic: 0.04 us -> 10.8 us  [the longest x3 7.82 us: shards(): right = right + from_left[piece]]
    reduce_sum x3 -> x7, other arithmetic: 4.98 us -> 12.8 us  [the longest x3 10.6 us: shards(): row_sum = axis_sum(jnp.sum(squares, axis=1, keepdims=True), 'col')]
    convert_element_type x1, other arithmetic: 7.83 us -> 3.32 us  [own(): lax.dynamic_slice_in_dim(grad_local, start, piece_rows, 0)]
  transfers between devices with their start and end apart: 1 -> 33, of which waited for: 1 -> 21; matrix products, arithmetic and copies ran while one was open for 0% -> 6% of each run, Pallas kernels for 0% -> 0%
where the time goes in v1:
time: 249 us; the launch traced here: 247 us
  waiting for transfers between devices  151 us (61%)
  starting transfers between devices  59.1 us (24%)
  other arithmetic  29.6 us (12%)
  between operations  4.59 us (2%)
    ppermute x12, waiting for transfers between devices, shards(): from_right[piece] = lax.ppermute(left, 'dp', to_left)  85.1 us
    ppermute x12, waiting for transfers between devices, shards(): from_left[piece] = lax.ppermute(right, 'dp', to_right)  52.3 us
    ppermute x12, starting transfers between devices, shards(): from_right[piece] = lax.ppermute(left, 'dp', to_left)  28.3 us
    ppermute x12, starting transfers between devices, shards(): from_left[piece] = lax.ppermute(right, 'dp', to_right)  26 us
    ppermute x9, waiting for transfers between devices, axis_sum(): values = values + lax.ppermute(values, axis, pairs)  13.8 us
    reduce_sum x3, other arithmetic, shards(): row_sum = axis_sum(jnp.sum(squares, axis=1, keepdims=True), 'col')  10.6 us
    add x3, other arithmetic, shards(): right = right + from_left[piece]  7.82 us
  transfers between devices with their start and end apart: 33, of which 21 were waited for; matrix products, arithmetic and copies ran while one was open for 6% of the time, Pallas kernels for 0%

profile of v1, /device:TPU:16, one launch (start us, length us, event | category | flops | bytes accessed | tf_op | source)
XLA Modules:
  0.0 246.7 jit_solution(6801133062336399671)
XLA Ops:
  0.7 3.3 %bitcast_convert_fusion.7 = (f32[32,5120]{1,0:T(8,128)}, f32[32,5120]{1,0:T(8,128)S(1)}, f32[32,5120]{1,0:T(8,128)S(1)}, f32[32,5120]{1,0:T(8,128)S(1)}, f32[32,...) fusion(bf16[1,1,1,512,5120]{4,3,2,1,0:T(8,128)(2,1)} %param.4, ...), kind=kLoop, calls=%fused_computation.46 | loop fusion | flops 1310720 | bytes 7864352 | tf_op jit(solution)/shard_map/convert_element_type | solution.py:38
  8.1 2.1 convert_add_fusion.17
  11.5 13.8 %collective-permute-done.21 = f32[32,5120]{1,0:T(8,128)} collective-permute-done((f32[32,5120]{1,0:T(8,128)}, f32[32,5120]{1,0:T(8,128)}, u32[]{:S(2)}, u32[]{:S(2)}) %collective-permute-start.21) | collective-permute-done | bytes 655392 | tf_op jit(solution)/shard_map/ppermute | solution.py:52
  25.3 12.9 %collective-permute-done.3 = f32[32,5120]{1,0:T(8,128)} collective-permute-done((f32[32,5120]{1,0:T(8,128)}, f32[32,5120]{1,0:T(8,128)}, u32[]{:S(2)}, u32[]{:S(2)}) %collective-permute-start.3) | collective-permute-done | bytes 655392 | tf_op jit(solution)/shard_map/ppermute | solution.py:52
  38.2 3.0 %collective-permute-done.1 = f32[32,5120]{1,0:T(8,128)} collective-permute-done((f32[32,5120]{1,0:T(8,128)}, f32[32,5120]{1,0:T(8,128)}, u32[]{:S(2)}, u32[]{:S(2)}) %collective-permute-start.1) | collective-permute-done | bytes 655392 | tf_op jit(solution)/shard_map/ppermute | solution.py:51
  41.2 3.1 %convert_add_fusion.18 = (f32[32,5120]{1,0:T(8,128)}, f32[32,5120]{1,0:T(8,128)}, f32[32,5120]{1,0:T(8,128)}) fusion(f32[32,5120]{1,0:T(8,128)} %collective-permute-done.1, bf16[1,1,1,512,5120]{4,3,2,1,0:T(8,128)(2,1)} %param.4, s32[]{:T(128)S(6)} %select_n.88, f32[32,5120]{1,0:T(8,128)} %collective-permute-done.3, s32[]{:T(128)S(6)} %select_n.92, ...), kind=kLoop, calls=%fused_computation.24 | loop fusion | flops 983040 | bytes 4915212 | tf_op jit(solution)/shard_map/add | solution.py:49
  44.3 3.6 %collective-permute-start.4 = (f32[32,5120]{1,0:T(8,128)}, f32[32,5120]{1,0:T(8,128)}, u32[]{:S(2)}, u32[]{:S(2)}) collective-permute-start(f32[32,5120]{1,0:T(8,128)} %get-tuple-element.36), channel_id=1, source_target_pairs={{24,16},{16,8},{25,17},{17,9},{26,18},{18,10},{27,19},{19,11},{28,... | collective-permute-start | bytes 1966088 | tf_op jit(solution)/shard_map/ppermute | solution.py:52
  53.8 10.4 %collective-permute-done.4 = f32[32,5120]{1,0:T(8,128)} collective-permute-done((f32[32,5120]{1,0:T(8,128)}, f32[32,5120]{1,0:T(8,128)}, u32[]{:S(2)}, u32[]{:S(2)}) %collective-permute-start.4) | collective-permute-done | bytes 655392 | tf_op jit(solution)/shard_map/ppermute | solution.py:52
  65.5 2.1 convert_add_fusion.16
  67.6 5.4 %collective-permute-start.2 = (f32[32,5120]{1,0:T(8,128)}, f32[32,5120]{1,0:T(8,128)S(1)}, u32[]{:S(2)}, u32[]{:S(2)}) collective-permute-start(f32[32,5120]{1,0:T(8,128)} %get-tuple-element.35), channel_id=1, source_target_pairs={{0,8},{8,16},{16,24},{1,9},{9,17},{17,25},{2,10},{10,18},{18,26},{... | collective-permute-start | bytes 1966088 | tf_op jit(solution)/shard_map/ppermute | solution.py:51
  73.0 5.3 %collective-permute-done.15 = f32[32,5120]{1,0:T(8,128)} collective-permute-done((f32[32,5120]{1,0:T(8,128)S(1)}, f32[32,5120]{1,0:T(8,128)}, u32[]{:S(2)}, u32[]{:S(2)}) %collective-permute-start.15) | collective-permute-done | bytes 655392 | tf_op jit(solution)/shard_map/ppermute | solution.py:52
  80.2 2.8 %collective-permute-start.5 = (f32[32,5120]{1,0:T(8,128)}, f32[32,5120]{1,0:T(8,128)}, u32[]{:S(2)}, u32[]{:S(2)}) collective-permute-start(f32[32,5120]{1,0:T(8,128)} %convert_add_fusion.16), channel_id=1, source_target_pairs={{24,16},{16,8},{8,0},{25,17},{17,9},{9,1},{26,18},{18,10},{10,2},{... | collective-permute-start | bytes 1966088 | tf_op jit(solution)/shard_map/ppermute | solution.py:52
  83.0 9.3 %collective-permute-done.9 = f32[32,5120]{1,0:T(8,128)} collective-permute-done((f32[32,5120]{1,0:T(8,128)S(1)}, f32[32,5120]{1,0:T(8,128)}, u32[]{:S(2)}, u32[]{:S(2)}) %collective-permute-start.9) | collective-permute-done | bytes 655392 | tf_op jit(solution)/shard_map/ppermute | solution.py:52
  92.3 13.9 %collective-permute-done.22 = f32[32,5120]{1,0:T(8,128)S(1)} collective-permute-done((f32[32,5120]{1,0:T(8,128)}, f32[32,5120]{1,0:T(8,128)S(1)}, u32[]{:S(2)}, u32[]{:S(2)}) %collective-permute-start.22) | collective-permute-done | bytes 655392 | tf_op jit(solution)/shard_map/ppermute | solution.py:52
  107.1 10.6 %collective-permute-done.5 = f32[32,5120]{1,0:T(8,128)} collective-permute-done((f32[32,5120]{1,0:T(8,128)}, f32[32,5120]{1,0:T(8,128)}, u32[]{:S(2)}, u32[]{:S(2)}) %collective-permute-start.5) | collective-permute-done | bytes 655392 | tf_op jit(solution)/shard_map/ppermute | solution.py:52
  117.7 4.9 %add_reduce_fusion.7 = (f32[32]{0:T(128)S(1)}, f32[32,5120]{1,0:T(8,128)S(1)}, f32[32,5120]{1,0:T(8,128)S(1)}, f32[32,5120]{1,0:T(8,128)S(1)}, f32[32,5120]{1,0:...) fusion(f32[32,5120]{1,0:T(8,128)} %collective-permute-done.5, ...), kind=kLoop, calls=%fused_computation.38 | loop fusion | flops 2949088 | bytes 12124316 | tf_op jit(solution)/shard_map/reduce_sum | solution.py:61
  127.1 5.2 %collective-permute-start.16 = (f32[32,5120]{1,0:T(8,128)S(1)}, f32[32,5120]{1,0:T(8,128)}, u32[]{:S(2)}, u32[]{:S(2)}) collective-permute-start(f32[32,5120]{1,0:T(8,128)S(1)} %get-tuple-element.31), channel_id=1, source_target_pairs={{24,16},{16,8},{25,17},{17,9},{26,18},{18,10},{27,19},{19,11},{28,... | collective-permute-start | bytes 1966088 | tf_op jit(solution)/shard_map/ppermute | solution.py:52
  133.6 8.9 %collective-permute-done.10 = f32[32,5120]{1,0:T(8,128)} collective-permute-done((f32[32,5120]{1,0:T(8,128)}, f32[32,5120]{1,0:T(8,128)}, u32[]{:S(2)}, u32[]{:S(2)}) %collective-permute-start.10) | collective-permute-done | bytes 655392 | tf_op jit(solution)/shard_map/ppermute | solution.py:52
  144.4 2.6 %convert_add_fusion.13 = (f32[32,5120]{1,0:T(8,128)}, f32[32,5120]{1,0:T(8,128)}) fusion(f32[32,5120]{1,0:T(8,128)} %collective-permute-done.7, bf16[1,1,1,512,5120]{4,3,2,1,0:T(8,128)(2,1)} %param.4, s32[]{:T(128)S(6)} %select_n.95, f32[32,5120]{1,0:T(8,128)} %collective-permute-done.10, s32[]{:T(128)S(6)} %select_n.98), kind=kLoop, calls=%fused_computation.18 | loop fusion | flops 655360 | bytes 3276808 | tf_op jit(solution)/shard_map/add | solution.py:49
  148.9 4.8 %collective-permute-start.8 = (f32[32,5120]{1,0:T(8,128)}, f32[32,5120]{1,0:T(8,128)}, u32[]{:S(2)}, u32[]{:S(2)}) collective-permute-start(f32[32,5120]{1,0:T(8,128)} %get-tuple-element.49), channel_id=1, source_target_pairs={{0,8},{8,16},{16,24},{1,9},{9,17},{17,25},{2,10},{10,18},{18,26},{... | collective-permute-start | bytes 1966088 | tf_op jit(solution)/shard_map/ppermute | solution.py:51
  153.7 4.7 %collective-permute-done.13 = f32[32,5120]{1,0:T(8,128)} collective-permute-done((f32[32,5120]{1,0:T(8,128)S(1)}, f32[32,5120]{1,0:T(8,128)}, u32[]{:S(2)}, u32[]{:S(2)}) %collective-permute-start.13) | collective-permute-done | bytes 655392 | tf_op jit(solution)/shard_map/ppermute | solution.py:51
  160.3 12.1 %collective-permute-done.19 = f32[32,5120]{1,0:T(8,128)} collective-permute-done((f32[32,5120]{1,0:T(8,128)S(1)}, f32[32,5120]{1,0:T(8,128)}, u32[]{:S(2)}, u32[]{:S(2)}) %collective-permute-start.19) | collective-permute-done | bytes 655392 | tf_op jit(solution)/shard_map/ppermute | solution.py:51
  172.5 10.4 %collective-permute-done.8 = f32[32,5120]{1,0:T(8,128)} collective-permute-done((f32[32,5120]{1,0:T(8,128)}, f32[32,5120]{1,0:T(8,128)}, u32[]{:S(2)}, u32[]{:S(2)}) %collective-permute-start.8) | collective-permute-done | bytes 655392 | tf_op jit(solution)/shard_map/ppermute | solution.py:51
  182.9 3.7 %add_reduce_fusion.5 = (f32[32]{0:T(128)S(1)}, f32[32,5120]{1,0:T(8,128)S(1)}, f32[32,5120]{1,0:T(8,128)S(1)}, f32[32,5120]{1,0:T(8,128)}, f32[32,5120]{1,0:T(8,128)}) fusion(f32[32,5120]{1,0:T(8,128)} %collective-permute-done.11, f32[32,5120]{1,0:T(8,128)} %collective-permute-done.8, bf16[1,1,1,512,5120]{4,3,2,1,0:T(8,128)(2,1)} %param.4, s32[]{:T(128)S(6)} %select_n.94, ...), kind=kLoop, calls=%fused_computation.36 | loop fusion | flops 1966048 | bytes 7209104 | tf_op jit(solution)/shard_map/reduce_sum | solution.py:61
  188.5 3.9 %collective-permute-start.17 = (f32[32,5120]{1,0:T(8,128)}, f32[32,5120]{1,0:T(8,128)}, u32[]{:S(2)}, u32[]{:S(2)}) collective-permute-start(f32[32,5120]{1,0:T(8,128)} %get-tuple-element.47), channel_id=1, source_target_pairs={{24,16},{16,8},{8,0},{25,17},{17,9},{9,1},{26,18},{18,10},{10,2},{... | collective-permute-start | bytes 1966088 | tf_op jit(solution)/shard_map/ppermute | solution.py:52
  192.4 2.8 %collective-permute-start.20 = (f32[32,5120]{1,0:T(8,128)S(1)}, f32[32,5120]{1,0:T(8,128)}, u32[]{:S(2)}, u32[]{:S(2)}) collective-permute-start(f32[32,5120]{1,0:T(8,128)S(1)} %get-tuple-element.46), channel_id=1, source_target_pairs={{0,8},{8,16},{16,24},{1,9},{9,17},{17,25},{2,10},{10,18},{18,26},{... | collective-permute-start | bytes 1966088 | tf_op jit(solution)/shard_map/ppermute | solution.py:51
  195.8 10.6 %collective-permute-done.14 = f32[32,5120]{1,0:T(8,128)} collective-permute-done((f32[32,5120]{1,0:T(8,128)}, f32[32,5120]{1,0:T(8,128)}, u32[]{:S(2)}, u32[]{:S(2)}) %collective-permute-start.14) | collective-permute-done | bytes 655392 | tf_op jit(solution)/shard_map/ppermute | solution.py:51
  206.5 9.5 %collective-permute-done.20 = f32[32,5120]{1,0:T(8,128)} collective-permute-done((f32[32,5120]{1,0:T(8,128)S(1)}, f32[32,5120]{1,0:T(8,128)}, u32[]{:S(2)}, u32[]{:S(2)}) %collective-permute-start.20) | collective-permute-done | bytes 655392 | tf_op jit(solution)/shard_map/ppermute | solution.py:51
  225.2 2.5 %collective-permute-done.28 = f32[1,10368]{1,0:T(1,128)S(1)} collective-permute-done((f32[1,10368]{1,0:T(1,128)S(1)}, f32[1,10368]{1,0:T(1,128)S(1)}, u32[]{:S(2)}, u32[]{:S(2)}) %collective-permute-start.28) | collective-permute-done | bytes 41504 | tf_op jit(solution)/shard_map/ppermute | solution.py:17
  229.4 2.5 %collective-permute-done.29 = f32[1,10368]{1,0:T(1,128)S(1)} collective-permute-done((f32[1,10368]{1,0:T(1,128)S(1)}, f32[1,10368]{1,0:T(1,128)S(1)}, u32[]{:S(2)}, u32[]{:S(2)}) %collective-permute-start.29) | collective-permute-done | bytes 41504 | tf_op jit(solution)/shard_map/ppermute | solution.py:17
  232.3 3.7 %collective-permute-done.30 = f32[1,10368]{1,0:T(1,128)S(1)} collective-permute-done((f32[1,10368]{1,0:T(1,128)S(1)}, f32[1,10368]{1,0:T(1,128)S(1)}, u32[]{:S(2)}, u32[]{:S(2)}) %collective-permute-start.30) | collective-permute-done | bytes 41504 | tf_op jit(solution)/shard_map/ppermute | solution.py:17
  236.7 4.3 %collective-permute-done.31 = f32[1,10368]{1,0:T(1,128)S(1)} collective-permute-done((f32[1,10368]{1,0:T(1,128)S(1)}, f32[1,10368]{1,0:T(1,128)S(1)}, u32[]{:S(2)}, u32[]{:S(2)}) %collective-permute-start.31) | collective-permute-done | bytes 41504 | tf_op jit(solution)/shard_map/ppermute | solution.py:17
  (75 shorter events, 43.3 us)
Async XLA Ops:
  4.0 4.1 %collective-permute-start = (f32[32,5120]{1,0:T(8,128)}, f32[32,5120]{1,0:T(8,128)}, u32[]{:S(2)}, u32[]{:S(2)}) collective-permute-start(f32[32,5120]{1,0:T(8,128)} %get-tuple-element.38), channel_id=1, source_target_pairs={{0,8},{1,9},{2,10},{3,11},{4,12},{5,13},{6,14},{7,15}} | collective-permute-start | bytes 1966088 | tf_op jit(solution)/shard_map/ppermute | solution.py:51
  5.5 19.8 %collective-permute-start.21 = (f32[32,5120]{1,0:T(8,128)}, f32[32,5120]{1,0:T(8,128)}, u32[]{:S(2)}, u32[]{:S(2)}) collective-permute-start(f32[32,5120]{1,0:T(8,128)} %get-tuple-element.45), channel_id=1, source_target_pairs={{24,16},{25,17},{26,18},{27,19},{28,20},{29,21},{30,22},{31,23}} | collective-permute-start | bytes 1966088 | tf_op jit(solution)/shard_map/ppermute | solution.py:52
  6.8 31.4 %collective-permute-start.3 = (f32[32,5120]{1,0:T(8,128)}, f32[32,5120]{1,0:T(8,128)}, u32[]{:S(2)}, u32[]{:S(2)}) collective-permute-start(f32[32,5120]{1,0:T(8,128)} %get-tuple-element.44), channel_id=1, source_target_pairs={{24,16},{25,17},{26,18},{27,19},{28,20},{29,21},{30,22},{31,23}} | collective-permute-start | bytes 1966088 | tf_op jit(solution)/shard_map/ppermute | solution.py:52
  10.2 31.1 %collective-permute-start.1 = (f32[32,5120]{1,0:T(8,128)}, f32[32,5120]{1,0:T(8,128)}, u32[]{:S(2)}, u32[]{:S(2)}) collective-permute-start(f32[32,5120]{1,0:T(8,128)} %convert_add_fusion.17), channel_id=1, source_target_pairs={{0,8},{8,16},{1,9},{9,17},{2,10},{10,18},{3,11},{11,19},{4,12},{12... | collective-permute-start | bytes 1966088 | tf_op jit(solution)/shard_map/ppermute | solution.py:51
  44.3 19.9 %collective-permute-start.4 = (f32[32,5120]{1,0:T(8,128)}, f32[32,5120]{1,0:T(8,128)}, u32[]{:S(2)}, u32[]{:S(2)}) collective-permute-start(f32[32,5120]{1,0:T(8,128)} %get-tuple-element.36), channel_id=1, source_target_pairs={{24,16},{16,8},{25,17},{17,9},{26,18},{18,10},{27,19},{19,11},{28,... | collective-permute-start | bytes 1966088 | tf_op jit(solution)/shard_map/ppermute | solution.py:52
  48.0 19.6 %collective-permute-start.12 = (f32[32,5120]{1,0:T(8,128)S(1)}, f32[32,5120]{1,0:T(8,128)}, u32[]{:S(2)}, u32[]{:S(2)}) collective-permute-start(f32[32,5120]{1,0:T(8,128)S(1)} %get-tuple-element.41), channel_id=1, source_target_pairs={{0,8},{1,9},{2,10},{3,11},{4,12},{5,13},{6,14},{7,15}} | collective-permute-start | bytes 1966088 | tf_op jit(solution)/shard_map/ppermute | solution.py:51
  49.5 28.8 %collective-permute-start.15 = (f32[32,5120]{1,0:T(8,128)S(1)}, f32[32,5120]{1,0:T(8,128)}, u32[]{:S(2)}, u32[]{:S(2)}) collective-permute-start(f32[32,5120]{1,0:T(8,128)S(1)} %get-tuple-element.40), channel_id=1, source_target_pairs={{24,16},{25,17},{26,18},{27,19},{28,20},{29,21},{30,22},{31,23}} | collective-permute-start | bytes 1966088 | tf_op jit(solution)/shard_map/ppermute | solution.py:52
  50.8 29.4 %collective-permute-start.18 = (f32[32,5120]{1,0:T(8,128)S(1)}, f32[32,5120]{1,0:T(8,128)}, u32[]{:S(2)}, u32[]{:S(2)}) collective-permute-start(f32[32,5120]{1,0:T(8,128)S(1)} %get-tuple-element.39), channel_id=1, source_target_pairs={{0,8},{1,9},{2,10},{3,11},{4,12},{5,13},{6,14},{7,15}} | collective-permute-start | bytes 1966088 | tf_op jit(solution)/shard_map/ppermute | solution.py:51
  52.3 30.7 %collective-permute-start.6 = (f32[32,5120]{1,0:T(8,128)S(1)}, f32[32,5120]{1,0:T(8,128)}, u32[]{:S(2)}, u32[]{:S(2)}) collective-permute-start(f32[32,5120]{1,0:T(8,128)S(1)} %get-tuple-element.43), channel_id=1, source_target_pairs={{0,8},{1,9},{2,10},{3,11},{4,12},{5,13},{6,14},{7,15}} | collective-permute-start | bytes 1966088 | tf_op jit(solution)/shard_map/ppermute | solution.py:51
  64.2 28.1 %collective-permute-start.9 = (f32[32,5120]{1,0:T(8,128)S(1)}, f32[32,5120]{1,0:T(8,128)}, u32[]{:S(2)}, u32[]{:S(2)}) collective-permute-start(f32[32,5120]{1,0:T(8,128)S(1)} %get-tuple-element.42), channel_id=1, source_target_pairs={{24,16},{25,17},{26,18},{27,19},{28,20},{29,21},{30,22},{31,23}} | collective-permute-start | bytes 1966088 | tf_op jit(solution)/shard_map/ppermute | solution.py:52
  67.6 24.7 %collective-permute-start.2 = (f32[32,5120]{1,0:T(8,128)}, f32[32,5120]{1,0:T(8,128)S(1)}, u32[]{:S(2)}, u32[]{:S(2)}) collective-permute-start(f32[32,5120]{1,0:T(8,128)} %get-tuple-element.35), channel_id=1, source_target_pairs={{0,8},{8,16},{16,24},{1,9},{9,17},{17,25},{2,10},{10,18},{18,26},{... | collective-permute-start | bytes 1966088 | tf_op jit(solution)/shard_map/ppermute | solution.py:51
  78.3 28.0 %collective-permute-start.22 = (f32[32,5120]{1,0:T(8,128)}, f32[32,5120]{1,0:T(8,128)S(1)}, u32[]{:S(2)}, u32[]{:S(2)}) collective-permute-start(f32[32,5120]{1,0:T(8,128)} %get-tuple-element.37), channel_id=1, source_target_pairs={{24,16},{16,8},{25,17},{17,9},{26,18},{18,10},{27,19},{19,11},{28,... | collective-permute-start | bytes 1966088 | tf_op jit(solution)/shard_map/ppermute | solution.py:52
  80.2 37.5 %collective-permute-start.5 = (f32[32,5120]{1,0:T(8,128)}, f32[32,5120]{1,0:T(8,128)}, u32[]{:S(2)}, u32[]{:S(2)}) collective-permute-start(f32[32,5120]{1,0:T(8,128)} %convert_add_fusion.16), channel_id=1, source_target_pairs={{24,16},{16,8},{8,0},{25,17},{17,9},{9,1},{26,18},{18,10},{10,2},{... | collective-permute-start | bytes 1966088 | tf_op jit(solution)/shard_map/ppermute | solution.py:52
  122.6 19.9 %collective-permute-start.10 = (f32[32,5120]{1,0:T(8,128)}, f32[32,5120]{1,0:T(8,128)}, u32[]{:S(2)}, u32[]{:S(2)}) collective-permute-start(f32[32,5120]{1,0:T(8,128)} %get-tuple-element.33), channel_id=1, source_target_pairs={{24,16},{16,8},{25,17},{17,9},{26,18},{18,10},{27,19},{19,11},{28,... | collective-permute-start | bytes 1966088 | tf_op jit(solution)/shard_map/ppermute | solution.py:52
  124.5 19.9 %collective-permute-start.7 = (f32[32,5120]{1,0:T(8,128)}, f32[32,5120]{1,0:T(8,128)}, u32[]{:S(2)}, u32[]{:S(2)}) collective-permute-start(f32[32,5120]{1,0:T(8,128)} %get-tuple-element.34), channel_id=1, source_target_pairs={{0,8},{8,16},{1,9},{9,17},{2,10},{10,18},{3,11},{11,19},{4,12},{12... | collective-permute-start | bytes 1966088 | tf_op jit(solution)/shard_map/ppermute | solution.py:51
  125.8 32.6 %collective-permute-start.13 = (f32[32,5120]{1,0:T(8,128)S(1)}, f32[32,5120]{1,0:T(8,128)}, u32[]{:S(2)}, u32[]{:S(2)}) collective-permute-start(f32[32,5120]{1,0:T(8,128)S(1)} %get-tuple-element.32), channel_id=1, source_target_pairs={{0,8},{8,16},{1,9},{9,17},{2,10},{10,18},{3,11},{11,19},{4,12},{12... | collective-permute-start | bytes 1966088 | tf_op jit(solution)/shard_map/ppermute | solution.py:51
  127.1 33.2 %collective-permute-start.16 = (f32[32,5120]{1,0:T(8,128)S(1)}, f32[32,5120]{1,0:T(8,128)}, u32[]{:S(2)}, u32[]{:S(2)}) collective-permute-start(f32[32,5120]{1,0:T(8,128)S(1)} %get-tuple-element.31), channel_id=1, source_target_pairs={{24,16},{16,8},{25,17},{17,9},{26,18},{18,10},{27,19},{19,11},{28,... | collective-permute-start | bytes 1966088 | tf_op jit(solution)/shard_map/ppermute | solution.py:52
  132.3 40.2 %collective-permute-start.19 = (f32[32,5120]{1,0:T(8,128)S(1)}, f32[32,5120]{1,0:T(8,128)}, u32[]{:S(2)}, u32[]{:S(2)}) collective-permute-start(f32[32,5120]{1,0:T(8,128)S(1)} %get-tuple-element.30), channel_id=1, source_target_pairs={{0,8},{8,16},{1,9},{9,17},{2,10},{10,18},{3,11},{11,19},{4,12},{12... | collective-permute-start | bytes 1966088 | tf_op jit(solution)/shard_map/ppermute | solution.py:51
  147.0 25.4 %collective-permute-start.11 = (f32[32,5120]{1,0:T(8,128)}, f32[32,5120]{1,0:T(8,128)}, u32[]{:S(2)}, u32[]{:S(2)}) collective-permute-start(f32[32,5120]{1,0:T(8,128)} %get-tuple-element.50), channel_id=1, source_target_pairs={{24,16},{16,8},{8,0},{25,17},{17,9},{9,1},{26,18},{18,10},{10,2},{... | collective-permute-start | bytes 1966088 | tf_op jit(solution)/shard_map/ppermute | solution.py:52
  148.9 33.9 %collective-permute-start.8 = (f32[32,5120]{1,0:T(8,128)}, f32[32,5120]{1,0:T(8,128)}, u32[]{:S(2)}, u32[]{:S(2)}) collective-permute-start(f32[32,5120]{1,0:T(8,128)} %get-tuple-element.49), channel_id=1, source_target_pairs={{0,8},{8,16},{16,24},{1,9},{9,17},{17,25},{2,10},{10,18},{18,26},{... | collective-permute-start | bytes 1966088 | tf_op jit(solution)/shard_map/ppermute | solution.py:51
  158.4 36.9 %collective-permute-start.23 = (f32[32,5120]{1,0:T(8,128)S(1)}, f32[32,5120]{1,0:T(8,128)S(1)}, u32[]{:S(2)}, u32[]{:S(2)}) collective-permute-start(f32[32,5120]{1,0:T(8,128)S(1)} %get-tuple-element.29), channel_id=1, source_target_pairs={{24,16},{16,8},{8,0},{25,17},{17,9},{9,1},{26,18},{18,10},{10,2},{... | collective-permute-start | bytes 1966088 | tf_op jit(solution)/shard_map/ppermute | solution.py:52
  186.6 19.9 %collective-permute-start.14 = (f32[32,5120]{1,0:T(8,128)}, f32[32,5120]{1,0:T(8,128)}, u32[]{:S(2)}, u32[]{:S(2)}) collective-permute-start(f32[32,5120]{1,0:T(8,128)} %get-tuple-element.48), channel_id=1, source_target_pairs={{0,8},{8,16},{16,24},{1,9},{9,17},{17,25},{2,10},{10,18},{18,26},{... | collective-permute-start | bytes 1966088 | tf_op jit(solution)/shard_map/ppermute | solution.py:51
  188.5 18.0 %collective-permute-start.17 = (f32[32,5120]{1,0:T(8,128)}, f32[32,5120]{1,0:T(8,128)}, u32[]{:S(2)}, u32[]{:S(2)}) collective-permute-start(f32[32,5120]{1,0:T(8,128)} %get-tuple-element.47), channel_id=1, source_target_pairs={{24,16},{16,8},{8,0},{25,17},{17,9},{9,1},{26,18},{18,10},{10,2},{... | collective-permute-start | bytes 1966088 | tf_op jit(solution)/shard_map/ppermute | solution.py:52
  192.4 23.5 %collective-permute-start.20 = (f32[32,5120]{1,0:T(8,128)S(1)}, f32[32,5120]{1,0:T(8,128)}, u32[]{:S(2)}, u32[]{:S(2)}) collective-permute-start(f32[32,5120]{1,0:T(8,128)S(1)} %get-tuple-element.46), channel_id=1, source_target_pairs={{0,8},{8,16},{16,24},{1,9},{9,17},{17,25},{2,10},{10,18},{18,26},{... | collective-permute-start | bytes 1966088 | tf_op jit(solution)/shard_map/ppermute | solution.py:51
  195.2 23.3 %collective-permute-start.24 = (f32[32,1]{0,1:T(1,128)S(1)}, f32[32,1]{0,1:T(1,128)S(1)}, u32[]{:S(2)}, u32[]{:S(2)}) collective-permute-start(f32[32,1]{0,1:T(1,128)S(1)} %bitcast.142), channel_id=1, source_target_pairs={{0,1},{1,0},{2,3},{3,2},{4,5},{5,4},{6,7},{7,6},{8,9},{9,8},{10,11... | collective-permute-start | bytes 392 | tf_op jit(solution)/shard_map/ppermute | solution.py:17
  195.3 23.3 %collective-permute-start.25 = (f32[32,1]{0,1:T(1,128)S(1)}, f32[32,1]{0,1:T(1,128)S(1)}, u32[]{:S(2)}, u32[]{:S(2)}) collective-permute-start(f32[32,1]{0,1:T(1,128)S(1)} %bitcast.143), channel_id=1, source_target_pairs={{0,1},{1,0},{2,3},{3,2},{4,5},{5,4},{6,7},{7,6},{8,9},{9,8},{10,11... | collective-permute-start | bytes 392 | tf_op jit(solution)/shard_map/ppermute | solution.py:17
  218.1 1.3 collective-permute-start.27
  223.7 4.1 %collective-permute-start.28 = (f32[1,10368]{1,0:T(1,128)S(1)}, f32[1,10368]{1,0:T(1,128)S(1)}, u32[]{:S(2)}, u32[]{:S(2)}) collective-permute-start(f32[1,10368]{1,0:T(1,128)S(1)} %reshape_maximum_fusion), channel_id=1, source_target_pairs={{0,2},{2,0},{4,6},{6,4},{1,3},{3,1},{5,7},{7,5},{8,10},{10,8},{12,... | collective-permute-start | bytes 124424 | tf_op jit(solution)/shard_map/ppermute | solution.py:17
  227.8 4.1 %collective-permute-start.29 = (f32[1,10368]{1,0:T(1,128)S(1)}, f32[1,10368]{1,0:T(1,128)S(1)}, u32[]{:S(2)}, u32[]{:S(2)}) collective-permute-start(f32[1,10368]{1,0:T(1,128)S(1)} %add.530), channel_id=1, source_target_pairs={{0,4},{2,6},{4,0},{6,2},{1,5},{3,7},{5,1},{7,3},{8,12},{10,14},{12... | collective-permute-start | bytes 124424 | tf_op jit(solution)/shard_map/ppermute | solution.py:17
  231.9 4.1 %collective-permute-start.30 = (f32[1,10368]{1,0:T(1,128)S(1)}, f32[1,10368]{1,0:T(1,128)S(1)}, u32[]{:S(2)}, u32[]{:S(2)}) collective-permute-start(f32[1,10368]{1,0:T(1,128)S(1)} %add.531), channel_id=1, source_target_pairs={{0,8},{8,0},{16,24},{24,16},{1,9},{9,1},{17,25},{25,17},{2,10},{10... | collective-permute-start | bytes 124424 | tf_op jit(solution)/shard_map/ppermute | solution.py:17
  236.0 5.0 %collective-permute-start.31 = (f32[1,10368]{1,0:T(1,128)S(1)}, f32[1,10368]{1,0:T(1,128)S(1)}, u32[]{:S(2)}, u32[]{:S(2)}) collective-permute-start(f32[1,10368]{1,0:T(1,128)S(1)} %add.532), channel_id=1, source_target_pairs={{0,16},{8,24},{16,0},{24,8},{1,17},{9,25},{17,1},{25,9},{2,18},{10... | collective-permute-start | bytes 124424 | tf_op jit(solution)/shard_map/ppermute | solution.py:17
  242.4 1.5 collective-permute-start.32
  (7 other events, 260.5 us)

commit v2 on v0

v2 whole, which is shorter than its diff:
```python
import jax
import jax.numpy as jnp
from jax import lax
from jax.experimental import pallas as pl
from jax.experimental.pallas import tpu as pltpu
from jax.sharding import PartitionSpec as P

beta_two = 1.0 - 8.0 ** (-0.8)
step_rate = 0.5
tiny_add = 1e-30
lanes = 128
in_flight = 2
ON_CHIP = pl.BlockSpec(memory_space=pltpu.VMEM)
IN_PLACE = pl.BlockSpec(memory_space=pl.ANY)
limits = pltpu.CompilerParams(vmem_limit_bytes=32 * 1024 * 1024)


def f32(*shape):
    return jax.ShapeDtypeStruct(shape, jnp.float32)


def cost(elements, flops, width):
    return pl.CostEstimate(flops=flops * elements, bytes_accessed=width * elements, transcendentals=0)


def axis_sum(values, axis):
    size = lax.axis_size(axis)
    hop = 1
    while hop < size:
        pairs = [(i, i ^ hop) for i in range(size)]
        values = values + lax.ppermute(values, axis, pairs)
        hop *= 2
    return values


def other_parts(values, axis):
    size = lax.axis_size(axis)
    return [lax.ppermute(values, axis, [(i, (i + k) % size) for i in range(size)]) for k in range(1, size)]


def make_partials(grad, arrived, tokens, owners, replicas, pieces, piece, rows):
    cols = grad.shape[1]

    def body(grad_ref, *refs):
        right_out, left_out, right_own, left_own, sems = refs[-5:]
        place = lax.axis_index("dp")
        copies = []
        for k, own in enumerate((right_own, left_own)):
            owner = jnp.clip(place + owners[k], 0, replicas - 1)
            start = pl.multiple_of((owner * pieces + piece) * rows, rows)
            copies.append(pltpu.make_async_copy(grad_ref.at[pl.ds(start, rows), :], own, sems.at[k]))
            copies[-1].start()
        for k, out in enumerate((right_out, left_out)):
            copies[k].wait()
            values = (right_own, left_own)[k][...].astype(jnp.float32)
            if arrived:
                values = values + refs[k][...]
            out[...] = values

    return pl.pallas_call(
        body,
        out_shape=(f32(rows, cols), f32(rows, cols)),
        in_specs=[IN_PLACE] + [ON_CHIP] * (len(arrived) + len(tokens)),
        out_specs=(ON_CHIP, ON_CHIP),
        scratch_shapes=[
            pltpu.VMEM((rows, cols), grad.dtype),
            pltpu.VMEM((rows, cols), grad.dtype),
            pltpu.SemaphoreType.DMA((2,)),
        ],
        compiler_params=limits,
        cost_estimate=cost(rows * cols, 2, 20),
        name="partials",
    )(grad, *arrived, *tokens)


def finish_piece(own, arrived, tokens, piece, rows):
    cols = own.shape[1]

    def body(own_ref, left_ref, right_ref, *refs):
        grad_ref, row_ref, col_ref = refs[-3:]
        for k in range(cols // lanes):
            at = pl.ds(k * lanes, lanes)
            values = own_ref[piece * rows : (piece + 1) * rows, at].astype(jnp.float32)
            values = values + left_ref[:, at] + right_ref[:, at]
            grad_ref[:, at] = values
            squares = values * values + tiny_add
            row_part = squares if k == 0 else row_part + squares
            col_ref[:, at] = jnp.sum(squares, axis=0, keepdims=True)
        row_ref[...] = row_part

    return pl.pallas_call(
        body,
        out_shape=(f32(rows, cols), f32(rows, lanes), f32(1, cols)),
        in_specs=[ON_CHIP] * (3 + len(tokens)),
        out_specs=(ON_CHIP,) * 3,
        compiler_params=limits,
        cost_estimate=cost(rows * cols, 6, 14),
        name="finish",
    )(own, *arrived, *tokens)


def scale_piece(gradient, row_parts, old_rows, col_part, before, hidden_width, piece, rows):
    cols = gradient.shape[1]
    held = [] if before is None else [before]

    def body(grad_ref, col_ref, old_ref, *refs):
        row_out, sums_out = refs[-2:]
        total = refs[0][...]
        for ref in refs[1 : len(row_parts)]:
            total = total + ref[...]
        row_sum = jnp.sum(total, axis=1, keepdims=True)
        old = old_ref[piece * rows : (piece + 1) * rows, :]
        row = beta_two * old + (1.0 - beta_two) * (row_sum / hidden_width)
        row_out[...] = row
        inverse = 1.0 / row
        row_total = jnp.sum(row, axis=0, keepdims=True)
        end = pl.ds(2 * cols, lanes)
        sums_out[:, end] = refs[len(row_parts)][:, end] + row_total if held else row_total
        for k in range(cols // lanes):
            at = pl.ds(k * lanes, lanes)
            after = pl.ds(cols + k * lanes, lanes)
            values = grad_ref[:, at]
            scaled = jnp.sum(values * values * inverse, axis=0, keepdims=True)
            col = col_ref[:, at]
            if held:
                col = col + refs[len(row_parts)][:, at]
                scaled = scaled + refs[len(row_parts)][:, after]
            sums_out[:, at] = col
            sums_out[:, after] = scaled

    return pl.pallas_call(
        body,
        out_shape=(f32(rows, lanes), f32(1, 2 * cols + lanes)),
        in_specs=[ON_CHIP] * (3 + len(row_parts) + len(held)),
        out_specs=(ON_CHIP, ON_CHIP),
        compiler_params=limits,
        cost_estimate=cost(rows * cols, 4, 4),
        name="scale",
    )(gradient, col_part, old_rows, *row_parts, *held)


def column_factor(sums, old_cols, matrix_rows):
    cols = old_cols.shape[1]

    def body(sums_ref, old_ref, col_out, update_out):
        col = beta_two * old_ref[...] + (1.0 - beta_two) * (sums_ref[:, :cols] / matrix_rows)
        col_out[...] = col
        ratio = sums_ref[:, cols : 2 * cols] / col
        total = ratio[:, :lanes]
        for k in range(1, cols // lanes):
            total = total + ratio[:, k * lanes : (k + 1) * lanes]
        update_out[...] = total

    return pl.pallas_call(
        body,
        out_shape=(f32(1, cols), f32(1, lanes)),
        in_specs=[ON_CHIP] * 2,
        out_specs=(ON_CHIP, ON_CHIP),
        compiler_params=limits,
        cost_estimate=cost(cols, 4, 12),
        name="columns",
    )(sums, old_cols)


def apply_update(weights, gradient, new_row, new_col, sums, updates, matrix_rows, hidden_width):
    rows, cols = gradient[0].shape
    count = len(gradient)

    def body(weights_ref, col_ref, sums_ref, *refs):
        grad_refs = refs[:count]
        row_refs = refs[count : 2 * count]
        update_refs = refs[2 * count : 2 * count + len(updates)]
        out_ref, held, sems = refs[-3:]
        update_total = update_refs[0][...]
        for ref in update_refs[1:]:
            update_total = update_total + ref[...]
        update_total = jnp.sum(update_total, axis=1, keepdims=True)
        row_mean = sums_ref[:, 2 * cols : 2 * cols + 1] / matrix_rows
        clip_ratio = jnp.sqrt(update_total * row_mean / (matrix_rows * hidden_width))
        factor = step_rate * jnp.sqrt(row_mean) / jnp.maximum(1.0, clip_ratio)
        col_scale = factor * lax.rsqrt(col_ref[...])
        copies = []
        for k in range(count):
            here = slice(k * rows, (k + 1) * rows)
            row_scale = lax.rsqrt(row_refs[k][:, :1])
            held[here, :] = weights_ref[here, :] - grad_refs[k][...] * row_scale * col_scale
            copies.append(pltpu.make_async_copy(held.at[here, :], out_ref.at[here, :], sems.at[k]))
            copies[-1].start()
        for copy in copies:
            copy.wait()

    return pl.pallas_call(
        body,
        out_shape=f32(rows * count, cols),
        in_specs=[ON_CHIP] * (3 + 2 * count + len(updates)),
        out_specs=IN_PLACE,
        scratch_shapes=[pltpu.VMEM((rows * count, cols), jnp.float32), pltpu.SemaphoreType.DMA((count,))],
        compiler_params=limits,
        cost_estimate=cost(rows * count * cols, 4, 12),
        name="apply",
    )(weights, new_col, sums, *gradient, *new_row, *updates)


def shards(grad_parts, params, row_second, col_second):
    owned_rows = params.shape[2]
    local_cols = params.shape[3]
    slab_rows = row_second.shape[2]
    hidden_width = local_cols * lax.axis_size("col")
    matrix_rows = slab_rows * lax.axis_size("row")
    replicas = lax.axis_size("dp")
    first_row = lax.axis_index("dp") * owned_rows
    pieces = max(1, min(4, owned_rows // 16))
    piece_rows = owned_rows // pieces
    grad = grad_parts.reshape(slab_rows, local_cols)
    weights = params.reshape(owned_rows, local_cols)
    own = lax.dynamic_slice_in_dim(grad, first_row, owned_rows, 0)
    old_rows = lax.dynamic_slice_in_dim(row_second.reshape(slab_rows, 1), first_row, owned_rows, 0)
    old_rows = jnp.broadcast_to(old_rows, (owned_rows, lanes))
    old_cols = col_second.reshape(1, local_cols)

    slots = []
    for slot in range((replicas - 1) * pieces):
        step, piece = divmod(slot, pieces)
        arrived = slots[slot - pieces] if step else ()
        tokens = slots[slot - in_flight] if slot >= in_flight and in_flight != pieces else ()
        owners = (replicas - 1 - step, step - (replicas - 1))
        right, left = make_partials(grad, arrived, tokens, owners, replicas, pieces, piece, piece_rows)
        to_right = [(i, i + 1) for i in range(step + 1)]
        to_left = [(replicas - 1 - i, replicas - 2 - i) for i in range(step + 1)]
        slots.append((lax.ppermute(right, "dp", to_right), lax.ppermute(left, "dp", to_left)))

    gradient = []
    new_row = []
    sums = None
    for piece in range(pieces):
        arrived = slots[len(slots) - pieces + piece]
        tokens = () if sums is None else (sums,)
        grad_piece, row_part, col_part = finish_piece(own, arrived, tokens, piece, piece_rows)
        row_parts = [row_part] + other_parts(row_part, "col")
        row_piece, sums = scale_piece(
            grad_piece, row_parts, old_rows, col_part, sums, hidden_width, piece, piece_rows
        )
        gradient.append(grad_piece)
        new_row.append(row_piece)
    sums = axis_sum(axis_sum(sums, "row"), "dp")
    new_col, update_part = column_factor(sums, old_cols, matrix_rows)
    updates = [update_part] + other_parts(update_part, "col")
    new_params = apply_update(
        weights, gradient, new_row, new_col, sums, updates, matrix_rows, hidden_width
    )
    new_row = jnp.concatenate([row[:, 0] for row in new_row])
    return (new_params.reshape(params.shape), new_row.reshape(1, 1, owned_rows), new_col)


def solution(mesh):
    return jax.shard_map(
        shards,
        mesh=mesh,
        in_specs=(
            P("dp", None, "row", None, "col"),
            P(None, "row", "dp", "col"),
            P(None, "row", None),
            P(None, "col"),
        ),
        out_specs=(P(None, "row", "dp", "col"), P(None, "row", "dp"), P(None, "col")),
        check_vma=False,
    )
```

time: 331 us -> 202 us (0.61)
  blocking collectives: 116 us -> 0 us
  starting transfers between devices: 0.04 us -> 58.4 us
  waiting for transfers between devices: 180 us -> 123 us
  other arithmetic: 16.8 us -> 0.76 us
  between operations: 15.4 us -> 1.21 us
  Pallas kernels: 0 us -> 9.93 us
  local copies, waits for them, and re-layouts: 0.02 us -> 7.45 us
    reduce_scatter x1 -> x0, waiting for transfers between devices: 180 us -> none  [shards(): lax.psum_scatter(grad_local, 'dp', scatter_dimension=2, tiled=True)]
    ppermute x0 -> x33, waiting for transfers between devices: none -> 123 us  [the longest x12 99.4 us: shards(): lax.ppermute(left, 'dp', to_left)]
    psum x3 -> x0, blocking collectives: 116 us -> none  [the longest x1 63.1 us: shards(): row_total = lax.psum(jnp.sum(new_row, axis=(1, 2)), ('dp', 'row'))]
    ppermute x0 -> x33, starting transfers between devices: none -> 58.4 us  [the longest x12 39.1 us: shards(): lax.ppermute(left, 'dp', to_left)]
    pallas_call x0 -> x22, Pallas kernels: none -> 9.93 us  [the longest x12 6.06 us: make_partials(): pl.pallas_call(body, out_shape=(f32(rows, cols), f32(rows, cols)), in_spe...]
    convert_element_type x1 -> x0, other arithmetic: 7.83 us -> none  [shards(): grad_local = grad_parts[0].astype(jnp.float32)]
    unnamed x8 -> x24, local copies, waits for them, and re-layouts: 0.02 us -> 6.83 us
    reduce_sum x3 -> x0, other arithmetic: 4.98 us -> none  [the longest x1 2.33 us: shards(): col_part = jnp.sum(squares, axis=(1, 2))]
  transfers between devices with their start and end apart: 1 -> 33, of which waited for: 1 -> 22; matrix products, arithmetic and copies ran while one was open for 0% -> 1% of each run, Pallas kernels for 0% -> 3%
where the time goes in v2:
time: 202 us; the launch traced here: 200 us
  waiting for transfers between devices  123 us (61%)
  starting transfers between devices  58.4 us (29%)
  Pallas kernels  9.93 us (5%)
  local copies, waits for them, and re-layouts  7.45 us (4%)
    ppermute x12, waiting for transfers between devices, shards(): lax.ppermute(left, 'dp', to_left)  99.4 us
    ppermute x12, starting transfers between devices, shards(): lax.ppermute(left, 'dp', to_left)  39.1 us
    ppermute x12, starting transfers between devices, shards(): lax.ppermute(right, 'dp', to_right)  15.7 us
    ppermute x4, waiting for transfers between devices, axis_sum(): values = values + lax.ppermute(values, axis, pairs)  13.5 us
    unnamed x24, local copies, waits for them, and re-layouts  6.83 us
    pallas_call x12, Pallas kernels, make_partials(): pl.pallas_call(body, out_shape=(f32(rows, cols), f32(rows, cols)), in_spe...  6.06 us
    ppermute x5, waiting for transfers between devices, other_parts(): lax.ppermute(values, axis, [(i, (i + k) % size) for i in range(size)])  5.03 us
    ppermute x12, waiting for transfers between devices, shards(): lax.ppermute(right, 'dp', to_right)  4.66 us
  transfers between devices with their start and end apart: 33, of which 22 were waited for; matrix products, arithmetic and copies ran while one was open for 1% of the time, Pallas kernels for 3%

profile of v2, /device:TPU:16, one launch (start us, length us, event | category | flops | bytes accessed | tf_op | source)
XLA Modules:
  0.0 200.3 jit_solution(18052911982411152783)
XLA Ops:
  0.7 2.5 %copy-done.1 = bf16[1,1,1,512,5120]{4,3,2,1,0:T(8,128)(2,1)S(1)} copy-done((bf16[1,1,1,512,5120]{4,3,2,1,0:T(8,128)(2,1)S(1)}, bf16[1,1,1,512,5120]{4,3,2,1,0:T(8,128)(2,1)}, u32[]{:S(2)}) %copy-start.1) | copy-done | bytes 5242904
  7.8 15.9 %collective-permute-done.13.refs_1_ = f32[32,5120]{1,0:T(8,128)S(1)} collective-permute-done((f32[32,5120]{1,0:T(8,128)S(1)}, f32[32,5120]{1,0:T(8,128)S(1)}, u32[]{:S(2)}, u32[]{:S(2)}) %collective-permute-start.13) | collective-permute-done | bytes 655392 | tf_op jit(solution)/shard_map/ppermute | solution.py:230
  26.0 11.7 %collective-permute-done.1.refs_1_ = f32[32,5120]{1,0:T(8,128)S(1)} collective-permute-done((f32[32,5120]{1,0:T(8,128)S(1)}, f32[32,5120]{1,0:T(8,128)S(1)}, u32[]{:S(2)}, u32[]{:S(2)}) %collective-permute-start.1) | collective-permute-done | bytes 655392 | tf_op jit(solution)/shard_map/ppermute | solution.py:230
  40.1 11.7 %collective-permute-done.15.refs_3_.refs_1_ = f32[32,5120]{1,0:T(8,128)S(1)} collective-permute-done((f32[32,5120]{1,0:T(8,128)S(1)}, f32[32,5120]{1,0:T(8,128)S(1)}, u32[]{:S(2)}, u32[]{:S(2)}) %collective-permute-start.15) | collective-permute-done | bytes 655392 | tf_op jit(solution)/shard_map/ppermute | solution.py:230
  53.4 4.6 %collective-permute-start.17 = (f32[32,5120]{1,0:T(8,128)S(1)}, f32[32,5120]{1,0:T(8,128)S(1)}, u32[]{:S(2)}, u32[]{:S(2)}) collective-permute-start(f32[32,5120]{1,0:T(8,128)S(1)} %get-tuple-element.66), channel_id=1, source_target_pairs={{24,16},{16,8},{25,17},{17,9},{26,18},{18,10},{27,19},{19,11},{28,... | collective-permute-start | bytes 1966088 | tf_op jit(solution)/shard_map/ppermute | solution.py:230
  58.0 7.8 %collective-permute-done.3.refs_3_.refs_1_ = f32[32,5120]{1,0:T(8,128)S(1)} collective-permute-done((f32[32,5120]{1,0:T(8,128)S(1)}, f32[32,5120]{1,0:T(8,128)S(1)}, u32[]{:S(2)}, u32[]{:S(2)}) %collective-permute-start.3) | collective-permute-done | bytes 655392 | tf_op jit(solution)/shard_map/ppermute | solution.py:230
  67.5 4.6 %collective-permute-start.5 = (f32[32,5120]{1,0:T(8,128)S(1)}, f32[32,5120]{1,0:T(8,128)S(1)}, u32[]{:S(2)}, u32[]{:S(2)}) collective-permute-start(f32[32,5120]{1,0:T(8,128)S(1)} %get-tuple-element.54), channel_id=1, source_target_pairs={{24,16},{16,8},{25,17},{17,9},{26,18},{18,10},{27,19},{19,11},{28,... | collective-permute-start | bytes 1966088 | tf_op jit(solution)/shard_map/ppermute | solution.py:230
  72.0 7.8 %collective-permute-done.17.refs_3_.refs_1_ = f32[32,5120]{1,0:T(8,128)S(1)} collective-permute-done((f32[32,5120]{1,0:T(8,128)S(1)}, f32[32,5120]{1,0:T(8,128)S(1)}, u32[]{:S(2)}, u32[]{:S(2)}) %collective-permute-start.17) | collective-permute-done | bytes 655392 | tf_op jit(solution)/shard_map/ppermute | solution.py:230
  81.5 4.6 %collective-permute-start.19 = (f32[32,5120]{1,0:T(8,128)S(1)}, f32[32,5120]{1,0:T(8,128)S(1)}, u32[]{:S(2)}, u32[]{:S(2)}) collective-permute-start(f32[32,5120]{1,0:T(8,128)S(1)} %get-tuple-element.68), channel_id=1, source_target_pairs={{24,16},{16,8},{25,17},{17,9},{26,18},{18,10},{27,19},{19,11},{28,... | collective-permute-start | bytes 1966088 | tf_op jit(solution)/shard_map/ppermute | solution.py:230
  86.1 7.8 %collective-permute-done.5.refs_3_.refs_1_ = f32[32,5120]{1,0:T(8,128)S(1)} collective-permute-done((f32[32,5120]{1,0:T(8,128)S(1)}, f32[32,5120]{1,0:T(8,128)S(1)}, u32[]{:S(2)}, u32[]{:S(2)}) %collective-permute-start.5) | collective-permute-done | bytes 655392 | tf_op jit(solution)/shard_map/ppermute | solution.py:230
  95.6 4.6 %collective-permute-start.7 = (f32[32,5120]{1,0:T(8,128)S(1)}, f32[32,5120]{1,0:T(8,128)S(1)}, u32[]{:S(2)}, u32[]{:S(2)}) collective-permute-start(f32[32,5120]{1,0:T(8,128)S(1)} %get-tuple-element.56), channel_id=1, source_target_pairs={{24,16},{16,8},{25,17},{17,9},{26,18},{18,10},{27,19},{19,11},{28,... | collective-permute-start | bytes 1966088 | tf_op jit(solution)/shard_map/ppermute | solution.py:230
  100.1 7.8 %collective-permute-done.19.refs_3_.refs_1_ = f32[32,5120]{1,0:T(8,128)S(1)} collective-permute-done((f32[32,5120]{1,0:T(8,128)S(1)}, f32[32,5120]{1,0:T(8,128)S(1)}, u32[]{:S(2)}, u32[]{:S(2)}) %collective-permute-start.19) | collective-permute-done | bytes 655392 | tf_op jit(solution)/shard_map/ppermute | solution.py:230
  109.3 1.9 collective-permute-start.20
  111.3 3.9 %collective-permute-start.21 = (f32[32,5120]{1,0:T(8,128)}, f32[32,5120]{1,0:T(8,128)S(1)}, u32[]{:S(2)}, u32[]{:S(2)}) collective-permute-start(f32[32,5120]{1,0:T(8,128)} %get-tuple-element.70), channel_id=1, source_target_pairs={{24,16},{16,8},{8,0},{25,17},{17,9},{9,1},{26,18},{18,10},{10,2},{... | collective-permute-start | bytes 1966088 | tf_op jit(solution)/shard_map/ppermute | solution.py:230
  115.2 6.8 %collective-permute-done.7.refs_3_.refs_1_ = f32[32,5120]{1,0:T(8,128)S(1)} collective-permute-done((f32[32,5120]{1,0:T(8,128)S(1)}, f32[32,5120]{1,0:T(8,128)S(1)}, u32[]{:S(2)}, u32[]{:S(2)}) %collective-permute-start.7) | collective-permute-done | bytes 655392 | tf_op jit(solution)/shard_map/ppermute | solution.py:230
  123.4 1.9 collective-permute-start.8
  125.3 3.9 %collective-permute-start.9 = (f32[32,5120]{1,0:T(8,128)}, f32[32,5120]{1,0:T(8,128)S(1)}, u32[]{:S(2)}, u32[]{:S(2)}) collective-permute-start(f32[32,5120]{1,0:T(8,128)} %get-tuple-element.58), channel_id=1, source_target_pairs={{24,16},{16,8},{8,0},{25,17},{17,9},{9,1},{26,18},{18,10},{10,2},{... | collective-permute-start | bytes 1966088 | tf_op jit(solution)/shard_map/ppermute | solution.py:230
  129.2 6.8 %collective-permute-done.21.refs_3_.right_ref = f32[32,5120]{1,0:T(8,128)S(1)} collective-permute-done((f32[32,5120]{1,0:T(8,128)}, f32[32,5120]{1,0:T(8,128)S(1)}, u32[]{:S(2)}, u32[]{:S(2)}) %collective-permute-start.21) | collective-permute-done | bytes 655392 | tf_op jit(solution)/shard_map/ppermute | solution.py:230
  136.0 2.5 %copy-done.2 = bf16[1,1,1,512,5120]{4,3,2,1,0:T(8,128)(2,1)S(1)} copy-done((bf16[1,1,1,512,5120]{4,3,2,1,0:T(8,128)(2,1)S(1)}, bf16[1,1,1,512,5120]{4,3,2,1,0:T(8,128)(2,1)}, u32[]{:S(2)}) %copy-start.2) | copy-done | bytes 5242904
  140.0 1.9 collective-permute-start.22
  141.9 3.9 %collective-permute-start.23 = (f32[32,5120]{1,0:T(8,128)S(1)}, f32[32,5120]{1,0:T(8,128)S(1)}, u32[]{:S(2)}, u32[]{:S(2)}) collective-permute-start(f32[32,5120]{1,0:T(8,128)S(1)} %get-tuple-element.72), channel_id=1, source_target_pairs={{24,16},{16,8},{8,0},{25,17},{17,9},{9,1},{26,18},{18,10},{10,2},{... | collective-permute-start | bytes 1966088 | tf_op jit(solution)/shard_map/ppermute | solution.py:230
  145.9 4.2 %collective-permute-done.9.refs_3_.right_ref = f32[32,5120]{1,0:T(8,128)S(1)} collective-permute-done((f32[32,5120]{1,0:T(8,128)}, f32[32,5120]{1,0:T(8,128)S(1)}, u32[]{:S(2)}, u32[]{:S(2)}) %collective-permute-start.9) | collective-permute-done | bytes 655392 | tf_op jit(solution)/shard_map/ppermute | solution.py:230
  150.4 1.9 collective-permute-start.10
  152.4 3.9 %collective-permute-start.11 = (f32[32,5120]{1,0:T(8,128)S(1)}, f32[32,5120]{1,0:T(8,128)S(1)}, u32[]{:S(2)}, u32[]{:S(2)}) collective-permute-start(f32[32,5120]{1,0:T(8,128)S(1)} %get-tuple-element.60), channel_id=1, source_target_pairs={{24,16},{16,8},{8,0},{25,17},{17,9},{9,1},{26,18},{18,10},{10,2},{... | collective-permute-start | bytes 1966088 | tf_op jit(solution)/shard_map/ppermute | solution.py:230
  159.7 4.4 %collective-permute-done.23.right_ref = f32[32,5120]{1,0:T(8,128)S(1)} collective-permute-done((f32[32,5120]{1,0:T(8,128)S(1)}, f32[32,5120]{1,0:T(8,128)S(1)}, u32[]{:S(2)}, u32[]{:S(2)}) %collective-permute-start.23) | collective-permute-done | bytes 655392 | tf_op jit(solution)/shard_map/ppermute | solution.py:230
  165.8 4.6 %collective-permute-done.10.left_ref = f32[32,5120]{1,0:T(8,128)S(1)} collective-permute-done((f32[32,5120]{1,0:T(8,128)S(1)}, f32[32,5120]{1,0:T(8,128)S(1)}, u32[]{:S(2)}, u32[]{:S(2)}) %collective-permute-start.10) | collective-permute-done | bytes 655392 | tf_op jit(solution)/shard_map/ppermute | solution.py:230
  170.4 6.6 %collective-permute-done.11.right_ref = f32[32,5120]{1,0:T(8,128)S(1)} collective-permute-done((f32[32,5120]{1,0:T(8,128)S(1)}, f32[32,5120]{1,0:T(8,128)S(1)}, u32[]{:S(2)}, u32[]{:S(2)}) %collective-permute-start.11) | collective-permute-done | bytes 655392 | tf_op jit(solution)/shard_map/ppermute | solution.py:230
  180.3 2.4 %collective-permute-done.28 = f32[1,10368]{1,0:T(1,128)S(1)} collective-permute-done((f32[1,10368]{1,0:T(1,128)S(1)}, f32[1,10368]{1,0:T(1,128)S(1)}, u32[]{:S(2)}, u32[]{:S(2)}) %collective-permute-start.28) | collective-permute-done | bytes 41504 | tf_op jit(solution)/shard_map/ppermute | solution.py:31
  184.4 2.4 %collective-permute-done.29 = f32[1,10368]{1,0:T(1,128)S(1)} collective-permute-done((f32[1,10368]{1,0:T(1,128)S(1)}, f32[1,10368]{1,0:T(1,128)S(1)}, u32[]{:S(2)}, u32[]{:S(2)}) %collective-permute-start.29) | collective-permute-done | bytes 41504 | tf_op jit(solution)/shard_map/ppermute | solution.py:31
  187.1 3.9 %collective-permute-done.30 = f32[1,10368]{1,0:T(1,128)S(1)} collective-permute-done((f32[1,10368]{1,0:T(1,128)S(1)}, f32[1,10368]{1,0:T(1,128)S(1)}, u32[]{:S(2)}, u32[]{:S(2)}) %collective-permute-start.30) | collective-permute-done | bytes 41504 | tf_op jit(solution)/shard_map/ppermute | solution.py:31
  191.2 4.8 %collective-permute-done.31 = f32[1,10368]{1,0:T(1,128)S(1)} collective-permute-done((f32[1,10368]{1,0:T(1,128)S(1)}, f32[1,10368]{1,0:T(1,128)S(1)}, u32[]{:S(2)}, u32[]{:S(2)}) %collective-permute-start.31) | collective-permute-done | bytes 41504 | tf_op jit(solution)/shard_map/ppermute | solution.py:31
  198.5 1.8 apply.1
  (92 shorter events, 33.3 us)
Async XLA Ops:
  3.5 4.4 %collective-permute-start.12 = (f32[32,5120]{1,0:T(8,128)S(1)}, f32[32,5120]{1,0:T(8,128)S(1)}, u32[]{:S(2)}, u32[]{:S(2)}) collective-permute-start(f32[32,5120]{1,0:T(8,128)S(1)} %get-tuple-element.61), channel_id=1, source_target_pairs={{0,8},{1,9},{2,10},{3,11},{4,12},{5,13},{6,14},{7,15}} | collective-permute-start | bytes 1966088 | tf_op jit(solution)/shard_map/ppermute | solution.py:230
  4.2 19.5 %collective-permute-start.13 = (f32[32,5120]{1,0:T(8,128)S(1)}, f32[32,5120]{1,0:T(8,128)S(1)}, u32[]{:S(2)}, u32[]{:S(2)}) collective-permute-start(f32[32,5120]{1,0:T(8,128)S(1)} %get-tuple-element.62), channel_id=1, source_target_pairs={{24,16},{25,17},{26,18},{27,19},{28,20},{29,21},{30,22},{31,23}} | collective-permute-start | bytes 1966088 | tf_op jit(solution)/shard_map/ppermute | solution.py:230
  5.8 20.2 %collective-permute-start = (f32[32,5120]{1,0:T(8,128)S(1)}, f32[32,5120]{1,0:T(8,128)S(1)}, u32[]{:S(2)}, u32[]{:S(2)}) collective-permute-start(f32[32,5120]{1,0:T(8,128)S(1)} %get-tuple-element.49), channel_id=1, source_target_pairs={{0,8},{1,9},{2,10},{3,11},{4,12},{5,13},{6,14},{7,15}} | collective-permute-start | bytes 1966088 | tf_op jit(solution)/shard_map/ppermute | solution.py:230
  6.5 31.2 %collective-permute-start.1 = (f32[32,5120]{1,0:T(8,128)S(1)}, f32[32,5120]{1,0:T(8,128)S(1)}, u32[]{:S(2)}, u32[]{:S(2)}) collective-permute-start(f32[32,5120]{1,0:T(8,128)S(1)} %get-tuple-element.50), channel_id=1, source_target_pairs={{24,16},{25,17},{26,18},{27,19},{28,20},{29,21},{30,22},{31,23}} | collective-permute-start | bytes 1966088 | tf_op jit(solution)/shard_map/ppermute | solution.py:230
  24.0 16.1 %collective-permute-start.14 = (f32[32,5120]{1,0:T(8,128)S(1)}, f32[32,5120]{1,0:T(8,128)S(1)}, u32[]{:S(2)}, u32[]{:S(2)}) collective-permute-start(f32[32,5120]{1,0:T(8,128)S(1)} %get-tuple-element.63), channel_id=1, source_target_pairs={{0,8},{1,9},{2,10},{3,11},{4,12},{5,13},{6,14},{7,15}} | collective-permute-start | bytes 1966088 | tf_op jit(solution)/shard_map/ppermute | solution.py:230
  24.7 27.1 %collective-permute-start.15 = (f32[32,5120]{1,0:T(8,128)S(1)}, f32[32,5120]{1,0:T(8,128)S(1)}, u32[]{:S(2)}, u32[]{:S(2)}) collective-permute-start(f32[32,5120]{1,0:T(8,128)S(1)} %get-tuple-element.64), channel_id=1, source_target_pairs={{24,16},{25,17},{26,18},{27,19},{28,20},{29,21},{30,22},{31,23}} | collective-permute-start | bytes 1966088 | tf_op jit(solution)/shard_map/ppermute | solution.py:230
  38.0 19.9 %collective-permute-start.2 = (f32[32,5120]{1,0:T(8,128)S(1)}, f32[32,5120]{1,0:T(8,128)S(1)}, u32[]{:S(2)}, u32[]{:S(2)}) collective-permute-start(f32[32,5120]{1,0:T(8,128)S(1)} %get-tuple-element.51), channel_id=1, source_target_pairs={{0,8},{1,9},{2,10},{3,11},{4,12},{5,13},{6,14},{7,15}} | collective-permute-start | bytes 1966088 | tf_op jit(solution)/shard_map/ppermute | solution.py:230
  38.7 27.1 %collective-permute-start.3 = (f32[32,5120]{1,0:T(8,128)S(1)}, f32[32,5120]{1,0:T(8,128)S(1)}, u32[]{:S(2)}, u32[]{:S(2)}) collective-permute-start(f32[32,5120]{1,0:T(8,128)S(1)} %get-tuple-element.52), channel_id=1, source_target_pairs={{24,16},{25,17},{26,18},{27,19},{28,20},{29,21},{30,22},{31,23}} | collective-permute-start | bytes 1966088 | tf_op jit(solution)/shard_map/ppermute | solution.py:230
  52.1 19.9 %collective-permute-start.16 = (f32[32,5120]{1,0:T(8,128)S(1)}, f32[32,5120]{1,0:T(8,128)S(1)}, u32[]{:S(2)}, u32[]{:S(2)}) collective-permute-start(f32[32,5120]{1,0:T(8,128)S(1)} %get-tuple-element.65), channel_id=1, source_target_pairs={{0,8},{8,16},{1,9},{9,17},{2,10},{10,18},{3,11},{11,19},{4,12},{12... | collective-permute-start | bytes 1966088 | tf_op jit(solution)/shard_map/ppermute | solution.py:230
  53.4 26.4 %collective-permute-start.17 = (f32[32,5120]{1,0:T(8,128)S(1)}, f32[32,5120]{1,0:T(8,128)S(1)}, u32[]{:S(2)}, u32[]{:S(2)}) collective-permute-start(f32[32,5120]{1,0:T(8,128)S(1)} %get-tuple-element.66), channel_id=1, source_target_pairs={{24,16},{16,8},{25,17},{17,9},{26,18},{18,10},{27,19},{19,11},{28,... | collective-permute-start | bytes 1966088 | tf_op jit(solution)/shard_map/ppermute | solution.py:230
  66.2 19.9 %collective-permute-start.4 = (f32[32,5120]{1,0:T(8,128)S(1)}, f32[32,5120]{1,0:T(8,128)S(1)}, u32[]{:S(2)}, u32[]{:S(2)}) collective-permute-start(f32[32,5120]{1,0:T(8,128)S(1)} %get-tuple-element.53), channel_id=1, source_target_pairs={{0,8},{8,16},{1,9},{9,17},{2,10},{10,18},{3,11},{11,19},{4,12},{12... | collective-permute-start | bytes 1966088 | tf_op jit(solution)/shard_map/ppermute | solution.py:230
  67.5 26.4 %collective-permute-start.5 = (f32[32,5120]{1,0:T(8,128)S(1)}, f32[32,5120]{1,0:T(8,128)S(1)}, u32[]{:S(2)}, u32[]{:S(2)}) collective-permute-start(f32[32,5120]{1,0:T(8,128)S(1)} %get-tuple-element.54), channel_id=1, source_target_pairs={{24,16},{16,8},{25,17},{17,9},{26,18},{18,10},{27,19},{19,11},{28,... | collective-permute-start | bytes 1966088 | tf_op jit(solution)/shard_map/ppermute | solution.py:230
  80.2 19.9 %collective-permute-start.18 = (f32[32,5120]{1,0:T(8,128)S(1)}, f32[32,5120]{1,0:T(8,128)S(1)}, u32[]{:S(2)}, u32[]{:S(2)}) collective-permute-start(f32[32,5120]{1,0:T(8,128)S(1)} %get-tuple-element.67), channel_id=1, source_target_pairs={{0,8},{8,16},{1,9},{9,17},{2,10},{10,18},{3,11},{11,19},{4,12},{12... | collective-permute-start | bytes 1966088 | tf_op jit(solution)/shard_map/ppermute | solution.py:230
  81.5 26.4 %collective-permute-start.19 = (f32[32,5120]{1,0:T(8,128)S(1)}, f32[32,5120]{1,0:T(8,128)S(1)}, u32[]{:S(2)}, u32[]{:S(2)}) collective-permute-start(f32[32,5120]{1,0:T(8,128)S(1)} %get-tuple-element.68), channel_id=1, source_target_pairs={{24,16},{16,8},{25,17},{17,9},{26,18},{18,10},{27,19},{19,11},{28,... | collective-permute-start | bytes 1966088 | tf_op jit(solution)/shard_map/ppermute | solution.py:230
  94.3 20.9 %collective-permute-start.6 = (f32[32,5120]{1,0:T(8,128)S(1)}, f32[32,5120]{1,0:T(8,128)S(1)}, u32[]{:S(2)}, u32[]{:S(2)}) collective-permute-start(f32[32,5120]{1,0:T(8,128)S(1)} %get-tuple-element.55), channel_id=1, source_target_pairs={{0,8},{8,16},{1,9},{9,17},{2,10},{10,18},{3,11},{11,19},{4,12},{12... | collective-permute-start | bytes 1966088 | tf_op jit(solution)/shard_map/ppermute | solution.py:230
  95.6 26.4 %collective-permute-start.7 = (f32[32,5120]{1,0:T(8,128)S(1)}, f32[32,5120]{1,0:T(8,128)S(1)}, u32[]{:S(2)}, u32[]{:S(2)}) collective-permute-start(f32[32,5120]{1,0:T(8,128)S(1)} %get-tuple-element.56), channel_id=1, source_target_pairs={{24,16},{16,8},{25,17},{17,9},{26,18},{18,10},{27,19},{19,11},{28,... | collective-permute-start | bytes 1966088 | tf_op jit(solution)/shard_map/ppermute | solution.py:230
  109.3 19.9 %collective-permute-start.20 = (f32[32,5120]{1,0:T(8,128)}, f32[32,5120]{1,0:T(8,128)S(1)}, u32[]{:S(2)}, u32[]{:S(2)}) collective-permute-start(f32[32,5120]{1,0:T(8,128)} %get-tuple-element.69), channel_id=1, source_target_pairs={{0,8},{8,16},{16,24},{1,9},{9,17},{17,25},{2,10},{10,18},{18,26},{... | collective-permute-start | bytes 1966088 | tf_op jit(solution)/shard_map/ppermute | solution.py:230
  111.3 24.8 %collective-permute-start.21 = (f32[32,5120]{1,0:T(8,128)}, f32[32,5120]{1,0:T(8,128)S(1)}, u32[]{:S(2)}, u32[]{:S(2)}) collective-permute-start(f32[32,5120]{1,0:T(8,128)} %get-tuple-element.70), channel_id=1, source_target_pairs={{24,16},{16,8},{8,0},{25,17},{17,9},{9,1},{26,18},{18,10},{10,2},{... | collective-permute-start | bytes 1966088 | tf_op jit(solution)/shard_map/ppermute | solution.py:230
  123.4 22.5 %collective-permute-start.8 = (f32[32,5120]{1,0:T(8,128)}, f32[32,5120]{1,0:T(8,128)S(1)}, u32[]{:S(2)}, u32[]{:S(2)}) collective-permute-start(f32[32,5120]{1,0:T(8,128)} %get-tuple-element.57), channel_id=1, source_target_pairs={{0,8},{8,16},{16,24},{1,9},{9,17},{17,25},{2,10},{10,18},{18,26},{... | collective-permute-start | bytes 1966088 | tf_op jit(solution)/shard_map/ppermute | solution.py:230
  125.3 24.8 %collective-permute-start.9 = (f32[32,5120]{1,0:T(8,128)}, f32[32,5120]{1,0:T(8,128)S(1)}, u32[]{:S(2)}, u32[]{:S(2)}) collective-permute-start(f32[32,5120]{1,0:T(8,128)} %get-tuple-element.58), channel_id=1, source_target_pairs={{24,16},{16,8},{8,0},{25,17},{17,9},{9,1},{26,18},{18,10},{10,2},{... | collective-permute-start | bytes 1966088 | tf_op jit(solution)/shard_map/ppermute | solution.py:230
  140.0 19.7 %collective-permute-start.22 = (f32[32,5120]{1,0:T(8,128)S(1)}, f32[32,5120]{1,0:T(8,128)S(1)}, u32[]{:S(2)}, u32[]{:S(2)}) collective-permute-start(f32[32,5120]{1,0:T(8,128)S(1)} %get-tuple-element.71), channel_id=1, source_target_pairs={{0,8},{8,16},{16,24},{1,9},{9,17},{17,25},{2,10},{10,18},{18,26},{... | collective-permute-start | bytes 1966088 | tf_op jit(solution)/shard_map/ppermute | solution.py:230
  141.9 22.2 %collective-permute-start.23 = (f32[32,5120]{1,0:T(8,128)S(1)}, f32[32,5120]{1,0:T(8,128)S(1)}, u32[]{:S(2)}, u32[]{:S(2)}) collective-permute-start(f32[32,5120]{1,0:T(8,128)S(1)} %get-tuple-element.72), channel_id=1, source_target_pairs={{24,16},{16,8},{8,0},{25,17},{17,9},{9,1},{26,18},{18,10},{10,2},{... | collective-permute-start | bytes 1966088 | tf_op jit(solution)/shard_map/ppermute | solution.py:230
  150.4 20.0 %collective-permute-start.10 = (f32[32,5120]{1,0:T(8,128)S(1)}, f32[32,5120]{1,0:T(8,128)S(1)}, u32[]{:S(2)}, u32[]{:S(2)}) collective-permute-start(f32[32,5120]{1,0:T(8,128)S(1)} %get-tuple-element.59), channel_id=1, source_target_pairs={{0,8},{8,16},{16,24},{1,9},{9,17},{17,25},{2,10},{10,18},{18,26},{... | collective-permute-start | bytes 1966088 | tf_op jit(solution)/shard_map/ppermute | solution.py:230
  152.4 24.7 %collective-permute-start.11 = (f32[32,5120]{1,0:T(8,128)S(1)}, f32[32,5120]{1,0:T(8,128)S(1)}, u32[]{:S(2)}, u32[]{:S(2)}) collective-permute-start(f32[32,5120]{1,0:T(8,128)S(1)} %get-tuple-element.60), channel_id=1, source_target_pairs={{24,16},{16,8},{8,0},{25,17},{17,9},{9,1},{26,18},{18,10},{10,2},{... | collective-permute-start | bytes 1966088 | tf_op jit(solution)/shard_map/ppermute | solution.py:230
  156.6 1.2 collective-permute-start.24
  158.3 1.2 collective-permute-start.25
  164.3 1.2 collective-permute-start.26
  177.2 1.2 collective-permute-start.27
  178.6 4.1 %collective-permute-start.28 = (f32[1,10368]{1,0:T(1,128)S(1)}, f32[1,10368]{1,0:T(1,128)S(1)}, u32[]{:S(2)}, u32[]{:S(2)}) collective-permute-start(f32[1,10368]{1,0:T(1,128)S(1)} %get-tuple-element.88), channel_id=1, source_target_pairs={{0,2},{2,0},{4,6},{6,4},{1,3},{3,1},{5,7},{7,5},{8,10},{10,8},{12,... | collective-permute-start | bytes 124424 | tf_op jit(solution)/shard_map/ppermute | solution.py:31
  182.7 4.1 %collective-permute-start.29 = (f32[1,10368]{1,0:T(1,128)S(1)}, f32[1,10368]{1,0:T(1,128)S(1)}, u32[]{:S(2)}, u32[]{:S(2)}) collective-permute-start(f32[1,10368]{1,0:T(1,128)S(1)} %add.17), channel_id=1, source_target_pairs={{0,4},{2,6},{4,0},{6,2},{1,5},{3,7},{5,1},{7,3},{8,12},{10,14},{12... | collective-permute-start | bytes 124424 | tf_op jit(solution)/shard_map/ppermute | solution.py:31
  186.9 4.1 %collective-permute-start.30 = (f32[1,10368]{1,0:T(1,128)S(1)}, f32[1,10368]{1,0:T(1,128)S(1)}, u32[]{:S(2)}, u32[]{:S(2)}) collective-permute-start(f32[1,10368]{1,0:T(1,128)S(1)} %add.18), channel_id=1, source_target_pairs={{0,8},{8,0},{16,24},{24,16},{1,9},{9,1},{17,25},{25,17},{2,10},{10... | collective-permute-start | bytes 124424 | tf_op jit(solution)/shard_map/ppermute | solution.py:31
  191.0 5.0 %collective-permute-start.31 = (f32[1,10368]{1,0:T(1,128)S(1)}, f32[1,10368]{1,0:T(1,128)S(1)}, u32[]{:S(2)}, u32[]{:S(2)}) collective-permute-start(f32[1,10368]{1,0:T(1,128)S(1)} %add.19), channel_id=1, source_target_pairs={{0,16},{8,24},{16,0},{24,8},{1,17},{9,25},{17,1},{25,9},{2,18},{10... | collective-permute-start | bytes 124424 | tf_op jit(solution)/shard_map/ppermute | solution.py:31
  (13 other events, 260.9 us)

commit v3 on v0

v3 whole, which is shorter than its diff:
```python
import jax
import jax.numpy as jnp
from jax import lax
from jax.experimental import pallas as pl
from jax.experimental.pallas import tpu as pltpu
from jax.sharding import PartitionSpec as P

beta_two = 1.0 - 8.0 ** (-0.8)
step_rate = 0.5
tiny_add = 1e-30
lanes = 128
ON_CHIP = pl.BlockSpec(memory_space=pltpu.VMEM)
IN_PLACE = pl.BlockSpec(memory_space=pltpu.HBM)
limits = pltpu.CompilerParams(vmem_limit_bytes=8 * 1024 * 1024)


def f32(*shape):
    return jax.ShapeDtypeStruct(shape, jnp.float32)


def cost(elements, flops, width):
    return pl.CostEstimate(flops=flops * elements, bytes_accessed=width * elements, transcendentals=0)


def axis_sum(values, axis):
    size = lax.axis_size(axis)
    hop = 1
    while hop < size:
        pairs = [(i, i ^ hop) for i in range(size)]
        values = values + lax.ppermute(values, axis, pairs)
        hop *= 2
    return values


def other_parts(values, axis):
    size = lax.axis_size(axis)
    return [lax.ppermute(values, axis, [(i, (i + k) % size) for i in range(size)]) for k in range(1, size)]


def pick(table):
    place = lax.axis_index("dp")
    value = jnp.int32(table[0])
    for k in range(1, len(table)):
        value = jnp.where(place == k, jnp.int32(table[k]), value)
    return value


def block_sum(grad, table, arrived, tokens, rows, fetch=False):
    cols = grad.shape[1]

    def body(grad_ref, *refs):
        start = pl.multiple_of(pick(table) * rows, rows)
        out_ref = refs[len(arrived) + len(tokens)]
        if fetch:
            own, sem = refs[-2:]
            copy = pltpu.make_async_copy(grad_ref.at[pl.ds(start, rows), :], own, sem)
            copy.start()
            copy.wait()
            values = own[...].astype(jnp.float32)
        else:
            values = grad_ref[pl.ds(start, rows), :].astype(jnp.float32)
        for ref in refs[: len(arrived)]:
            values = values + ref[...]
        out_ref[...] = values

    scratch = [pltpu.VMEM((rows, cols), grad.dtype), pltpu.SemaphoreType.DMA(())] if fetch else []
    if fetch:
        grad = pltpu.with_memory_space_constraint(grad, pltpu.HBM)
    return pl.pallas_call(
        body,
        out_shape=f32(rows, cols),
        in_specs=[IN_PLACE if fetch else ON_CHIP] + [ON_CHIP] * (len(arrived) + len(tokens)),
        out_specs=ON_CHIP,
        scratch_shapes=scratch,
        compiler_params=limits,
        cost_estimate=cost(rows * cols, 1, 10),
        name="block",
    )(grad, *arrived, *tokens)


def pass_on(values, tokens):
    def body(values_ref, *refs):
        refs[-1][...] = values_ref[...]

    return pl.pallas_call(
        body,
        out_shape=f32(*values.shape),
        in_specs=[ON_CHIP] * (1 + len(tokens)),
        out_specs=ON_CHIP,
        compiler_params=limits,
        cost_estimate=cost(values.size, 1, 8),
        name="pass",
    )(values, *tokens)


def finish_block(grad, table, arrived, rows):
    cols = grad.shape[1]

    def body(grad_ref, *refs):
        out_ref, row_ref, col_ref = refs[-3:]
        start = pl.multiple_of(pick(table) * rows, rows)
        for k in range(cols // lanes):
            at = pl.ds(k * lanes, lanes)
            values = grad_ref[pl.ds(start, rows), at].astype(jnp.float32)
            for ref in refs[: len(arrived)]:
                values = values + ref[:, at]
            out_ref[:, at] = values
            squares = values * values + tiny_add
            row_part = squares if k == 0 else row_part + squares
            col_ref[:, at] = jnp.sum(squares, axis=0, keepdims=True)
        row_ref[...] = row_part

    return pl.pallas_call(
        body,
        out_shape=(f32(rows, cols), f32(rows, lanes), f32(1, cols)),
        in_specs=[ON_CHIP] * (1 + len(arrived)),
        out_specs=(ON_CHIP,) * 3,
        compiler_params=limits,
        cost_estimate=cost(rows * cols, 6, 14),
        name="finish",
    )(grad, *arrived)


def diagonal(rows):
    row = lax.broadcasted_iota(jnp.int32, (rows, lanes), 0)
    return row == lax.broadcasted_iota(jnp.int32, (rows, lanes), 1)


def unpack_rows(sums, cols, count, rows):
    def body(sums_ref, *outs):
        for k, out in enumerate(outs):
            values = sums_ref[:, pl.ds(2 * cols + (k + 1) * lanes, lanes)]
            column = jnp.sum(jnp.where(diagonal(rows), values, 0.0), axis=1, keepdims=True)
            out[...] = jnp.broadcast_to(column, (rows, lanes))

    return pl.pallas_call(
        body,
        out_shape=(f32(rows, lanes),) * count,
        in_specs=[ON_CHIP],
        out_specs=(ON_CHIP,) * count,
        compiler_params=limits,
        cost_estimate=cost(rows * lanes, 2, 8),
        name="unpack",
    )(sums)


def scale_block(gradient, table, counted, row_parts, old_rows, col_part, held, carried, hidden_width):
    rows, cols = gradient.shape

    def body(grad_ref, col_ref, old_ref, *refs):
        row_out, sums_out = refs[-2:]
        total = refs[0][...]
        for ref in refs[1 : len(row_parts)]:
            total = total + ref[...]
        row_sum = jnp.sum(total, axis=1, keepdims=True)
        old = old_ref[pl.ds(pl.multiple_of(pick(table) * rows, rows), rows), :]
        row = beta_two * old + (1.0 - beta_two) * (row_sum / hidden_width)
        row_out[...] = row
        inverse = 1.0 / row
        before = refs[len(row_parts) : len(row_parts) + len(held)]
        counts = pick(counted) > 0

        def put(at, value):
            value = jnp.where(counts, value, 0.0)
            for ref in before:
                value = value + ref[:, at]
            sums_out[:, at] = value

        put(pl.ds(2 * cols, lanes), jnp.sum(row, axis=0, keepdims=True))
        for k in range(len(carried)):
            values = refs[len(row_parts) + len(held) + k][...]
            at = pl.ds(2 * cols + (k + 1) * lanes, lanes)
            sums_out[:, at] = jnp.sum(jnp.where(diagonal(rows), values, 0.0), axis=0, keepdims=True)
        for k in range(cols // lanes):
            at = pl.ds(k * lanes, lanes)
            values = grad_ref[:, at]
            put(at, col_ref[:, at])
            put(pl.ds(cols + k * lanes, lanes), jnp.sum(values * values * inverse, axis=0, keepdims=True))

    return pl.pallas_call(
        body,
        out_shape=(f32(rows, lanes), f32(1, 2 * cols + (1 + len(carried)) * lanes)),
        in_specs=[ON_CHIP] * (3 + len(row_parts) + len(held) + len(carried)),
        out_specs=(ON_CHIP, ON_CHIP),
        compiler_params=limits,
        cost_estimate=cost(rows * cols, 4, 4),
        name="scale",
    )(gradient, col_part, old_rows, *row_parts, *held, *carried)


def column_factor(sums, extra, old_cols, matrix_rows):
    cols = old_cols.shape[1]

    def body(sums_ref, old_ref, *refs):
        col_out, scale_out, update_out, mean_out = refs[-4:]
        weight = 1.0
        if extra:
            place = lax.axis_index("dp")
            ends = jnp.logical_or(place == 0, place == lax.axis_size("dp") - 1)
            weight = jnp.where(ends, 0.0, 1.0)

        def total(at):
            value = sums_ref[:, at]
            if extra:
                value = value * weight
            for ref in refs[: len(extra)]:
                value = value + ref[:, at]
            return value

        col = beta_two * old_ref[...] + (1.0 - beta_two) * (total(pl.ds(0, cols)) / matrix_rows)
        col_out[...] = col
        scale_out[...] = lax.rsqrt(col)
        ratio = total(pl.ds(cols, cols)) / col
        update = ratio[:, :lanes]
        for k in range(1, cols // lanes):
            update = update + ratio[:, k * lanes : (k + 1) * lanes]
        update_out[...] = update
        mean_out[...] = total(pl.ds(2 * cols, lanes)) / matrix_rows

    return pl.pallas_call(
        body,
        out_shape=(f32(1, cols), f32(1, cols), f32(1, lanes), f32(1, lanes)),
        in_specs=[ON_CHIP] * (2 + len(extra)),
        out_specs=(ON_CHIP,) * 4,
        compiler_params=limits,
        cost_estimate=cost(cols, 4, 12),
        name="columns",
    )(sums, old_cols, *extra)


def apply_update(weights, choices, part, held_out, col_scale, row_mean, updates, matrix_rows, hidden_width):
    pieces = len(choices[0][1])
    choices = [(places, gradient[part], new_row[part]) for places, gradient, new_row in choices]
    first = part.start
    count = len(choices[0][1])
    rows, cols = choices[0][1][0].shape
    arrays = [array for _, gradient, new_row in choices for array in (*gradient, *new_row)]

    def body(weights_ref, col_ref, mean_ref, *refs):
        update_refs = refs[len(arrays) : len(arrays) + len(updates)]
        out_ref, held, sems = refs[-3:]
        update_total = update_refs[0][...]
        for ref in update_refs[1:]:
            update_total = update_total + ref[...]
        update_total = jnp.sum(update_total, axis=1, keepdims=True)
        row_mean = mean_ref[:, :1]
        clip_ratio = jnp.sqrt(update_total * row_mean / (matrix_rows * hidden_width))
        factor = step_rate * jnp.sqrt(row_mean) / jnp.maximum(1.0, clip_ratio)
        col_factor = factor * col_ref[...]
        place = lax.axis_index("dp")

        def copy(k):
            here = held.at[pl.ds(k * rows, rows), :]
            return pltpu.make_async_copy(here, out_ref.at[pl.ds((first + k) * rows, rows), :], sems.at[k])

        for k in range(count):
            here = pl.ds(k * rows, rows)
            for c, (places, _, _) in enumerate(choices):
                grad_ref = refs[c * 2 * count + k]
                row_ref = refs[c * 2 * count + count + k]

                def write(k=k, grad_ref=grad_ref, row_ref=row_ref, here=here):
                    row_scale = lax.rsqrt(row_ref[:, :1])
                    mine = weights_ref[(first + k) * rows : (first + k + 1) * rows, :]
                    held[here, :] = mine - grad_ref[...] * row_scale * col_factor

                if len(choices) == 1:
                    write()
                else:
                    chosen = place == places[0]
                    for other in places[1:]:
                        chosen = jnp.logical_or(chosen, place == other)
                    pl.when(chosen)(write)
            copy(k).start()
        for k in range(count):
            copy(k).wait()

    return pl.pallas_call(
        body,
        out_shape=f32(rows * pieces, cols),
        in_specs=[ON_CHIP] * (3 + len(arrays) + len(updates)) + [IN_PLACE] * len(held_out),
        out_specs=IN_PLACE,
        scratch_shapes=[pltpu.VMEM((rows * count, cols), jnp.float32), pltpu.SemaphoreType.DMA((count,))],
        input_output_aliases={3 + len(arrays) + len(updates): 0} if held_out else {},
        compiler_params=limits,
        cost_estimate=cost(rows * count * cols, 4, 12),
        name="apply",
    )(weights, col_scale, row_mean, *arrays, *updates, *held_out)


def short_line(grad, old_rows, hidden_width, pieces, rows):
    last = 3
    late = range(pieces // 2, pieces)
    soon = range(pieces // 2)
    order = [(2, p) for p in late] + [(3, p) for p in range(pieces)] + [(2, p) for p in soon]
    order += [(1, p) for p in soon] + [(1, p) for p in late]
    swap = [(0, 1), (1, 0), (2, 3), (3, 2)]
    middle = [(1, 2), (2, 1)]
    outward = [(0, 1), (3, 2)]
    ends = [0, last]

    def right(m):
        shard, piece = order[min(max(m, 0), len(order) - 1)]
        return shard * pieces + piece

    def left(m):
        shard, piece = order[min(max(m, 0), len(order) - 1)]
        return (last - shard) * pieces + piece

    P, M = {}, {}
    finished, new_row = {}, {}
    sums = []

    def settle(slot, extra=()):
        table = [left(slot - 3), right(slot), left(slot), right(slot - 3)]
        counted = [int(slot <= 8), int(slot >= 8), int(slot >= 8), int(slot <= 8)]
        arrived = [P[slot]] + ([M[slot]] if slot >= 8 else [])
        gradient, row_part, col_part = finish_block(grad, table, arrived, rows)
        row_parts = [row_part] + other_parts(row_part, "col")
        finished[slot] = gradient
        carried = [new_row[3], new_row[4]] if slot == 8 else []
        new_row[slot], total = scale_block(
            gradient, table, counted, row_parts, old_rows, col_part, [*sums[-1:], *extra], carried, hidden_width
        )
        sums.append(total)

    for slot in range(10):
        if slot >= 2:
            operand = block_sum(grad, [0, right(slot - 2), left(slot - 2), 0], [P[slot - 2]], [], rows)
            M[slot] = lax.ppermute(operand, "dp", middle)
        table = [right(slot), left(slot - 3), right(slot - 3), left(slot)]
        arrived = [M[slot - 1]] if slot >= 3 else []
        tokens = [P[0]] if slot == 2 else []
        operand = block_sum(grad, table, arrived, tokens, rows, fetch=slot < 2)
        P[slot] = lax.ppermute(operand, "dp", swap)
        if 3 <= slot <= 8:
            settle(slot)
    early = lax.ppermute(sums[-1], "dp", outward)
    late_rows = unpack_rows(early, grad.shape[1], 2, rows)
    operand = pass_on(finished[3], [sums[-1]])
    P[10] = lax.ppermute(operand, "dp", outward)
    P[11] = lax.ppermute(pass_on(finished[4], [operand]), "dp", outward)
    settle(9, [early])
    total = axis_sum(sums[-1], "row")
    total = total + lax.ppermute(total, "dp", middle)
    extra = [lax.ppermute(total, "dp", [(1, 0), (2, 3)])]
    outer = ([finished[k] for k in range(5, 9)], [new_row[k] for k in range(5, 9)])
    inner = (
        [finished[8], finished[9], P[10], P[11]],
        [new_row[8], new_row[9], *late_rows],
    )
    return total, extra, [(ends, *outer), ([1, 2], *inner)]


def long_line(grad, old_rows, hidden_width, pieces, rows):
    replicas = lax.axis_size("dp")
    to_right = [(i, i + 1) for i in range(replicas - 1)]
    to_left = [(i + 1, i) for i in range(replicas - 1)]
    rights, lefts = {}, {}
    for slot in range((replicas - 1) * pieces):
        step, piece = divmod(slot, pieces)
        right_table = [min(replicas - 1 - step + z, replicas - 1) * pieces + piece for z in range(replicas)]
        left_table = [max(step - (replicas - 1) + z, 0) * pieces + piece for z in range(replicas)]
        before = slot - pieces
        right = block_sum(grad, right_table, [rights[before]] if step else [], [], rows)
        left = block_sum(grad, left_table, [lefts[before]] if step else [], [], rows)
        rights[slot] = lax.ppermute(right, "dp", to_right[: step + 1])
        lefts[slot] = lax.ppermute(left, "dp", to_left[replicas - 2 - step :])
    gradient, new_row, held = [], [], []
    for piece in range(pieces):
        slot = (replicas - 2) * pieces + piece
        table = [z * pieces + piece for z in range(replicas)]
        grad_piece, row_part, col_part = finish_block(grad, table, [rights[slot], lefts[slot]], rows)
        row_parts = [row_part] + other_parts(row_part, "col")
        row_piece, sums = scale_block(
            grad_piece, table, [1] * replicas, row_parts, old_rows, col_part, held, [], hidden_width
        )
        held = [sums]
        gradient.append(grad_piece)
        new_row.append(row_piece)
    total = axis_sum(axis_sum(sums, "row"), "dp")
    return total, [], [(list(range(replicas)), gradient, new_row)]


def shards(grad_parts, params, row_second, col_second):
    owned_rows = params.shape[2]
    local_cols = params.shape[3]
    slab_rows = row_second.shape[2]
    hidden_width = local_cols * lax.axis_size("col")
    matrix_rows = slab_rows * lax.axis_size("row")
    replicas = lax.axis_size("dp")
    pieces = max(1, min(4, owned_rows // 16))
    rows = owned_rows // pieces
    grad = grad_parts.reshape(slab_rows, local_cols)
    weights = params.reshape(owned_rows, local_cols)
    old_rows = jnp.broadcast_to(row_second.reshape(slab_rows, 1), (slab_rows, lanes))
    old_cols = col_second.reshape(1, local_cols)
    line = short_line if replicas == 4 and pieces == 4 else long_line
    total, extra, choices = line(grad, old_rows, hidden_width, pieces, rows)
    new_col, col_scale, update_part, row_mean = column_factor(total, extra, old_cols, matrix_rows)
    updates = [update_part] + other_parts(update_part, "col")
    new_params = []
    for part in (slice(0, pieces - 1), slice(pieces - 1, pieces)) if pieces > 1 else (slice(0, 1),):
        new_params = [
            apply_update(
                weights, choices, part, new_params, col_scale, row_mean, updates, matrix_rows, hidden_width
            )
        ]
    new_params = new_params[0]
    new_row = [jnp.concatenate([row[:, 0] for row in rows_here]) for _, _, rows_here in choices]
    place = lax.axis_index("dp")
    if len(choices) > 1:
        inner = jnp.logical_and(place > 0, place < replicas - 1)
        new_row = [jnp.where(inner, new_row[1], new_row[0])]
    return (new_params.reshape(params.shape), new_row[0].reshape(1, 1, owned_rows), new_col)


def solution(mesh):
    return jax.shard_map(
        shards,
        mesh=mesh,
        in_specs=(
            P("dp", None, "row", None, "col"),
            P(None, "row", "dp", "col"),
            P(None, "row", None),
            P(None, "col"),
        ),
        out_specs=(P(None, "row", "dp", "col"), P(None, "row", "dp"), P(None, "col")),
        check_vma=False,
    )
```

time: 331 us -> 176 us (0.53)
  blocking collectives: 116 us -> 0 us
  waiting for transfers between devices: 180 us -> 121 us
  starting transfers between devices: 0.04 us -> 34.6 us
  other arithmetic: 16.8 us -> 0.72 us
  Pallas kernels: 0 us -> 14.5 us
  between operations: 15.4 us -> 1.14 us
  local copies, waits for them, and re-layouts: 0.02 us -> 3.42 us
    reduce_scatter x1 -> x0, waiting for transfers between devices: 180 us -> none  [shards(): lax.psum_scatter(grad_local, 'dp', scatter_dimension=2, tiled=True)]
    ppermute x0 -> x33, waiting for transfers between devices: none -> 121 us  [the longest x10 104 us: short_line(): P[slot] = lax.ppermute(operand, 'dp', swap)]
    psum x3 -> x0, blocking collectives: 116 us -> none  [the longest x1 63.1 us: shards(): row_total = lax.psum(jnp.sum(new_row, axis=(1, 2)), ('dp', 'row'))]
    ppermute x0 -> x33, starting transfers between devices: none -> 34.6 us  [the longest x8 18.9 us: short_line(): M[slot] = lax.ppermute(operand, 'dp', middle)]
    pallas_call x0 -> x38, Pallas kernels: none -> 14.5 us  [the longest x18 5.8 us: block_sum(): pl.pallas_call(body, out_shape=f32(rows, cols), in_specs=[IN_PLACE if fet...]
    convert_element_type x1 -> x0, other arithmetic: 7.83 us -> none  [shards(): grad_local = grad_parts[0].astype(jnp.float32)]
    reduce_sum x3 -> x0, other arithmetic: 4.98 us -> none  [the longest x1 2.33 us: shards(): col_part = jnp.sum(squares, axis=(1, 2))]
    sub x1 -> x0, other arithmetic: 3.91 us -> none  [shards(): params - step_rate * update / jnp.maximum(1.0, clip_ratio)[:, None, None,...]
  transfers between devices with their start and end apart: 1 -> 33, of which waited for: 1 -> 20; matrix products, arithmetic and copies ran while one was open for 0% -> 1% of each run, Pallas kernels for 0% -> 7%
where the time goes in v3:
time: 176 us; the launch traced here: 175 us
  waiting for transfers between devices  121 us (69%)
  starting transfers between devices  34.6 us (20%)
  Pallas kernels  14.5 us (8%)
  local copies, waits for them, and re-layouts  3.42 us (2%)
    ppermute x10, waiting for transfers between devices, short_line(): P[slot] = lax.ppermute(operand, 'dp', swap)  104 us
    ppermute x8, starting transfers between devices, short_line(): M[slot] = lax.ppermute(operand, 'dp', middle)  18.9 us
    pallas_call x18, Pallas kernels, block_sum(): pl.pallas_call(body, out_shape=f32(rows, cols), in_specs=[IN_PLACE if fet...  5.8 us
    ppermute x2, waiting for transfers between devices, axis_sum(): values = values + lax.ppermute(values, axis, pairs)  4.7 us
    ppermute x1, waiting for transfers between devices, short_line(): P[11] = lax.ppermute(pass_on(finished[4], [operand]), 'dp', outward)  4.16 us
    pallas_call x7, Pallas kernels, finish_block(): pl.pallas_call(body, out_shape=(f32(rows, cols), f32(rows, lanes), f32(1,...  3.6 us
  transfers between devices with their start and end apart: 33, of which 20 were waited for; matrix products, arithmetic and copies ran while one was open for 1% of the time, Pallas kernels for 7%

profile of v3, /device:TPU:16, one launch (start us, length us, event | category | flops | bytes accessed | tf_op | source)
XLA Modules:
  0.0 175.0 jit_solution(16890701599963410616)
XLA Ops:
  1.9 1.6 collective-permute-start
  5.0 14.5 %collective-permute-done.refs_0_ = f32[32,5120]{1,0:T(8,128)S(1)} collective-permute-done((f32[32,5120]{1,0:T(8,128)S(1)}, f32[32,5120]{1,0:T(8,128)S(1)}, u32[]{:S(2)}, u32[]{:S(2)}) %collective-permute-start) | collective-permute-done | bytes 655392 | tf_op jit(solution)/shard_map/ppermute | solution.py:335
  19.6 2.4 %collective-permute-start.1 = (f32[32,5120]{1,0:T(8,128)S(1)}, f32[32,5120]{1,0:T(8,128)S(1)}, u32[]{:S(2)}, u32[]{:S(2)}) collective-permute-start(f32[32,5120]{1,0:T(8,128)S(1)} %block.19), channel_id=1, source_target_pairs={{8,16},{16,8},{9,17},{17,9},{10,18},{18,10},{11,19},{19,11},{12,20... | collective-permute-start | bytes 1966088 | tf_op jit(solution)/shard_map/ppermute | solution.py:330
  22.1 11.5 %collective-permute-done.7.refs_0_ = f32[32,5120]{1,0:T(8,128)S(1)} collective-permute-done((f32[32,5120]{1,0:T(8,128)S(1)}, f32[32,5120]{1,0:T(8,128)S(1)}, u32[]{:S(2)}, u32[]{:S(2)}) %collective-permute-start.7) | collective-permute-done | bytes 655392 | tf_op jit(solution)/shard_map/ppermute | solution.py:335
  33.6 2.4 %collective-permute-start.8 = (f32[32,5120]{1,0:T(8,128)S(1)}, f32[32,5120]{1,0:T(8,128)S(1)}, u32[]{:S(2)}, u32[]{:S(2)}) collective-permute-start(f32[32,5120]{1,0:T(8,128)S(1)} %block.26), channel_id=1, source_target_pairs={{8,16},{16,8},{9,17},{17,9},{10,18},{18,10},{11,19},{19,11},{12,20... | collective-permute-start | bytes 1966088 | tf_op jit(solution)/shard_map/ppermute | solution.py:330
  36.2 11.5 %collective-permute-done.14.refs_0_ = f32[32,5120]{1,0:T(8,128)S(1)} collective-permute-done((f32[32,5120]{1,0:T(8,128)S(1)}, f32[32,5120]{1,0:T(8,128)S(1)}, u32[]{:S(2)}, u32[]{:S(2)}) %collective-permute-start.14) | collective-permute-done | bytes 655392 | tf_op jit(solution)/shard_map/ppermute | solution.py:335
  47.7 2.4 %collective-permute-start.15 = (f32[32,5120]{1,0:T(8,128)S(1)}, f32[32,5120]{1,0:T(8,128)S(1)}, u32[]{:S(2)}, u32[]{:S(2)}) collective-permute-start(f32[32,5120]{1,0:T(8,128)S(1)} %block.32), channel_id=1, source_target_pairs={{8,16},{16,8},{9,17},{17,9},{10,18},{18,10},{11,19},{19,11},{12,20... | collective-permute-start | bytes 1966088 | tf_op jit(solution)/shard_map/ppermute | solution.py:330
  50.2 11.5 %collective-permute-done.2.refs_0_ = f32[32,5120]{1,0:T(8,128)S(1)} collective-permute-done((f32[32,5120]{1,0:T(8,128)S(1)}, f32[32,5120]{1,0:T(8,128)S(1)}, u32[]{:S(2)}, u32[]{:S(2)}) %collective-permute-start.2) | collective-permute-done | bytes 655392 | tf_op jit(solution)/shard_map/ppermute | solution.py:335
  61.7 2.4 %collective-permute-start.3 = (f32[32,5120]{1,0:T(8,128)S(1)}, f32[32,5120]{1,0:T(8,128)S(1)}, u32[]{:S(2)}, u32[]{:S(2)}) collective-permute-start(f32[32,5120]{1,0:T(8,128)S(1)} %block.21), channel_id=1, source_target_pairs={{8,16},{16,8},{9,17},{17,9},{10,18},{18,10},{11,19},{19,11},{12,20... | collective-permute-start | bytes 1966088 | tf_op jit(solution)/shard_map/ppermute | solution.py:330
  64.3 11.5 %collective-permute-done.9.refs_0_ = f32[32,5120]{1,0:T(8,128)S(1)} collective-permute-done((f32[32,5120]{1,0:T(8,128)S(1)}, f32[32,5120]{1,0:T(8,128)S(1)}, u32[]{:S(2)}, u32[]{:S(2)}) %collective-permute-start.9) | collective-permute-done | bytes 655392 | tf_op jit(solution)/shard_map/ppermute | solution.py:335
  75.8 2.4 %collective-permute-start.10 = (f32[32,5120]{1,0:T(8,128)S(1)}, f32[32,5120]{1,0:T(8,128)S(1)}, u32[]{:S(2)}, u32[]{:S(2)}) collective-permute-start(f32[32,5120]{1,0:T(8,128)S(1)} %block.28), channel_id=1, source_target_pairs={{8,16},{16,8},{9,17},{17,9},{10,18},{18,10},{11,19},{19,11},{12,20... | collective-permute-start | bytes 1966088 | tf_op jit(solution)/shard_map/ppermute | solution.py:330
  78.3 11.5 %collective-permute-done.16.refs_0_ = f32[32,5120]{1,0:T(8,128)S(1)} collective-permute-done((f32[32,5120]{1,0:T(8,128)S(1)}, f32[32,5120]{1,0:T(8,128)S(1)}, u32[]{:S(2)}, u32[]{:S(2)}) %collective-permute-start.16) | collective-permute-done | bytes 655392 | tf_op jit(solution)/shard_map/ppermute | solution.py:335
  89.8 2.4 %collective-permute-start.17 = (f32[32,5120]{1,0:T(8,128)S(1)}, f32[32,5120]{1,0:T(8,128)S(1)}, u32[]{:S(2)}, u32[]{:S(2)}) collective-permute-start(f32[32,5120]{1,0:T(8,128)S(1)} %block.34), channel_id=1, source_target_pairs={{8,16},{16,8},{9,17},{17,9},{10,18},{18,10},{11,19},{19,11},{12,20... | collective-permute-start | bytes 1966088 | tf_op jit(solution)/shard_map/ppermute | solution.py:330
  92.3 11.5 %collective-permute-done.4.refs_0_ = f32[32,5120]{1,0:T(8,128)S(1)} collective-permute-done((f32[32,5120]{1,0:T(8,128)S(1)}, f32[32,5120]{1,0:T(8,128)S(1)}, u32[]{:S(2)}, u32[]{:S(2)}) %collective-permute-start.4) | collective-permute-done | bytes 655392 | tf_op jit(solution)/shard_map/ppermute | solution.py:335
  103.9 2.4 %collective-permute-start.5 = (f32[32,5120]{1,0:T(8,128)S(1)}, f32[32,5120]{1,0:T(8,128)S(1)}, u32[]{:S(2)}, u32[]{:S(2)}) collective-permute-start(f32[32,5120]{1,0:T(8,128)S(1)} %block.23), channel_id=1, source_target_pairs={{8,16},{16,8},{9,17},{17,9},{10,18},{18,10},{11,19},{19,11},{12,20... | collective-permute-start | bytes 1966088 | tf_op jit(solution)/shard_map/ppermute | solution.py:330
  107.1 10.7 %collective-permute-done.11.refs_0_ = f32[32,5120]{1,0:T(8,128)S(1)} collective-permute-done((f32[32,5120]{1,0:T(8,128)S(1)}, f32[32,5120]{1,0:T(8,128)S(1)}, u32[]{:S(2)}, u32[]{:S(2)}) %collective-permute-start.11) | collective-permute-done | bytes 655392 | tf_op jit(solution)/shard_map/ppermute | solution.py:335
  118.9 2.3 %collective-permute-start.12 = (f32[32,5120]{1,0:T(8,128)}, f32[32,5120]{1,0:T(8,128)}, u32[]{:S(2)}, u32[]{:S(2)}) collective-permute-start(f32[32,5120]{1,0:T(8,128)} %block.30), channel_id=1, source_target_pairs={{8,16},{16,8},{9,17},{17,9},{10,18},{18,10},{11,19},{19,11},{12,20... | collective-permute-start | bytes 1966088 | tf_op jit(solution)/shard_map/ppermute | solution.py:330
  125.7 2.5 %copy-done = bf16[1,1,1,512,5120]{4,3,2,1,0:T(8,128)(2,1)S(1)} copy-done((bf16[1,1,1,512,5120]{4,3,2,1,0:T(8,128)(2,1)S(1)}, bf16[1,1,1,512,5120]{4,3,2,1,0:T(8,128)(2,1)}, u32[]{:S(2)}) %copy-start) | copy-done | bytes 5242904
  129.2 2.8 %collective-permute-done.18.refs_0_ = f32[32,5120]{1,0:T(8,128)} collective-permute-done((f32[32,5120]{1,0:T(8,128)}, f32[32,5120]{1,0:T(8,128)}, u32[]{:S(2)}, u32[]{:S(2)}) %collective-permute-start.18) | collective-permute-done | bytes 655392 | tf_op jit(solution)/shard_map/ppermute | solution.py:335
  134.7 1.3 collective-permute-start.25
  136.1 1.6 collective-permute-start.32
  139.0 7.0 %collective-permute-done.6.refs_0_ = f32[32,5120]{1,0:T(8,128)} collective-permute-done((f32[32,5120]{1,0:T(8,128)}, f32[32,5120]{1,0:T(8,128)}, u32[]{:S(2)}, u32[]{:S(2)}) %collective-permute-start.6) | collective-permute-done | bytes 655392 | tf_op jit(solution)/shard_map/ppermute | solution.py:335
  146.0 1.5 finish.7
  149.0 1.6 collective-permute-start.26
  150.6 2.4 %collective-permute-done.26 = f32[1,10368]{1,0:T(1,128)S(1)} collective-permute-done((f32[1,10368]{1,0:T(1,128)S(1)}, f32[1,10368]{1,0:T(1,128)S(1)}, u32[]{:S(2)}, u32[]{:S(2)}) %collective-permute-start.26) | collective-permute-done | bytes 41504 | tf_op jit(solution)/shard_map/ppermute | solution.py:30
  153.1 1.6 collective-permute-start.27
  154.9 2.3 %collective-permute-done.27 = f32[1,10368]{1,0:T(1,128)S(1)} collective-permute-done((f32[1,10368]{1,0:T(1,128)S(1)}, f32[1,10368]{1,0:T(1,128)S(1)}, u32[]{:S(2)}, u32[]{:S(2)}) %collective-permute-start.27) | collective-permute-done | bytes 41504 | tf_op jit(solution)/shard_map/ppermute | solution.py:30
  157.2 2.4 %collective-permute-start.28 = (f32[1,10368]{1,0:T(1,128)S(1)}, f32[1,10368]{1,0:T(1,128)S(1)}, u32[]{:S(2)}, u32[]{:S(2)}) collective-permute-start(f32[1,10368]{1,0:T(1,128)S(1)} %add.10), channel_id=1, source_target_pairs={{8,16},{16,8},{9,17},{17,9},{10,18},{18,10},{11,19},{19,11},{12,20... | collective-permute-start | bytes 124424 | tf_op jit(solution)/shard_map/ppermute | solution.py:345
  159.7 3.4 %collective-permute-done.28 = f32[1,10368]{1,0:T(1,128)S(1)} collective-permute-done((f32[1,10368]{1,0:T(1,128)S(1)}, f32[1,10368]{1,0:T(1,128)S(1)}, u32[]{:S(2)}, u32[]{:S(2)}) %collective-permute-start.28) | collective-permute-done | bytes 41504 | tf_op jit(solution)/shard_map/ppermute | solution.py:345
  164.6 1.5 collective-permute-done.29.refs_0_
  167.9 1.7 apply.2.refs_6_
  169.6 4.2 %collective-permute-done.30.refs_2_ = f32[32,5120]{1,0:T(8,128)S(1)} collective-permute-done((f32[32,5120]{1,0:T(8,128)S(1)}, f32[32,5120]{1,0:T(8,128)S(1)}, u32[]{:S(2)}, u32[]{:S(2)}) %collective-permute-start.30) | collective-permute-done | bytes 655392 | tf_op jit(solution)/shard_map/ppermute | solution.py:342
  (105 shorter events, 21.8 us)
Async XLA Ops:
  1.9 17.7 %collective-permute-start = (f32[32,5120]{1,0:T(8,128)S(1)}, f32[32,5120]{1,0:T(8,128)S(1)}, u32[]{:S(2)}, u32[]{:S(2)}) collective-permute-start(f32[32,5120]{1,0:T(8,128)S(1)} %block.18), channel_id=1, source_target_pairs={{0,8},{8,0},{16,24},{24,16},{1,9},{9,1},{17,25},{25,17},{2,10},{10... | collective-permute-start | bytes 1966088 | tf_op jit(solution)/shard_map/ppermute | solution.py:335
  4.5 29.1 %collective-permute-start.7 = (f32[32,5120]{1,0:T(8,128)S(1)}, f32[32,5120]{1,0:T(8,128)S(1)}, u32[]{:S(2)}, u32[]{:S(2)}) collective-permute-start(f32[32,5120]{1,0:T(8,128)S(1)} %block.25), channel_id=1, source_target_pairs={{0,8},{8,0},{16,24},{24,16},{1,9},{9,1},{17,25},{25,17},{2,10},{10... | collective-permute-start | bytes 1966088 | tf_op jit(solution)/shard_map/ppermute | solution.py:335
  19.6 16.4 %collective-permute-start.1 = (f32[32,5120]{1,0:T(8,128)S(1)}, f32[32,5120]{1,0:T(8,128)S(1)}, u32[]{:S(2)}, u32[]{:S(2)}) collective-permute-start(f32[32,5120]{1,0:T(8,128)S(1)} %block.19), channel_id=1, source_target_pairs={{8,16},{16,8},{9,17},{17,9},{10,18},{18,10},{11,19},{19,11},{12,20... | collective-permute-start | bytes 1966088 | tf_op jit(solution)/shard_map/ppermute | solution.py:330
  22.0 25.6 %collective-permute-start.14 = (f32[32,5120]{1,0:T(8,128)S(1)}, f32[32,5120]{1,0:T(8,128)S(1)}, u32[]{:S(2)}, u32[]{:S(2)}) collective-permute-start(f32[32,5120]{1,0:T(8,128)S(1)} %block.31), channel_id=1, source_target_pairs={{0,8},{8,0},{16,24},{24,16},{1,9},{9,1},{17,25},{25,17},{2,10},{10... | collective-permute-start | bytes 1966088 | tf_op jit(solution)/shard_map/ppermute | solution.py:335
  33.6 16.4 %collective-permute-start.8 = (f32[32,5120]{1,0:T(8,128)S(1)}, f32[32,5120]{1,0:T(8,128)S(1)}, u32[]{:S(2)}, u32[]{:S(2)}) collective-permute-start(f32[32,5120]{1,0:T(8,128)S(1)} %block.26), channel_id=1, source_target_pairs={{8,16},{16,8},{9,17},{17,9},{10,18},{18,10},{11,19},{19,11},{12,20... | collective-permute-start | bytes 1966088 | tf_op jit(solution)/shard_map/ppermute | solution.py:330
  36.1 25.6 %collective-permute-start.2 = (f32[32,5120]{1,0:T(8,128)S(1)}, f32[32,5120]{1,0:T(8,128)S(1)}, u32[]{:S(2)}, u32[]{:S(2)}) collective-permute-start(f32[32,5120]{1,0:T(8,128)S(1)} %block.20), channel_id=1, source_target_pairs={{0,8},{8,0},{16,24},{24,16},{1,9},{9,1},{17,25},{25,17},{2,10},{10... | collective-permute-start | bytes 1966088 | tf_op jit(solution)/shard_map/ppermute | solution.py:335
  47.7 16.4 %collective-permute-start.15 = (f32[32,5120]{1,0:T(8,128)S(1)}, f32[32,5120]{1,0:T(8,128)S(1)}, u32[]{:S(2)}, u32[]{:S(2)}) collective-permute-start(f32[32,5120]{1,0:T(8,128)S(1)} %block.32), channel_id=1, source_target_pairs={{8,16},{16,8},{9,17},{17,9},{10,18},{18,10},{11,19},{19,11},{12,20... | collective-permute-start | bytes 1966088 | tf_op jit(solution)/shard_map/ppermute | solution.py:330
  50.1 25.6 %collective-permute-start.9 = (f32[32,5120]{1,0:T(8,128)S(1)}, f32[32,5120]{1,0:T(8,128)S(1)}, u32[]{:S(2)}, u32[]{:S(2)}) collective-permute-start(f32[32,5120]{1,0:T(8,128)S(1)} %block.27), channel_id=1, source_target_pairs={{0,8},{8,0},{16,24},{24,16},{1,9},{9,1},{17,25},{25,17},{2,10},{10... | collective-permute-start | bytes 1966088 | tf_op jit(solution)/shard_map/ppermute | solution.py:335
  61.7 16.4 %collective-permute-start.3 = (f32[32,5120]{1,0:T(8,128)S(1)}, f32[32,5120]{1,0:T(8,128)S(1)}, u32[]{:S(2)}, u32[]{:S(2)}) collective-permute-start(f32[32,5120]{1,0:T(8,128)S(1)} %block.21), channel_id=1, source_target_pairs={{8,16},{16,8},{9,17},{17,9},{10,18},{18,10},{11,19},{19,11},{12,20... | collective-permute-start | bytes 1966088 | tf_op jit(solution)/shard_map/ppermute | solution.py:330
  64.2 25.6 %collective-permute-start.16 = (f32[32,5120]{1,0:T(8,128)S(1)}, f32[32,5120]{1,0:T(8,128)S(1)}, u32[]{:S(2)}, u32[]{:S(2)}) collective-permute-start(f32[32,5120]{1,0:T(8,128)S(1)} %block.33), channel_id=1, source_target_pairs={{0,8},{8,0},{16,24},{24,16},{1,9},{9,1},{17,25},{25,17},{2,10},{10... | collective-permute-start | bytes 1966088 | tf_op jit(solution)/shard_map/ppermute | solution.py:335
  75.8 16.4 %collective-permute-start.10 = (f32[32,5120]{1,0:T(8,128)S(1)}, f32[32,5120]{1,0:T(8,128)S(1)}, u32[]{:S(2)}, u32[]{:S(2)}) collective-permute-start(f32[32,5120]{1,0:T(8,128)S(1)} %block.28), channel_id=1, source_target_pairs={{8,16},{16,8},{9,17},{17,9},{10,18},{18,10},{11,19},{19,11},{12,20... | collective-permute-start | bytes 1966088 | tf_op jit(solution)/shard_map/ppermute | solution.py:330
  78.2 25.6 %collective-permute-start.4 = (f32[32,5120]{1,0:T(8,128)S(1)}, f32[32,5120]{1,0:T(8,128)S(1)}, u32[]{:S(2)}, u32[]{:S(2)}) collective-permute-start(f32[32,5120]{1,0:T(8,128)S(1)} %block.22), channel_id=1, source_target_pairs={{0,8},{8,0},{16,24},{24,16},{1,9},{9,1},{17,25},{25,17},{2,10},{10... | collective-permute-start | bytes 1966088 | tf_op jit(solution)/shard_map/ppermute | solution.py:335
  89.8 16.4 %collective-permute-start.17 = (f32[32,5120]{1,0:T(8,128)S(1)}, f32[32,5120]{1,0:T(8,128)S(1)}, u32[]{:S(2)}, u32[]{:S(2)}) collective-permute-start(f32[32,5120]{1,0:T(8,128)S(1)} %block.34), channel_id=1, source_target_pairs={{8,16},{16,8},{9,17},{17,9},{10,18},{18,10},{11,19},{19,11},{12,20... | collective-permute-start | bytes 1966088 | tf_op jit(solution)/shard_map/ppermute | solution.py:330
  92.3 25.6 %collective-permute-start.11 = (f32[32,5120]{1,0:T(8,128)S(1)}, f32[32,5120]{1,0:T(8,128)S(1)}, u32[]{:S(2)}, u32[]{:S(2)}) collective-permute-start(f32[32,5120]{1,0:T(8,128)S(1)} %block.29), channel_id=1, source_target_pairs={{0,8},{8,0},{16,24},{24,16},{1,9},{9,1},{17,25},{25,17},{2,10},{10... | collective-permute-start | bytes 1966088 | tf_op jit(solution)/shard_map/ppermute | solution.py:335
  103.9 17.4 %collective-permute-start.5 = (f32[32,5120]{1,0:T(8,128)S(1)}, f32[32,5120]{1,0:T(8,128)S(1)}, u32[]{:S(2)}, u32[]{:S(2)}) collective-permute-start(f32[32,5120]{1,0:T(8,128)S(1)} %block.23), channel_id=1, source_target_pairs={{8,16},{16,8},{9,17},{17,9},{10,18},{18,10},{11,19},{19,11},{12,20... | collective-permute-start | bytes 1966088 | tf_op jit(solution)/shard_map/ppermute | solution.py:330
  107.1 24.8 %collective-permute-start.18 = (f32[32,5120]{1,0:T(8,128)}, f32[32,5120]{1,0:T(8,128)}, u32[]{:S(2)}, u32[]{:S(2)}) collective-permute-start(f32[32,5120]{1,0:T(8,128)} %block.35), channel_id=1, source_target_pairs={{0,8},{8,0},{16,24},{24,16},{1,9},{9,1},{17,25},{25,17},{2,10},{10... | collective-permute-start | bytes 1966088 | tf_op jit(solution)/shard_map/ppermute | solution.py:335
  118.9 20.1 %collective-permute-start.12 = (f32[32,5120]{1,0:T(8,128)}, f32[32,5120]{1,0:T(8,128)}, u32[]{:S(2)}, u32[]{:S(2)}) collective-permute-start(f32[32,5120]{1,0:T(8,128)} %block.30), channel_id=1, source_target_pairs={{8,16},{16,8},{9,17},{17,9},{10,18},{18,10},{11,19},{19,11},{12,20... | collective-permute-start | bytes 1966088 | tf_op jit(solution)/shard_map/ppermute | solution.py:330
  122.2 23.8 %collective-permute-start.6 = (f32[32,5120]{1,0:T(8,128)}, f32[32,5120]{1,0:T(8,128)}, u32[]{:S(2)}, u32[]{:S(2)}) collective-permute-start(f32[32,5120]{1,0:T(8,128)} %block.24), channel_id=1, source_target_pairs={{0,8},{8,0},{16,24},{24,16},{1,9},{9,1},{17,25},{25,17},{2,10},{10... | collective-permute-start | bytes 1966088 | tf_op jit(solution)/shard_map/ppermute | solution.py:335
  123.1 1.2 collective-permute-start.24
  123.3 1.5 collective-permute-start.23
  124.3 1.2 collective-permute-start.22
  128.4 5.3 %collective-permute-start.20 = (f32[32,128]{1,0:T(8,128)S(1)}, f32[32,128]{1,0:T(8,128)S(1)}, u32[]{:S(2)}, u32[]{:S(2)}) collective-permute-start(f32[32,128]{1,0:T(8,128)S(1)} %get-tuple-element.52.refs_0_), channel_id=1, source_target_pairs={{0,1},{1,0},{2,3},{3,2},{4,5},{5,4},{6,7},{7,6},{8,9},{9,8},{10,11... | collective-permute-start | bytes 49160 | tf_op jit(solution)/shard_map/ppermute | solution.py:37
  128.8 4.6 %collective-permute-start.21 = (f32[32,128]{1,0:T(8,128)S(1)}, f32[32,128]{1,0:T(8,128)S(1)}, u32[]{:S(2)}, u32[]{:S(2)}) collective-permute-start(f32[32,128]{1,0:T(8,128)S(1)} %get-tuple-element.55.refs_0_), channel_id=1, source_target_pairs={{0,1},{1,0},{2,3},{3,2},{4,5},{5,4},{6,7},{7,6},{8,9},{9,8},{10,11... | collective-permute-start | bytes 49160 | tf_op jit(solution)/shard_map/ppermute | solution.py:37
  133.3 1.2 collective-permute-start.19
  134.7 13.0 %collective-permute-start.25 = (f32[1,10624]{1,0:T(1,128)S(1)}, f32[1,10624]{1,0:T(1,128)S(1)}, u32[]{:S(2)}, u32[]{:S(2)}) collective-permute-start(f32[1,10624]{1,0:T(1,128)S(1)} %get-tuple-element.72.refs_2_.refs_0_), channel_id=1, source_target_pairs={{0,8},{24,16},{1,9},{25,17},{2,10},{26,18},{3,11},{27,19},{4,12},{... | collective-permute-start | bytes 127496 | tf_op jit(solution)/shard_map/ppermute | solution.py:338
  136.1 31.2 %collective-permute-start.32 = (f32[32,5120]{1,0:T(8,128)S(1)}, f32[32,5120]{1,0:T(8,128)S(1)}, u32[]{:S(2)}, u32[]{:S(2)}) collective-permute-start(f32[32,5120]{1,0:T(8,128)S(1)} %pass.2.refs_0_), channel_id=1, source_target_pairs={{0,8},{24,16},{1,9},{25,17},{2,10},{26,18},{3,11},{27,19},{4,12},{... | collective-permute-start | bytes 1966088 | tf_op jit(solution)/shard_map/ppermute | solution.py:341
  137.7 36.1 %collective-permute-start.30 = (f32[32,5120]{1,0:T(8,128)S(1)}, f32[32,5120]{1,0:T(8,128)S(1)}, u32[]{:S(2)}, u32[]{:S(2)}) collective-permute-start(f32[32,5120]{1,0:T(8,128)S(1)} %pass.3), channel_id=1, source_target_pairs={{0,8},{24,16},{1,9},{25,17},{2,10},{26,18},{3,11},{27,19},{4,12},{... | collective-permute-start | bytes 1966088 | tf_op jit(solution)/shard_map/ppermute | solution.py:342
  147.5 1.2 collective-permute-start.13
  149.0 4.1 %collective-permute-start.26 = (f32[1,10368]{1,0:T(1,128)S(1)}, f32[1,10368]{1,0:T(1,128)S(1)}, u32[]{:S(2)}, u32[]{:S(2)}) collective-permute-start(f32[1,10368]{1,0:T(1,128)S(1)} %get-tuple-element.73), channel_id=1, source_target_pairs={{0,2},{2,0},{4,6},{6,4},{1,3},{3,1},{5,7},{7,5},{8,10},{10,8},{12,... | collective-permute-start | bytes 124424 | tf_op jit(solution)/shard_map/ppermute | solution.py:30
  153.1 4.1 %collective-permute-start.27 = (f32[1,10368]{1,0:T(1,128)S(1)}, f32[1,10368]{1,0:T(1,128)S(1)}, u32[]{:S(2)}, u32[]{:S(2)}) collective-permute-start(f32[1,10368]{1,0:T(1,128)S(1)} %add.9), channel_id=1, source_target_pairs={{0,4},{2,6},{4,0},{6,2},{1,5},{3,7},{5,1},{7,3},{8,12},{10,14},{12... | collective-permute-start | bytes 124424 | tf_op jit(solution)/shard_map/ppermute | solution.py:30
  157.2 5.9 %collective-permute-start.28 = (f32[1,10368]{1,0:T(1,128)S(1)}, f32[1,10368]{1,0:T(1,128)S(1)}, u32[]{:S(2)}, u32[]{:S(2)}) collective-permute-start(f32[1,10368]{1,0:T(1,128)S(1)} %add.10), channel_id=1, source_target_pairs={{8,16},{16,8},{9,17},{17,9},{10,18},{18,10},{11,19},{19,11},{12,20... | collective-permute-start | bytes 124424 | tf_op jit(solution)/shard_map/ppermute | solution.py:345
  163.2 3.0 %collective-permute-start.29 = (f32[1,10368]{1,0:T(1,128)S(1)}, f32[1,10368]{1,0:T(1,128)S(1)}, u32[]{:S(2)}, u32[]{:S(2)}) collective-permute-start(f32[1,10368]{1,0:T(1,128)S(1)} %add.11.sums_ref), channel_id=1, source_target_pairs={{8,0},{16,24},{9,1},{17,25},{10,2},{18,26},{11,3},{19,27},{12,4},{... | collective-permute-start | bytes 124424 | tf_op jit(solution)/shard_map/ppermute | solution.py:346
  (11 other events, 141.3 us)

commit v4 on v3

--- a/solution.py
+++ b/solution.py
@@ -45,39 +45,64 @@
     return value
 
 
-def block_sum(grad, table, arrived, tokens, rows, fetch=False):
+def block_sum(grad, table, arrived, tokens, rows):
     cols = grad.shape[1]
 
     def body(grad_ref, *refs):
         start = pl.multiple_of(pick(table) * rows, rows)
-        out_ref = refs[len(arrived) + len(tokens)]
-        if fetch:
-            own, sem = refs[-2:]
-            copy = pltpu.make_async_copy(grad_ref.at[pl.ds(start, rows), :], own, sem)
-            copy.start()
-            copy.wait()
-            values = own[...].astype(jnp.float32)
-        else:
-            values = grad_ref[pl.ds(start, rows), :].astype(jnp.float32)
+        values = grad_ref[pl.ds(start, rows), :].astype(jnp.float32)
         for ref in refs[: len(arrived)]:
             values = values + ref[...]
-        out_ref[...] = values
-
-    scratch = [pltpu.VMEM((rows, cols), grad.dtype), pltpu.SemaphoreType.DMA(())] if fetch else []
-    if fetch:
-        grad = pltpu.with_memory_space_constraint(grad, pltpu.HBM)
+        refs[-1][...] = values
+
     return pl.pallas_call(
         body,
         out_shape=f32(rows, cols),
-        in_specs=[IN_PLACE if fetch else ON_CHIP] + [ON_CHIP] * (len(arrived) + len(tokens)),
+        in_specs=[ON_CHIP] * (1 + len(arrived) + len(tokens)),
         out_specs=ON_CHIP,
-        scratch_shapes=scratch,
         compiler_params=limits,
         cost_estimate=cost(rows * cols, 1, 10),
         name="block",
     )(grad, *arrived, *tokens)
 
 
+def fetch_block(grad, table, places, rows):
+    cols = grad.shape[1]
+    chunk = min(rows, 8)
+
+    def body(grad_ref, out_ref, held, sems):
+        wanted = pick(places) > 0
+        start = pick(table) * rows
+
+        def copy(k):
+            at = pl.ds(pl.multiple_of(start + k * chunk, chunk), chunk)
+            return pltpu.make_async_copy(grad_ref.at[at, :], held.at[pl.ds(k * chunk, chunk), :], sems.at[k])
+
+        @pl.when(wanted)
+        def _():
+            for k in range(rows // chunk):
+                copy(k).start()
+            for k in range(rows // chunk):
+                at = pl.ds(k * chunk, chunk)
+                copy(k).wait()
+                out_ref[at, :] = held[at, :].astype(jnp.float32)
+
+        @pl.when(jnp.logical_not(wanted))
+        def _():
+            out_ref[...] = jnp.zeros((rows, cols), jnp.float32)
+
+    return pl.pallas_call(
+        body,
+        out_shape=f32(rows, cols),
+        in_specs=[IN_PLACE],
+        out_specs=ON_CHIP,
+        scratch_shapes=[pltpu.VMEM((rows, cols), grad.dtype), pltpu.SemaphoreType.DMA((rows // chunk,))],
+        compiler_params=limits,
+        cost_estimate=cost(rows * cols, 1, 6),
+        name="fetch",
+    )(pltpu.with_memory_space_constraint(grad, pltpu.HBM))
+
+
 def pass_on(values, tokens):
     def body(values_ref, *refs):
         refs[-1][...] = values_ref[...]
@@ -94,16 +119,20 @@
 
 
 def finish_block(grad, table, arrived, rows):
-    cols = grad.shape[1]
-
-    def body(grad_ref, *refs):
+    cols = arrived[0].shape[1]
+    from_grad = [] if grad is None else [grad]
+
+    def body(*refs):
         out_ref, row_ref, col_ref = refs[-3:]
         start = pl.multiple_of(pick(table) * rows, rows)
+        sources = refs[len(from_grad) : len(from_grad) + len(arrived)]
         for k in range(cols // lanes):
             at = pl.ds(k * lanes, lanes)
-            values = grad_ref[pl.ds(start, rows), at].astype(jnp.float32)
-            for ref in refs[: len(arrived)]:
+            values = sources[0][:, at]
+            for ref in sources[1:]:
                 values = values + ref[:, at]
+            if from_grad:
+                values = values + refs[0][pl.ds(start, rows), at].astype(jnp.float32)
             out_ref[:, at] = values
             squares = values * values + tiny_add
             row_part = squares if k == 0 else row_part + squares
@@ -113,12 +142,12 @@
     return pl.pallas_call(
         body,
         out_shape=(f32(rows, cols), f32(rows, lanes), f32(1, cols)),
-        in_specs=[ON_CHIP] * (1 + len(arrived)),
+        in_specs=[ON_CHIP] * (len(from_grad) + len(arrived)),
         out_specs=(ON_CHIP,) * 3,
         compiler_params=limits,
         cost_estimate=cost(rows * cols, 6, 14),
         name="finish",
-    )(grad, *arrived)
+    )(*from_grad, *arrived)
 
 
 def diagonal(rows):
@@ -228,17 +257,28 @@
     )(sums, old_cols, *extra)
 
 
-def apply_update(weights, choices, part, held_out, col_scale, row_mean, updates, matrix_rows, hidden_width):
+def select_run(choices, action):
+    place = lax.axis_index("dp")
+    for c, (places, _, _) in enumerate(choices):
+        if len(choices) == 1:
+            action(c)
+        else:
+            chosen = place == places[0]
+            for other in places[1:]:
+                chosen = jnp.logical_or(chosen, place == other)
+            pl.when(chosen)(lambda c=c: action(c))
+
+
+def apply_first(weights, choices, col_scale, row_mean, updates, matrix_rows, hidden_width):
     pieces = len(choices[0][1])
-    choices = [(places, gradient[part], new_row[part]) for places, gradient, new_row in choices]
-    first = part.start
-    count = len(choices[0][1])
+    count = pieces - 1
     rows, cols = choices[0][1][0].shape
-    arrays = [array for _, gradient, new_row in choices for array in (*gradient, *new_row)]
+    arrays = [array for _, gradient, new_row in choices for array in (*gradient[:count], *new_row)]
+    each = count + pieces
 
     def body(weights_ref, col_ref, mean_ref, *refs):
         update_refs = refs[len(arrays) : len(arrays) + len(updates)]
-        out_ref, held, sems = refs[-3:]
+        out_ref, factor_ref, scale_ref, held, sems = refs[-5:]
         update_total = update_refs[0][...]
         for ref in update_refs[1:]:
             update_total = update_total + ref[...]
@@ -247,45 +287,107 @@
         clip_ratio = jnp.sqrt(update_total * row_mean / (matrix_rows * hidden_width))
         factor = step_rate * jnp.sqrt(row_mean) / jnp.maximum(1.0, clip_ratio)
         col_factor = factor * col_ref[...]
-        place = lax.axis_index("dp")
+        factor_ref[...] = col_factor
 
         def copy(k):
-            here = held.at[pl.ds(k * rows, rows), :]
-            return pltpu.make_async_copy(here, out_ref.at[pl.ds((first + k) * rows, rows), :], sems.at[k])
+            here = pl.ds(k * rows, rows)
+            return pltpu.make_async_copy(held.at[here, :], out_ref.at[here, :], sems.at[k])
 
         for k in range(count):
-            here = pl.ds(k * rows, rows)
-            for c, (places, _, _) in enumerate(choices):
-                grad_ref = refs[c * 2 * count + k]
-                row_ref = refs[c * 2 * count + count + k]
-
-                def write(k=k, grad_ref=grad_ref, row_ref=row_ref, here=here):
-                    row_scale = lax.rsqrt(row_ref[:, :1])
-                    mine = weights_ref[(first + k) * rows : (first + k + 1) * rows, :]
-                    held[here, :] = mine - grad_ref[...] * row_scale * col_factor
-
-                if len(choices) == 1:
-                    write()
-                else:
-                    chosen = place == places[0]
-                    for other in places[1:]:
-                        chosen = jnp.logical_or(chosen, place == other)
-                    pl.when(chosen)(write)
+
+            def write(c, k=k):
+                here = pl.ds(k * rows, rows)
+                row_scale = lax.rsqrt(refs[c * each + count + k][:, :1])
+                held[here, :] = weights_ref[here, :] - refs[c * each + k][...] * row_scale * col_factor
+
+            select_run(choices, write)
             copy(k).start()
+
+        def last_scale(c):
+            scale_ref[...] = lax.rsqrt(refs[c * each + count + pieces - 1][...])
+
+        select_run(choices, last_scale)
         for k in range(count):
             copy(k).wait()
 
     return pl.pallas_call(
         body,
-        out_shape=f32(rows * pieces, cols),
-        in_specs=[ON_CHIP] * (3 + len(arrays) + len(updates)) + [IN_PLACE] * len(held_out),
-        out_specs=IN_PLACE,
+        out_shape=(f32(rows * pieces, cols), f32(1, cols), f32(rows, lanes)),
+        in_specs=[ON_CHIP] * (3 + len(arrays) + len(updates)),
+        out_specs=(IN_PLACE, ON_CHIP, ON_CHIP),
         scratch_shapes=[pltpu.VMEM((rows * count, cols), jnp.float32), pltpu.SemaphoreType.DMA((count,))],
-        input_output_aliases={3 + len(arrays) + len(updates): 0} if held_out else {},
         compiler_params=limits,
         cost_estimate=cost(rows * count * cols, 4, 12),
         name="apply",
-    )(weights, col_scale, row_mean, *arrays, *updates, *held_out)
+    )(weights, col_scale, row_mean, *arrays, *updates)
+
+
+def apply_last(weights, choices, begun, col_factor, row_scale):
+    pieces = len(choices[0][1])
+    rows, cols = choices[0][1][0].shape
+    chunk = min(rows, 8)
+    first = (pieces - 1) * rows
+    arrays = [gradient[-1] for _, gradient, _ in choices]
+
+    def body(weights_ref, factor_ref, scale_ref, *refs):
+        out_ref, held, sems = refs[-3:]
+
+        def copy(k):
+            here = held.at[pl.ds(k * chunk, chunk), :]
+            return pltpu.make_async_copy(here, out_ref.at[pl.ds(first + k * chunk, chunk), :], sems.at[k])
+
+        def write(c):
+            for k in range(rows // chunk):
+                here = pl.ds(k * chunk, chunk)
+                step = refs[c][here, :] * scale_ref[here, :1] * factor_ref[...]
+                held[here, :] = weights_ref[first + k * chunk : first + (k + 1) * chunk, :] - step
+                copy(k).start()
+
+        select_run(choices, write)
+        for k in range(rows // chunk):
+            copy(k).wait()
+
+    return pl.pallas_call(
+        body,
+        out_shape=f32(rows * pieces, cols),
+        in_specs=[ON_CHIP] * (3 + len(arrays)) + [IN_PLACE],
+        out_specs=IN_PLACE,
+        scratch_shapes=[pltpu.VMEM((rows, cols), jnp.float32), pltpu.SemaphoreType.DMA((rows // chunk,))],
+        input_output_aliases={3 + len(arrays): 0},
+        compiler_params=limits,
+        cost_estimate=cost(rows * cols, 3, 12),
+        name="last",
+    )(weights, col_factor, row_scale, *arrays, begun)
+
+
+def row_line(choices):
+    count = len(choices[0][2])
+    rows = choices[0][2][0].shape[0]
+    arrays = [array for _, _, new_row in choices for array in new_row]
+
+    def body(*refs):
+        place = lax.axis_index("dp")
+        row = lax.broadcasted_iota(jnp.int32, (rows, lanes), 0)
+        lane = lax.broadcasted_iota(jnp.int32, (rows, lanes), 1)
+        line = jnp.zeros((1, lanes), jnp.float32)
+        for piece in range(count):
+            values = refs[piece][...]
+            for c, (places, _, _) in enumerate(choices[1:], 1):
+                for other in places:
+                    values = jnp.where(place == other, refs[c * count + piece][...], values)
+            at = lane == row + piece * rows
+            line = line + jnp.sum(jnp.where(at, values, 0.0), axis=0, keepdims=True)
+        refs[-1][...] = line
+
+    return pl.pallas_call(
+        body,
+        out_shape=f32(1, lanes),
+        in_specs=[ON_CHIP] * len(arrays),
+        out_specs=ON_CHIP,
+        compiler_params=limits,
+        cost_estimate=cost(rows * count * lanes, 2, 4),
+        name="rows",
+    )(*arrays)
 
 
 def short_line(grad, old_rows, hidden_width, pieces, rows):
@@ -307,15 +409,18 @@
         shard, piece = order[min(max(m, 0), len(order) - 1)]
         return (last - shard) * pieces + piece
 
-    P, M = {}, {}
+    P, M, fetched = {}, {}, {}
     finished, new_row = {}, {}
     sums = []
 
+    def own_table(slot):
+        return [left(slot - 3), right(slot), left(slot), right(slot - 3)]
+
     def settle(slot, extra=()):
-        table = [left(slot - 3), right(slot), left(slot), right(slot - 3)]
+        table = own_table(slot)
         counted = [int(slot <= 8), int(slot >= 8), int(slot >= 8), int(slot <= 8)]
-        arrived = [P[slot]] + ([M[slot]] if slot >= 8 else [])
-        gradient, row_part, col_part = finish_block(grad, table, arrived, rows)
+        arrived = [P[slot], M[slot], fetched[slot]] if slot >= 8 else [P[slot]]
+        gradient, row_part, col_part = finish_block(None if slot >= 8 else grad, table, arrived, rows)
         row_parts = [row_part] + other_parts(row_part, "col")
         finished[slot] = gradient
         carried = [new_row[3], new_row[4]] if slot == 8 else []
@@ -330,16 +435,21 @@
             M[slot] = lax.ppermute(operand, "dp", middle)
         table = [right(slot), left(slot - 3), right(slot - 3), left(slot)]
         arrived = [M[slot - 1]] if slot >= 3 else []
-        tokens = [P[0]] if slot == 2 else []
-        operand = block_sum(grad, table, arrived, tokens, rows, fetch=slot < 2)
+        if slot < 2:
+            operand = fetch_block(grad, table, [1, 0, 0, 1], rows)
+        else:
+            tokens = [P[0]] if slot == 2 else list(fetched.values()) if slot == 7 else []
+            operand = block_sum(grad, table, arrived, tokens, rows)
         P[slot] = lax.ppermute(operand, "dp", swap)
+        if slot == 5:
+            fetched |= {k: fetch_block(grad, own_table(k), [1, 1, 1, 1], rows) for k in (8, 9)}
         if 3 <= slot <= 8:
             settle(slot)
     early = lax.ppermute(sums[-1], "dp", outward)
     late_rows = unpack_rows(early, grad.shape[1], 2, rows)
     operand = pass_on(finished[3], [sums[-1]])
     P[10] = lax.ppermute(operand, "dp", outward)
-    P[11] = lax.ppermute(pass_on(finished[4], [operand]), "dp", outward)
+    P[11] = lax.ppermute(pass_on(finished[4], [operand, early]), "dp", outward)
     settle(9, [early])
     total = axis_sum(sums[-1], "row")
     total = total + lax.ppermute(total, "dp", middle)
@@ -389,7 +499,7 @@
     hidden_width = local_cols * lax.axis_size("col")
     matrix_rows = slab_rows * lax.axis_size("row")
     replicas = lax.axis_size("dp")
-    pieces = max(1, min(4, owned_rows // 16))
+    pieces = 4 if owned_rows >= 64 else 2
     rows = owned_rows // pieces
     grad = grad_parts.reshape(slab_rows, local_cols)
     weights = params.reshape(owned_rows, local_cols)
@@ -399,20 +509,12 @@
     total, extra, choices = line(grad, old_rows, hidden_width, pieces, rows)
     new_col, col_scale, update_part, row_mean = column_factor(total, extra, old_cols, matrix_rows)
     updates = [update_part] + other_parts(update_part, "col")
-    new_params = []
-    for part in (slice(0, pieces - 1), slice(pieces - 1, pieces)) if pieces > 1 else (slice(0, 1),):
-        new_params = [
-            apply_update(
-                weights, choices, part, new_params, col_scale, row_mean, updates, matrix_rows, hidden_width
-            )
-        ]
-    new_params = new_params[0]
-    new_row = [jnp.concatenate([row[:, 0] for row in rows_here]) for _, _, rows_here in choices]
-    place = lax.axis_index("dp")
-    if len(choices) > 1:
-        inner = jnp.logical_and(place > 0, place < replicas - 1)
-        new_row = [jnp.where(inner, new_row[1], new_row[0])]
-    return (new_params.reshape(params.shape), new_row[0].reshape(1, 1, owned_rows), new_col)
+    begun, col_factor, row_scale = apply_first(
+        weights, choices, col_scale, row_mean, updates, matrix_rows, hidden_width
+    )
+    new_params = apply_last(weights, choices, begun, col_factor, row_scale)
+    new_row = row_line(choices)[:, :owned_rows]
+    return (new_params.reshape(params.shape), new_row.reshape(1, 1, owned_rows), new_col)
 
 
 def solution(mesh):

time: 176 us -> 175 us (level)
  waiting for transfers between devices: 121 us -> 129 us
  Pallas kernels: 14.5 us -> 9.93 us
  local copies, waits for them, and re-layouts: 3.42 us -> 0.16 us
    ppermute x1, waiting for transfers between devices: 0.01 us -> 9.98 us  [short_line(): early = lax.ppermute(sums[-1], 'dp', outward)]
    ppermute x10, waiting for transfers between devices: 104 us -> 95.3 us  [short_line(): P[slot] = lax.ppermute(operand, 'dp', swap)]
    ppermute x8, waiting for transfers between devices: 0.02 us -> 7.12 us  [short_line(): M[slot] = lax.ppermute(operand, 'dp', middle)]
    ppermute x10, starting transfers between devices: 3.28 us -> 6.77 us  [short_line(): P[slot] = lax.ppermute(operand, 'dp', swap)]
    ppermute x8, starting transfers between devices: 18.9 us -> 15.6 us  [short_line(): M[slot] = lax.ppermute(operand, 'dp', middle)]
    unnamed x20 -> x14, local copies, waits for them, and re-layouts: 2.64 us -> 0.04 us
    pallas_call x7, Pallas kernels: 3.6 us -> 1.23 us  [finish_block(): pl.pallas_call(body, out_shape=(f32(rows, cols), f32(rows, lanes), f32(1,...]
    pallas_call x20 -> x23, Pallas kernels: 8.8 us -> 6.62 us  [the longest x4 2.31 us: fetch_block(): pl.pallas_call(body, out_shape=f32(rows, cols), in_specs=[IN_PLACE], out_...]
  transfers between devices with their start and end apart: 33 -> 33, of which waited for: 20 -> 25; matrix products, arithmetic and copies ran while one was open for 1% -> 0% of each run, Pallas kernels for 7% -> 5%
where the time goes in v4:
time: 175 us
  waiting for transfers between devices  129 us (74%)
  starting transfers between devices  34.7 us (20%)
  Pallas kernels  9.93 us (6%)
    ppermute x10, waiting for transfers between devices, short_line(): P[slot] = lax.ppermute(operand, 'dp', swap)  95.3 us
    ppermute x8, starting transfers between devices, short_line(): M[slot] = lax.ppermute(operand, 'dp', middle)  15.6 us
    ppermute x1, waiting for transfers between devices, short_line(): early = lax.ppermute(sums[-1], 'dp', outward)  9.98 us
    ppermute x8, waiting for transfers between devices, short_line(): M[slot] = lax.ppermute(operand, 'dp', middle)  7.12 us
    ppermute x10, starting transfers between devices, short_line(): P[slot] = lax.ppermute(operand, 'dp', swap)  6.77 us
    ppermute x2, waiting for transfers between devices, axis_sum(): values = values + lax.ppermute(values, axis, pairs)  5 us
    ppermute x1, waiting for transfers between devices, short_line(): total = total + lax.ppermute(total, 'dp', middle)  3.97 us
    ppermute x1, waiting for transfers between devices, short_line(): P[11] = lax.ppermute(pass_on(finished[4], [operand, early]), 'dp', outward)  3.6 us
  transfers between devices with their start and end apart: 33, of which 25 were waited for; matrix products, arithmetic and copies ran while one was open for 0% of the time, Pallas kernels for 5%

profile of v4, /device:TPU:16, one launch (start us, length us, event | category | flops | bytes accessed | tf_op | source)
XLA Modules:
  0.0 174.6 jit_solution(11100430136177198471)
XLA Ops:
  0.8 2.8 %collective-permute-start = (f32[32,5120]{1,0:T(8,128)S(1)}, f32[32,5120]{1,0:T(8,128)S(1)}, u32[]{:S(2)}, u32[]{:S(2)}) collective-permute-start(f32[32,5120]{1,0:T(8,128)S(1)} %fetch.4), channel_id=1, source_target_pairs={{0,8},{8,0},{16,24},{24,16},{1,9},{9,1},{17,25},{25,17},{2,10},{10... | collective-permute-start | bytes 1966088 | tf_op jit(solution)/shard_map/ppermute | solution.py:443
  3.6 1.5 collective-permute-start.7
  5.1 14.0 %collective-permute-done.refs_0_ = f32[32,5120]{1,0:T(8,128)S(1)} collective-permute-done((f32[32,5120]{1,0:T(8,128)S(1)}, f32[32,5120]{1,0:T(8,128)S(1)}, u32[]{:S(2)}, u32[]{:S(2)}) %collective-permute-start) | collective-permute-done | bytes 655392 | tf_op jit(solution)/shard_map/ppermute | solution.py:443
  19.2 1.9 %collective-permute-start.1 = (f32[32,5120]{1,0:T(8,128)S(1)}, f32[32,5120]{1,0:T(8,128)S(1)}, u32[]{:S(2)}, u32[]{:S(2)}) collective-permute-start(f32[32,5120]{1,0:T(8,128)S(1)} %block.16), channel_id=1, source_target_pairs={{8,16},{16,8},{9,17},{17,9},{10,18},{18,10},{11,19},{19,11},{12,20... | collective-permute-start | bytes 1966088 | tf_op jit(solution)/shard_map/ppermute | solution.py:435
  22.1 11.1 %collective-permute-done.7.refs_0_ = f32[32,5120]{1,0:T(8,128)S(1)} collective-permute-done((f32[32,5120]{1,0:T(8,128)S(1)}, f32[32,5120]{1,0:T(8,128)S(1)}, u32[]{:S(2)}, u32[]{:S(2)}) %collective-permute-start.7) | collective-permute-done | bytes 655392 | tf_op jit(solution)/shard_map/ppermute | solution.py:443
  33.2 1.9 %collective-permute-start.8 = (f32[32,5120]{1,0:T(8,128)S(1)}, f32[32,5120]{1,0:T(8,128)S(1)}, u32[]{:S(2)}, u32[]{:S(2)}) collective-permute-start(f32[32,5120]{1,0:T(8,128)S(1)} %block.22), channel_id=1, source_target_pairs={{8,16},{16,8},{9,17},{17,9},{10,18},{18,10},{11,19},{19,11},{12,20... | collective-permute-start | bytes 1966088 | tf_op jit(solution)/shard_map/ppermute | solution.py:435
  36.3 10.9 %collective-permute-done.14.refs_0_ = f32[32,5120]{1,0:T(8,128)S(1)} collective-permute-done((f32[32,5120]{1,0:T(8,128)S(1)}, f32[32,5120]{1,0:T(8,128)S(1)}, u32[]{:S(2)}, u32[]{:S(2)}) %collective-permute-start.14) | collective-permute-done | bytes 655392 | tf_op jit(solution)/shard_map/ppermute | solution.py:443
  47.2 1.9 %collective-permute-start.15 = (f32[32,5120]{1,0:T(8,128)S(1)}, f32[32,5120]{1,0:T(8,128)S(1)}, u32[]{:S(2)}, u32[]{:S(2)}) collective-permute-start(f32[32,5120]{1,0:T(8,128)S(1)} %block.28), channel_id=1, source_target_pairs={{8,16},{16,8},{9,17},{17,9},{10,18},{18,10},{11,19},{19,11},{12,20... | collective-permute-start | bytes 1966088 | tf_op jit(solution)/shard_map/ppermute | solution.py:435
  50.3 10.9 %collective-permute-done.2.refs_0_.refs_1_ = f32[32,5120]{1,0:T(8,128)S(1)} collective-permute-done((f32[32,5120]{1,0:T(8,128)S(1)}, f32[32,5120]{1,0:T(8,128)S(1)}, u32[]{:S(2)}, u32[]{:S(2)}) %collective-permute-start.2) | collective-permute-done | bytes 655392 | tf_op jit(solution)/shard_map/ppermute | solution.py:443
  61.3 1.9 %collective-permute-start.3 = (f32[32,5120]{1,0:T(8,128)S(1)}, f32[32,5120]{1,0:T(8,128)S(1)}, u32[]{:S(2)}, u32[]{:S(2)}) collective-permute-start(f32[32,5120]{1,0:T(8,128)S(1)} %block.18), channel_id=1, source_target_pairs={{8,16},{16,8},{9,17},{17,9},{10,18},{18,10},{11,19},{19,11},{12,20... | collective-permute-start | bytes 1966088 | tf_op jit(solution)/shard_map/ppermute | solution.py:435
  64.4 10.9 %collective-permute-done.9.refs_0_.refs_1_ = f32[32,5120]{1,0:T(8,128)S(1)} collective-permute-done((f32[32,5120]{1,0:T(8,128)S(1)}, f32[32,5120]{1,0:T(8,128)S(1)}, u32[]{:S(2)}, u32[]{:S(2)}) %collective-permute-start.9) | collective-permute-done | bytes 655392 | tf_op jit(solution)/shard_map/ppermute | solution.py:443
  75.3 1.9 %collective-permute-start.10 = (f32[32,5120]{1,0:T(8,128)S(1)}, f32[32,5120]{1,0:T(8,128)S(1)}, u32[]{:S(2)}, u32[]{:S(2)}) collective-permute-start(f32[32,5120]{1,0:T(8,128)S(1)} %block.24), channel_id=1, source_target_pairs={{8,16},{16,8},{9,17},{17,9},{10,18},{18,10},{11,19},{19,11},{12,20... | collective-permute-start | bytes 1966088 | tf_op jit(solution)/shard_map/ppermute | solution.py:435
  78.4 10.9 %collective-permute-done.16.refs_0_.refs_1_ = f32[32,5120]{1,0:T(8,128)S(1)} collective-permute-done((f32[32,5120]{1,0:T(8,128)S(1)}, f32[32,5120]{1,0:T(8,128)S(1)}, u32[]{:S(2)}, u32[]{:S(2)}) %collective-permute-start.16) | collective-permute-done | bytes 655392 | tf_op jit(solution)/shard_map/ppermute | solution.py:443
  89.4 2.2 %collective-permute-start.17 = (f32[32,5120]{1,0:T(8,128)S(1)}, f32[32,5120]{1,0:T(8,128)S(1)}, u32[]{:S(2)}, u32[]{:S(2)}) collective-permute-start(f32[32,5120]{1,0:T(8,128)S(1)} %block.30), channel_id=1, source_target_pairs={{8,16},{16,8},{9,17},{17,9},{10,18},{18,10},{11,19},{19,11},{12,20... | collective-permute-start | bytes 1966088 | tf_op jit(solution)/shard_map/ppermute | solution.py:435
  95.1 8.2 %collective-permute-done.4.refs_0_.refs_1_ = f32[32,5120]{1,0:T(8,128)S(1)} collective-permute-done((f32[32,5120]{1,0:T(8,128)S(1)}, f32[32,5120]{1,0:T(8,128)S(1)}, u32[]{:S(2)}, u32[]{:S(2)}) %collective-permute-start.4) | collective-permute-done | bytes 655392 | tf_op jit(solution)/shard_map/ppermute | solution.py:443
  103.4 1.9 %collective-permute-start.5 = (f32[32,5120]{1,0:T(8,128)S(1)}, f32[32,5120]{1,0:T(8,128)S(1)}, u32[]{:S(2)}, u32[]{:S(2)}) collective-permute-start(f32[32,5120]{1,0:T(8,128)S(1)} %block.20), channel_id=1, source_target_pairs={{8,16},{16,8},{9,17},{17,9},{10,18},{18,10},{11,19},{19,11},{12,20... | collective-permute-start | bytes 1966088 | tf_op jit(solution)/shard_map/ppermute | solution.py:435
  105.4 1.5 collective-permute-done.17.refs_0_
  107.0 10.4 %collective-permute-done.11.refs_0_.refs_1_ = f32[32,5120]{1,0:T(8,128)S(1)} collective-permute-done((f32[32,5120]{1,0:T(8,128)S(1)}, f32[32,5120]{1,0:T(8,128)S(1)}, u32[]{:S(2)}, u32[]{:S(2)}) %collective-permute-start.11) | collective-permute-done | bytes 655392 | tf_op jit(solution)/shard_map/ppermute | solution.py:443
  117.5 1.9 %collective-permute-start.12 = (f32[32,5120]{1,0:T(8,128)S(1)}, f32[32,5120]{1,0:T(8,128)S(1)}, u32[]{:S(2)}, u32[]{:S(2)}) collective-permute-start(f32[32,5120]{1,0:T(8,128)S(1)} %block.26), channel_id=1, source_target_pairs={{8,16},{16,8},{9,17},{17,9},{10,18},{18,10},{11,19},{19,11},{12,20... | collective-permute-start | bytes 1966088 | tf_op jit(solution)/shard_map/ppermute | solution.py:435
  119.4 1.5 collective-permute-done.5.refs_0_.refs_1_
  123.4 8.0 %collective-permute-done.18.refs_0_ = f32[32,5120]{1,0:T(8,128)S(1)} collective-permute-done((f32[32,5120]{1,0:T(8,128)S(1)}, f32[32,5120]{1,0:T(8,128)S(1)}, u32[]{:S(2)}, u32[]{:S(2)}) %collective-permute-start.18) | collective-permute-done | bytes 655392 | tf_op jit(solution)/shard_map/ppermute | solution.py:443
  134.8 1.6 collective-permute-start.30
  136.4 10.0 %collective-permute-done.25.refs_3_.sums_ref.refs_1_ = f32[1,10624]{1,0:T(1,128)S(1)} collective-permute-done((f32[1,10624]{1,0:T(1,128)S(1)}, f32[1,10624]{1,0:T(1,128)S(1)}, u32[]{:S(2)}, u32[]{:S(2)}) %collective-permute-start.25) | collective-permute-done | bytes 42528 | tf_op jit(solution)/shard_map/ppermute | solution.py:448
  149.4 1.6 collective-permute-start.26
  151.0 2.5 %collective-permute-done.26 = f32[1,10368]{1,0:T(1,128)S(1)} collective-permute-done((f32[1,10368]{1,0:T(1,128)S(1)}, f32[1,10368]{1,0:T(1,128)S(1)}, u32[]{:S(2)}, u32[]{:S(2)}) %collective-permute-start.26) | collective-permute-done | bytes 41504 | tf_op jit(solution)/shard_map/ppermute | solution.py:30
  153.5 1.6 collective-permute-start.27
  155.1 2.5 %collective-permute-done.27 = f32[1,10368]{1,0:T(1,128)S(1)} collective-permute-done((f32[1,10368]{1,0:T(1,128)S(1)}, f32[1,10368]{1,0:T(1,128)S(1)}, u32[]{:S(2)}, u32[]{:S(2)}) %collective-permute-start.27) | collective-permute-done | bytes 41504 | tf_op jit(solution)/shard_map/ppermute | solution.py:30
  157.6 1.9 %collective-permute-start.28 = (f32[1,10368]{1,0:T(1,128)S(1)}, f32[1,10368]{1,0:T(1,128)S(1)}, u32[]{:S(2)}, u32[]{:S(2)}) collective-permute-start(f32[1,10368]{1,0:T(1,128)S(1)} %add.10), channel_id=1, source_target_pairs={{8,16},{16,8},{9,17},{17,9},{10,18},{18,10},{11,19},{19,11},{12,20... | collective-permute-start | bytes 124424 | tf_op jit(solution)/shard_map/ppermute | solution.py:455
  159.6 4.0 %collective-permute-done.28 = f32[1,10368]{1,0:T(1,128)S(1)} collective-permute-done((f32[1,10368]{1,0:T(1,128)S(1)}, f32[1,10368]{1,0:T(1,128)S(1)}, u32[]{:S(2)}, u32[]{:S(2)}) %collective-permute-start.28) | collective-permute-done | bytes 41504 | tf_op jit(solution)/shard_map/ppermute | solution.py:455
  164.9 1.7 collective-permute-done.29.refs_0_
  168.3 1.7 apply.1
  170.1 3.6 %collective-permute-done.32.refs_1_ = f32[32,5120]{1,0:T(8,128)S(1)} collective-permute-done((f32[32,5120]{1,0:T(8,128)S(1)}, f32[32,5120]{1,0:T(8,128)S(1)}, u32[]{:S(2)}, u32[]{:S(2)}) %collective-permute-start.32) | collective-permute-done | bytes 655392 | tf_op jit(solution)/shard_map/ppermute | solution.py:452
  (95 shorter events, 22.9 us)
Async XLA Ops:
  0.8 18.3 %collective-permute-start = (f32[32,5120]{1,0:T(8,128)S(1)}, f32[32,5120]{1,0:T(8,128)S(1)}, u32[]{:S(2)}, u32[]{:S(2)}) collective-permute-start(f32[32,5120]{1,0:T(8,128)S(1)} %fetch.4), channel_id=1, source_target_pairs={{0,8},{8,0},{16,24},{24,16},{1,9},{9,1},{17,25},{25,17},{2,10},{10... | collective-permute-start | bytes 1966088 | tf_op jit(solution)/shard_map/ppermute | solution.py:443
  3.6 29.5 %collective-permute-start.7 = (f32[32,5120]{1,0:T(8,128)S(1)}, f32[32,5120]{1,0:T(8,128)S(1)}, u32[]{:S(2)}, u32[]{:S(2)}) collective-permute-start(f32[32,5120]{1,0:T(8,128)S(1)} %fetch.5), channel_id=1, source_target_pairs={{0,8},{8,0},{16,24},{24,16},{1,9},{9,1},{17,25},{25,17},{2,10},{10... | collective-permute-start | bytes 1966088 | tf_op jit(solution)/shard_map/ppermute | solution.py:443
  19.2 17.0 %collective-permute-start.1 = (f32[32,5120]{1,0:T(8,128)S(1)}, f32[32,5120]{1,0:T(8,128)S(1)}, u32[]{:S(2)}, u32[]{:S(2)}) collective-permute-start(f32[32,5120]{1,0:T(8,128)S(1)} %block.16), channel_id=1, source_target_pairs={{8,16},{16,8},{9,17},{17,9},{10,18},{18,10},{11,19},{19,11},{12,20... | collective-permute-start | bytes 1966088 | tf_op jit(solution)/shard_map/ppermute | solution.py:435
  21.2 26.0 %collective-permute-start.14 = (f32[32,5120]{1,0:T(8,128)S(1)}, f32[32,5120]{1,0:T(8,128)S(1)}, u32[]{:S(2)}, u32[]{:S(2)}) collective-permute-start(f32[32,5120]{1,0:T(8,128)S(1)} %block.27), channel_id=1, source_target_pairs={{0,8},{8,0},{16,24},{24,16},{1,9},{9,1},{17,25},{25,17},{2,10},{10... | collective-permute-start | bytes 1966088 | tf_op jit(solution)/shard_map/ppermute | solution.py:443
  33.2 17.0 %collective-permute-start.8 = (f32[32,5120]{1,0:T(8,128)S(1)}, f32[32,5120]{1,0:T(8,128)S(1)}, u32[]{:S(2)}, u32[]{:S(2)}) collective-permute-start(f32[32,5120]{1,0:T(8,128)S(1)} %block.22), channel_id=1, source_target_pairs={{8,16},{16,8},{9,17},{17,9},{10,18},{18,10},{11,19},{19,11},{12,20... | collective-permute-start | bytes 1966088 | tf_op jit(solution)/shard_map/ppermute | solution.py:435
  36.2 25.0 %collective-permute-start.2 = (f32[32,5120]{1,0:T(8,128)S(1)}, f32[32,5120]{1,0:T(8,128)S(1)}, u32[]{:S(2)}, u32[]{:S(2)}) collective-permute-start(f32[32,5120]{1,0:T(8,128)S(1)} %block.17), channel_id=1, source_target_pairs={{0,8},{8,0},{16,24},{24,16},{1,9},{9,1},{17,25},{25,17},{2,10},{10... | collective-permute-start | bytes 1966088 | tf_op jit(solution)/shard_map/ppermute | solution.py:443
  47.2 17.0 %collective-permute-start.15 = (f32[32,5120]{1,0:T(8,128)S(1)}, f32[32,5120]{1,0:T(8,128)S(1)}, u32[]{:S(2)}, u32[]{:S(2)}) collective-permute-start(f32[32,5120]{1,0:T(8,128)S(1)} %block.28), channel_id=1, source_target_pairs={{8,16},{16,8},{9,17},{17,9},{10,18},{18,10},{11,19},{19,11},{12,20... | collective-permute-start | bytes 1966088 | tf_op jit(solution)/shard_map/ppermute | solution.py:435
  50.2 25.0 %collective-permute-start.9 = (f32[32,5120]{1,0:T(8,128)S(1)}, f32[32,5120]{1,0:T(8,128)S(1)}, u32[]{:S(2)}, u32[]{:S(2)}) collective-permute-start(f32[32,5120]{1,0:T(8,128)S(1)} %block.23), channel_id=1, source_target_pairs={{0,8},{8,0},{16,24},{24,16},{1,9},{9,1},{17,25},{25,17},{2,10},{10... | collective-permute-start | bytes 1966088 | tf_op jit(solution)/shard_map/ppermute | solution.py:443
  61.3 17.0 %collective-permute-start.3 = (f32[32,5120]{1,0:T(8,128)S(1)}, f32[32,5120]{1,0:T(8,128)S(1)}, u32[]{:S(2)}, u32[]{:S(2)}) collective-permute-start(f32[32,5120]{1,0:T(8,128)S(1)} %block.18), channel_id=1, source_target_pairs={{8,16},{16,8},{9,17},{17,9},{10,18},{18,10},{11,19},{19,11},{12,20... | collective-permute-start | bytes 1966088 | tf_op jit(solution)/shard_map/ppermute | solution.py:435
  64.3 25.0 %collective-permute-start.16 = (f32[32,5120]{1,0:T(8,128)S(1)}, f32[32,5120]{1,0:T(8,128)S(1)}, u32[]{:S(2)}, u32[]{:S(2)}) collective-permute-start(f32[32,5120]{1,0:T(8,128)S(1)} %block.29), channel_id=1, source_target_pairs={{0,8},{8,0},{16,24},{24,16},{1,9},{9,1},{17,25},{25,17},{2,10},{10... | collective-permute-start | bytes 1966088 | tf_op jit(solution)/shard_map/ppermute | solution.py:443
  75.3 18.4 %collective-permute-start.10 = (f32[32,5120]{1,0:T(8,128)S(1)}, f32[32,5120]{1,0:T(8,128)S(1)}, u32[]{:S(2)}, u32[]{:S(2)}) collective-permute-start(f32[32,5120]{1,0:T(8,128)S(1)} %block.24), channel_id=1, source_target_pairs={{8,16},{16,8},{9,17},{17,9},{10,18},{18,10},{11,19},{19,11},{12,20... | collective-permute-start | bytes 1966088 | tf_op jit(solution)/shard_map/ppermute | solution.py:435
  78.4 25.0 %collective-permute-start.4 = (f32[32,5120]{1,0:T(8,128)S(1)}, f32[32,5120]{1,0:T(8,128)S(1)}, u32[]{:S(2)}, u32[]{:S(2)}) collective-permute-start(f32[32,5120]{1,0:T(8,128)S(1)} %block.19), channel_id=1, source_target_pairs={{0,8},{8,0},{16,24},{24,16},{1,9},{9,1},{17,25},{25,17},{2,10},{10... | collective-permute-start | bytes 1966088 | tf_op jit(solution)/shard_map/ppermute | solution.py:443
  89.4 17.5 %collective-permute-start.17 = (f32[32,5120]{1,0:T(8,128)S(1)}, f32[32,5120]{1,0:T(8,128)S(1)}, u32[]{:S(2)}, u32[]{:S(2)}) collective-permute-start(f32[32,5120]{1,0:T(8,128)S(1)} %block.30), channel_id=1, source_target_pairs={{8,16},{16,8},{9,17},{17,9},{10,18},{18,10},{11,19},{19,11},{12,20... | collective-permute-start | bytes 1966088 | tf_op jit(solution)/shard_map/ppermute | solution.py:435
  93.9 23.5 %collective-permute-start.11 = (f32[32,5120]{1,0:T(8,128)S(1)}, f32[32,5120]{1,0:T(8,128)S(1)}, u32[]{:S(2)}, u32[]{:S(2)}) collective-permute-start(f32[32,5120]{1,0:T(8,128)S(1)} %block.25), channel_id=1, source_target_pairs={{0,8},{8,0},{16,24},{24,16},{1,9},{9,1},{17,25},{25,17},{2,10},{10... | collective-permute-start | bytes 1966088 | tf_op jit(solution)/shard_map/ppermute | solution.py:443
  103.4 17.5 %collective-permute-start.5 = (f32[32,5120]{1,0:T(8,128)S(1)}, f32[32,5120]{1,0:T(8,128)S(1)}, u32[]{:S(2)}, u32[]{:S(2)}) collective-permute-start(f32[32,5120]{1,0:T(8,128)S(1)} %block.20), channel_id=1, source_target_pairs={{8,16},{16,8},{9,17},{17,9},{10,18},{18,10},{11,19},{19,11},{12,20... | collective-permute-start | bytes 1966088 | tf_op jit(solution)/shard_map/ppermute | solution.py:435
  106.9 24.5 %collective-permute-start.18 = (f32[32,5120]{1,0:T(8,128)S(1)}, f32[32,5120]{1,0:T(8,128)S(1)}, u32[]{:S(2)}, u32[]{:S(2)}) collective-permute-start(f32[32,5120]{1,0:T(8,128)S(1)} %block.31), channel_id=1, source_target_pairs={{0,8},{8,0},{16,24},{24,16},{1,9},{9,1},{17,25},{25,17},{2,10},{10... | collective-permute-start | bytes 1966088 | tf_op jit(solution)/shard_map/ppermute | solution.py:443
  117.5 30.3 %collective-permute-start.12 = (f32[32,5120]{1,0:T(8,128)S(1)}, f32[32,5120]{1,0:T(8,128)S(1)}, u32[]{:S(2)}, u32[]{:S(2)}) collective-permute-start(f32[32,5120]{1,0:T(8,128)S(1)} %block.26), channel_id=1, source_target_pairs={{8,16},{16,8},{9,17},{17,9},{10,18},{18,10},{11,19},{19,11},{12,20... | collective-permute-start | bytes 1966088 | tf_op jit(solution)/shard_map/ppermute | solution.py:435
  121.0 26.8 %collective-permute-start.6 = (f32[32,5120]{1,0:T(8,128)S(1)}, f32[32,5120]{1,0:T(8,128)S(1)}, u32[]{:S(2)}, u32[]{:S(2)}) collective-permute-start(f32[32,5120]{1,0:T(8,128)S(1)} %block.21), channel_id=1, source_target_pairs={{0,8},{8,0},{16,24},{24,16},{1,9},{9,1},{17,25},{25,17},{2,10},{10... | collective-permute-start | bytes 1966088 | tf_op jit(solution)/shard_map/ppermute | solution.py:443
  121.2 1.2 collective-permute-start.24
  121.5 1.4 collective-permute-start.23
  122.5 9.1 %collective-permute-start.22 = (f32[32,128]{1,0:T(8,128)S(1)}, f32[32,128]{1,0:T(8,128)S(1)}, u32[]{:S(2)}, u32[]{:S(2)}) collective-permute-start(f32[32,128]{1,0:T(8,128)S(1)} %get-tuple-element.61.refs_0_), channel_id=1, source_target_pairs={{0,1},{1,0},{2,3},{3,2},{4,5},{5,4},{6,7},{7,6},{8,9},{9,8},{10,11... | collective-permute-start | bytes 49160 | tf_op jit(solution)/shard_map/ppermute | solution.py:37
  122.9 10.0 %collective-permute-start.21 = (f32[32,128]{1,0:T(8,128)S(1)}, f32[32,128]{1,0:T(8,128)S(1)}, u32[]{:S(2)}, u32[]{:S(2)}) collective-permute-start(f32[32,128]{1,0:T(8,128)S(1)} %get-tuple-element.58.refs_0_), channel_id=1, source_target_pairs={{0,1},{1,0},{2,3},{3,2},{4,5},{5,4},{6,7},{7,6},{8,9},{9,8},{10,11... | collective-permute-start | bytes 49160 | tf_op jit(solution)/shard_map/ppermute | solution.py:37
  131.4 1.7 collective-permute-start.20
  131.6 1.7 collective-permute-start.19
  133.5 12.9 %collective-permute-start.25 = (f32[1,10624]{1,0:T(1,128)S(1)}, f32[1,10624]{1,0:T(1,128)S(1)}, u32[]{:S(2)}, u32[]{:S(2)}) collective-permute-start(f32[1,10624]{1,0:T(1,128)S(1)} %get-tuple-element.75.refs_2_.refs_0_), channel_id=1, source_target_pairs={{0,8},{24,16},{1,9},{25,17},{2,10},{26,18},{3,11},{27,19},{4,12},{... | collective-permute-start | bytes 127496 | tf_op jit(solution)/shard_map/ppermute | solution.py:448
  134.8 33.0 %collective-permute-start.30 = (f32[32,5120]{1,0:T(8,128)S(1)}, f32[32,5120]{1,0:T(8,128)S(1)}, u32[]{:S(2)}, u32[]{:S(2)}) collective-permute-start(f32[32,5120]{1,0:T(8,128)S(1)} %pass.2.refs_0_), channel_id=1, source_target_pairs={{0,8},{24,16},{1,9},{25,17},{2,10},{26,18},{3,11},{27,19},{4,12},{... | collective-permute-start | bytes 1966088 | tf_op jit(solution)/shard_map/ppermute | solution.py:451
  146.4 27.2 %collective-permute-start.32 = (f32[32,5120]{1,0:T(8,128)S(1)}, f32[32,5120]{1,0:T(8,128)S(1)}, u32[]{:S(2)}, u32[]{:S(2)}) collective-permute-start(f32[32,5120]{1,0:T(8,128)S(1)} %pass.3), channel_id=1, source_target_pairs={{0,8},{24,16},{1,9},{25,17},{2,10},{26,18},{3,11},{27,19},{4,12},{... | collective-permute-start | bytes 1966088 | tf_op jit(solution)/shard_map/ppermute | solution.py:452
  148.0 1.2 collective-permute-start.13
  149.4 4.1 %collective-permute-start.26 = (f32[1,10368]{1,0:T(1,128)S(1)}, f32[1,10368]{1,0:T(1,128)S(1)}, u32[]{:S(2)}, u32[]{:S(2)}) collective-permute-start(f32[1,10368]{1,0:T(1,128)S(1)} %get-tuple-element.76), channel_id=1, source_target_pairs={{0,2},{2,0},{4,6},{6,4},{1,3},{3,1},{5,7},{7,5},{8,10},{10,8},{12,... | collective-permute-start | bytes 124424 | tf_op jit(solution)/shard_map/ppermute | solution.py:30
  153.5 4.1 %collective-permute-start.27 = (f32[1,10368]{1,0:T(1,128)S(1)}, f32[1,10368]{1,0:T(1,128)S(1)}, u32[]{:S(2)}, u32[]{:S(2)}) collective-permute-start(f32[1,10368]{1,0:T(1,128)S(1)} %add.9), channel_id=1, source_target_pairs={{0,4},{2,6},{4,0},{6,2},{1,5},{3,7},{5,1},{7,3},{8,12},{10,14},{12... | collective-permute-start | bytes 124424 | tf_op jit(solution)/shard_map/ppermute | solution.py:30
  157.6 5.9 %collective-permute-start.28 = (f32[1,10368]{1,0:T(1,128)S(1)}, f32[1,10368]{1,0:T(1,128)S(1)}, u32[]{:S(2)}, u32[]{:S(2)}) collective-permute-start(f32[1,10368]{1,0:T(1,128)S(1)} %add.10), channel_id=1, source_target_pairs={{8,16},{16,8},{9,17},{17,9},{10,18},{18,10},{11,19},{19,11},{12,20... | collective-permute-start | bytes 124424 | tf_op jit(solution)/shard_map/ppermute | solution.py:455
  163.6 3.0 %collective-permute-start.29 = (f32[1,10368]{1,0:T(1,128)S(1)}, f32[1,10368]{1,0:T(1,128)S(1)}, u32[]{:S(2)}, u32[]{:S(2)}) collective-permute-start(f32[1,10368]{1,0:T(1,128)S(1)} %add.11.sums_ref), channel_id=1, source_target_pairs={{8,0},{16,24},{9,1},{17,25},{10,2},{18,26},{11,3},{19,27},{12,4},{... | collective-permute-start | bytes 124424 | tf_op jit(solution)/shard_map/ppermute | solution.py:456
  (8 other events, 121.4 us)

commit v5 on v4

--- a/solution.py
+++ b/solution.py
@@ -66,6 +66,25 @@
     )(grad, *arrived, *tokens)
 
 
+def stage_gradient(grad, tokens):
+    def body(grad_ref, *refs):
+        out_ref, sem = refs[-2:]
+        copy = pltpu.make_async_copy(grad_ref, out_ref, sem)
+        copy.start()
+        copy.wait()
+
+    return pl.pallas_call(
+        body,
+        out_shape=jax.ShapeDtypeStruct(grad.shape, grad.dtype),
+        in_specs=[IN_PLACE] + [ON_CHIP] * len(tokens),
+        out_specs=ON_CHIP,
+        scratch_shapes=[pltpu.SemaphoreType.DMA(())],
+        compiler_params=limits,
+        cost_estimate=cost(grad.size, 0, 2),
+        name="stage",
+    )(pltpu.with_memory_space_constraint(grad, pltpu.HBM), *tokens)
+
+
 def fetch_block(grad, table, places, rows):
     cols = grad.shape[1]
     chunk = min(rows, 8)
@@ -120,19 +139,15 @@
 
 def finish_block(grad, table, arrived, rows):
     cols = arrived[0].shape[1]
-    from_grad = [] if grad is None else [grad]
-
-    def body(*refs):
+
+    def body(grad_ref, *refs):
         out_ref, row_ref, col_ref = refs[-3:]
         start = pl.multiple_of(pick(table) * rows, rows)
-        sources = refs[len(from_grad) : len(from_grad) + len(arrived)]
         for k in range(cols // lanes):
             at = pl.ds(k * lanes, lanes)
-            values = sources[0][:, at]
-            for ref in sources[1:]:
+            values = grad_ref[pl.ds(start, rows), at].astype(jnp.float32)
+            for ref in refs[: len(arrived)]:
                 values = values + ref[:, at]
-            if from_grad:
-                values = values + refs[0][pl.ds(start, rows), at].astype(jnp.float32)
             out_ref[:, at] = values
             squares = values * values + tiny_add
             row_part = squares if k == 0 else row_part + squares
@@ -142,12 +157,12 @@
     return pl.pallas_call(
         body,
         out_shape=(f32(rows, cols), f32(rows, lanes), f32(1, cols)),
-        in_specs=[ON_CHIP] * (len(from_grad) + len(arrived)),
+        in_specs=[ON_CHIP] * (1 + len(arrived)),
         out_specs=(ON_CHIP,) * 3,
         compiler_params=limits,
         cost_estimate=cost(rows * cols, 6, 14),
         name="finish",
-    )(*from_grad, *arrived)
+    )(grad, *arrived)
 
 
 def diagonal(rows):
@@ -409,7 +424,7 @@
         shard, piece = order[min(max(m, 0), len(order) - 1)]
         return (last - shard) * pieces + piece
 
-    P, M, fetched = {}, {}, {}
+    P, M = {}, {}
     finished, new_row = {}, {}
     sums = []
 
@@ -419,8 +434,8 @@
     def settle(slot, extra=()):
         table = own_table(slot)
         counted = [int(slot <= 8), int(slot >= 8), int(slot >= 8), int(slot <= 8)]
-        arrived = [P[slot], M[slot], fetched[slot]] if slot >= 8 else [P[slot]]
-        gradient, row_part, col_part = finish_block(None if slot >= 8 else grad, table, arrived, rows)
+        arrived = [P[slot], M[slot]] if slot >= 8 else [P[slot]]
+        gradient, row_part, col_part = finish_block(staged, table, arrived, rows)
         row_parts = [row_part] + other_parts(row_part, "col")
         finished[slot] = gradient
         carried = [new_row[3], new_row[4]] if slot == 8 else []
@@ -431,18 +446,16 @@
 
     for slot in range(10):
         if slot >= 2:
-            operand = block_sum(grad, [0, right(slot - 2), left(slot - 2), 0], [P[slot - 2]], [], rows)
+            operand = block_sum(staged, [0, right(slot - 2), left(slot - 2), 0], [P[slot - 2]], [], rows)
             M[slot] = lax.ppermute(operand, "dp", middle)
         table = [right(slot), left(slot - 3), right(slot - 3), left(slot)]
         arrived = [M[slot - 1]] if slot >= 3 else []
         if slot < 2:
             operand = fetch_block(grad, table, [1, 0, 0, 1], rows)
+            staged = stage_gradient(grad, [operand])
         else:
-            tokens = [P[0]] if slot == 2 else list(fetched.values()) if slot == 7 else []
-            operand = block_sum(grad, table, arrived, tokens, rows)
+            operand = block_sum(staged, table, arrived, [P[0]] if slot == 2 else [], rows)
         P[slot] = lax.ppermute(operand, "dp", swap)
-        if slot == 5:
-            fetched |= {k: fetch_block(grad, own_table(k), [1, 1, 1, 1], rows) for k in (8, 9)}
         if 3 <= slot <= 8:
             settle(slot)
     early = lax.ppermute(sums[-1], "dp", outward)

time: 175 us -> 175 us (level)
  starting transfers between devices: 34.7 us -> 32.7 us
    pallas_call x0 -> x1, Pallas kernels: none -> 2.49 us  [stage_gradient(): pl.pallas_call(body, out_shape=jax.ShapeDtypeStruct(grad.shape, grad.dtyp...]
    pallas_call x4 -> x2, Pallas kernels: 2.31 us -> 0.18 us  [fetch_block(): pl.pallas_call(body, out_shape=f32(rows, cols), in_specs=[IN_PLACE], out_...]
  transfers between devices with their start and end apart: 33 -> 33, of which waited for: 25 -> 26; matrix products, arithmetic and copies ran while one was open for 0% -> 0% of each run, Pallas kernels for 5% -> 5%
where the time goes in v5:
time: 175 us; the launch traced here: 174 us
  waiting for transfers between devices  130 us (74%)
  starting transfers between devices  32.7 us (19%)
  Pallas kernels  10.1 us (6%)
    ppermute x10, waiting for transfers between devices, short_line(): P[slot] = lax.ppermute(operand, 'dp', swap)  97 us
    ppermute x8, starting transfers between devices, short_line(): M[slot] = lax.ppermute(operand, 'dp', middle)  15.4 us
    ppermute x1, waiting for transfers between devices, short_line(): early = lax.ppermute(sums[-1], 'dp', outward)  10.3 us
    ppermute x8, waiting for transfers between devices, short_line(): M[slot] = lax.ppermute(operand, 'dp', middle)  7.08 us
    ppermute x10, starting transfers between devices, short_line(): P[slot] = lax.ppermute(operand, 'dp', swap)  5.08 us
    ppermute x2, waiting for transfers between devices, axis_sum(): values = values + lax.ppermute(values, axis, pairs)  5 us
    ppermute x1, waiting for transfers between devices, short_line(): total = total + lax.ppermute(total, 'dp', middle)  3.97 us
  transfers between devices with their start and end apart: 33, of which 26 were waited for; matrix products, arithmetic and copies ran while one was open for 0% of the time, Pallas kernels for 5%

profile of v5, /device:TPU:16, one launch (start us, length us, event | category | flops | bytes accessed | tf_op | source)
XLA Modules:
  0.0 174.4 jit_solution(18272359620951042193)
XLA Ops:
  0.7 2.6 %collective-permute-start = (f32[32,5120]{1,0:T(8,128)S(1)}, f32[32,5120]{1,0:T(8,128)S(1)}, u32[]{:S(2)}, u32[]{:S(2)}) collective-permute-start(f32[32,5120]{1,0:T(8,128)S(1)} %fetch.3), channel_id=1, source_target_pairs={{0,8},{8,0},{16,24},{24,16},{1,9},{9,1},{17,25},{25,17},{2,10},{10... | collective-permute-start | bytes 1966088 | tf_op jit(solution)/shard_map/ppermute | solution.py:458
  4.5 2.5 %stage.1.grad_ref = bf16[512,5120]{1,0:T(8,128)(2,1)S(1)} custom-call(bf16[512,5120]{1,0:T(8,128)(2,1)} %bitcast.9, f32[32,5120]{1,0:T(8,128)S(1)} %fetch.2.refs_0_), custom_call_target="tpu_custom_call" | custom-call | bytes 5242880 | tf_op jit(solution)/shard_map/stage/pallas_call | solution.py:76
  7.0 11.9 %collective-permute-done.refs_0_ = f32[32,5120]{1,0:T(8,128)S(1)} collective-permute-done((f32[32,5120]{1,0:T(8,128)S(1)}, f32[32,5120]{1,0:T(8,128)S(1)}, u32[]{:S(2)}, u32[]{:S(2)}) %collective-permute-start) | collective-permute-done | bytes 655392 | tf_op jit(solution)/shard_map/ppermute | solution.py:458
  19.0 1.9 %collective-permute-start.1 = (f32[32,5120]{1,0:T(8,128)S(1)}, f32[32,5120]{1,0:T(8,128)S(1)}, u32[]{:S(2)}, u32[]{:S(2)}) collective-permute-start(f32[32,5120]{1,0:T(8,128)S(1)} %block.16), channel_id=1, source_target_pairs={{8,16},{16,8},{9,17},{17,9},{10,18},{18,10},{11,19},{19,11},{12,20... | collective-permute-start | bytes 1966088 | tf_op jit(solution)/shard_map/ppermute | solution.py:450
  21.9 11.1 %collective-permute-done.7.refs_0_ = f32[32,5120]{1,0:T(8,128)S(1)} collective-permute-done((f32[32,5120]{1,0:T(8,128)S(1)}, f32[32,5120]{1,0:T(8,128)S(1)}, u32[]{:S(2)}, u32[]{:S(2)}) %collective-permute-start.7) | collective-permute-done | bytes 655392 | tf_op jit(solution)/shard_map/ppermute | solution.py:458
  33.0 1.9 %collective-permute-start.8 = (f32[32,5120]{1,0:T(8,128)S(1)}, f32[32,5120]{1,0:T(8,128)S(1)}, u32[]{:S(2)}, u32[]{:S(2)}) collective-permute-start(f32[32,5120]{1,0:T(8,128)S(1)} %block.22), channel_id=1, source_target_pairs={{8,16},{16,8},{9,17},{17,9},{10,18},{18,10},{11,19},{19,11},{12,20... | collective-permute-start | bytes 1966088 | tf_op jit(solution)/shard_map/ppermute | solution.py:450
  36.1 10.9 %collective-permute-done.14.refs_0_ = f32[32,5120]{1,0:T(8,128)S(1)} collective-permute-done((f32[32,5120]{1,0:T(8,128)S(1)}, f32[32,5120]{1,0:T(8,128)S(1)}, u32[]{:S(2)}, u32[]{:S(2)}) %collective-permute-start.14) | collective-permute-done | bytes 655392 | tf_op jit(solution)/shard_map/ppermute | solution.py:458
  47.1 1.9 %collective-permute-start.15 = (f32[32,5120]{1,0:T(8,128)S(1)}, f32[32,5120]{1,0:T(8,128)S(1)}, u32[]{:S(2)}, u32[]{:S(2)}) collective-permute-start(f32[32,5120]{1,0:T(8,128)S(1)} %block.28), channel_id=1, source_target_pairs={{8,16},{16,8},{9,17},{17,9},{10,18},{18,10},{11,19},{19,11},{12,20... | collective-permute-start | bytes 1966088 | tf_op jit(solution)/shard_map/ppermute | solution.py:450
  50.1 10.9 %collective-permute-done.2.refs_0_ = f32[32,5120]{1,0:T(8,128)S(1)} collective-permute-done((f32[32,5120]{1,0:T(8,128)S(1)}, f32[32,5120]{1,0:T(8,128)S(1)}, u32[]{:S(2)}, u32[]{:S(2)}) %collective-permute-start.2) | collective-permute-done | bytes 655392 | tf_op jit(solution)/shard_map/ppermute | solution.py:458
  61.1 1.9 %collective-permute-start.3 = (f32[32,5120]{1,0:T(8,128)S(1)}, f32[32,5120]{1,0:T(8,128)S(1)}, u32[]{:S(2)}, u32[]{:S(2)}) collective-permute-start(f32[32,5120]{1,0:T(8,128)S(1)} %block.18), channel_id=1, source_target_pairs={{8,16},{16,8},{9,17},{17,9},{10,18},{18,10},{11,19},{19,11},{12,20... | collective-permute-start | bytes 1966088 | tf_op jit(solution)/shard_map/ppermute | solution.py:450
  64.2 10.9 %collective-permute-done.9.refs_0_ = f32[32,5120]{1,0:T(8,128)S(1)} collective-permute-done((f32[32,5120]{1,0:T(8,128)S(1)}, f32[32,5120]{1,0:T(8,128)S(1)}, u32[]{:S(2)}, u32[]{:S(2)}) %collective-permute-start.9) | collective-permute-done | bytes 655392 | tf_op jit(solution)/shard_map/ppermute | solution.py:458
  75.1 1.9 %collective-permute-start.10 = (f32[32,5120]{1,0:T(8,128)S(1)}, f32[32,5120]{1,0:T(8,128)S(1)}, u32[]{:S(2)}, u32[]{:S(2)}) collective-permute-start(f32[32,5120]{1,0:T(8,128)S(1)} %block.24), channel_id=1, source_target_pairs={{8,16},{16,8},{9,17},{17,9},{10,18},{18,10},{11,19},{19,11},{12,20... | collective-permute-start | bytes 1966088 | tf_op jit(solution)/shard_map/ppermute | solution.py:450
  78.2 10.9 %collective-permute-done.16.refs_0_ = f32[32,5120]{1,0:T(8,128)S(1)} collective-permute-done((f32[32,5120]{1,0:T(8,128)S(1)}, f32[32,5120]{1,0:T(8,128)S(1)}, u32[]{:S(2)}, u32[]{:S(2)}) %collective-permute-start.16) | collective-permute-done | bytes 655392 | tf_op jit(solution)/shard_map/ppermute | solution.py:458
  89.2 1.9 %collective-permute-start.17 = (f32[32,5120]{1,0:T(8,128)S(1)}, f32[32,5120]{1,0:T(8,128)S(1)}, u32[]{:S(2)}, u32[]{:S(2)}) collective-permute-start(f32[32,5120]{1,0:T(8,128)S(1)} %block.30), channel_id=1, source_target_pairs={{8,16},{16,8},{9,17},{17,9},{10,18},{18,10},{11,19},{19,11},{12,20... | collective-permute-start | bytes 1966088 | tf_op jit(solution)/shard_map/ppermute | solution.py:450
  92.3 10.9 %collective-permute-done.4.refs_0_ = f32[32,5120]{1,0:T(8,128)S(1)} collective-permute-done((f32[32,5120]{1,0:T(8,128)S(1)}, f32[32,5120]{1,0:T(8,128)S(1)}, u32[]{:S(2)}, u32[]{:S(2)}) %collective-permute-start.4) | collective-permute-done | bytes 655392 | tf_op jit(solution)/shard_map/ppermute | solution.py:458
  103.2 1.9 %collective-permute-start.5 = (f32[32,5120]{1,0:T(8,128)S(1)}, f32[32,5120]{1,0:T(8,128)S(1)}, u32[]{:S(2)}, u32[]{:S(2)}) collective-permute-start(f32[32,5120]{1,0:T(8,128)S(1)} %block.20), channel_id=1, source_target_pairs={{8,16},{16,8},{9,17},{17,9},{10,18},{18,10},{11,19},{19,11},{12,20... | collective-permute-start | bytes 1966088 | tf_op jit(solution)/shard_map/ppermute | solution.py:450
  106.3 10.9 %collective-permute-done.11.refs_0_ = f32[32,5120]{1,0:T(8,128)S(1)} collective-permute-done((f32[32,5120]{1,0:T(8,128)S(1)}, f32[32,5120]{1,0:T(8,128)S(1)}, u32[]{:S(2)}, u32[]{:S(2)}) %collective-permute-start.11) | collective-permute-done | bytes 655392 | tf_op jit(solution)/shard_map/ppermute | solution.py:458
  117.3 1.9 %collective-permute-start.12 = (f32[32,5120]{1,0:T(8,128)S(1)}, f32[32,5120]{1,0:T(8,128)S(1)}, u32[]{:S(2)}, u32[]{:S(2)}) collective-permute-start(f32[32,5120]{1,0:T(8,128)S(1)} %block.26), channel_id=1, source_target_pairs={{8,16},{16,8},{9,17},{17,9},{10,18},{18,10},{11,19},{19,11},{12,20... | collective-permute-start | bytes 1966088 | tf_op jit(solution)/shard_map/ppermute | solution.py:450
  122.7 8.6 %collective-permute-done.18.refs_0_ = f32[32,5120]{1,0:T(8,128)S(1)} collective-permute-done((f32[32,5120]{1,0:T(8,128)S(1)}, f32[32,5120]{1,0:T(8,128)S(1)}, u32[]{:S(2)}, u32[]{:S(2)}) %collective-permute-start.18) | collective-permute-done | bytes 655392 | tf_op jit(solution)/shard_map/ppermute | solution.py:458
  133.3 1.3 collective-permute-start.25
  134.7 1.3 collective-permute-start.30
  136.0 10.3 %collective-permute-done.25.refs_3_.sums_ref.refs_1_ = f32[1,10624]{1,0:T(1,128)S(1)} collective-permute-done((f32[1,10624]{1,0:T(1,128)S(1)}, f32[1,10624]{1,0:T(1,128)S(1)}, u32[]{:S(2)}, u32[]{:S(2)}) %collective-permute-start.25) | collective-permute-done | bytes 42528 | tf_op jit(solution)/shard_map/ppermute | solution.py:461
  146.3 1.6 collective-permute-start.32
  149.5 1.6 collective-permute-start.26
  151.1 2.5 %collective-permute-done.26 = f32[1,10368]{1,0:T(1,128)S(1)} collective-permute-done((f32[1,10368]{1,0:T(1,128)S(1)}, f32[1,10368]{1,0:T(1,128)S(1)}, u32[]{:S(2)}, u32[]{:S(2)}) %collective-permute-start.26) | collective-permute-done | bytes 41504 | tf_op jit(solution)/shard_map/ppermute | solution.py:30
  153.6 1.6 collective-permute-start.27
  155.2 2.5 %collective-permute-done.27 = f32[1,10368]{1,0:T(1,128)S(1)} collective-permute-done((f32[1,10368]{1,0:T(1,128)S(1)}, f32[1,10368]{1,0:T(1,128)S(1)}, u32[]{:S(2)}, u32[]{:S(2)}) %collective-permute-start.27) | collective-permute-done | bytes 41504 | tf_op jit(solution)/shard_map/ppermute | solution.py:30
  157.8 1.9 %collective-permute-start.28 = (f32[1,10368]{1,0:T(1,128)S(1)}, f32[1,10368]{1,0:T(1,128)S(1)}, u32[]{:S(2)}, u32[]{:S(2)}) collective-permute-start(f32[1,10368]{1,0:T(1,128)S(1)} %add.10), channel_id=1, source_target_pairs={{8,16},{16,8},{9,17},{17,9},{10,18},{18,10},{11,19},{19,11},{12,20... | collective-permute-start | bytes 124424 | tf_op jit(solution)/shard_map/ppermute | solution.py:468
  159.7 4.0 %collective-permute-done.28 = f32[1,10368]{1,0:T(1,128)S(1)} collective-permute-done((f32[1,10368]{1,0:T(1,128)S(1)}, f32[1,10368]{1,0:T(1,128)S(1)}, u32[]{:S(2)}, u32[]{:S(2)}) %collective-permute-start.28) | collective-permute-done | bytes 41504 | tf_op jit(solution)/shard_map/ppermute | solution.py:468
  165.0 1.7 collective-permute-done.29.refs_0_
  168.4 1.7 apply.1
  170.2 3.3 %collective-permute-done.32.refs_1_ = f32[32,5120]{1,0:T(8,128)S(1)} collective-permute-done((f32[32,5120]{1,0:T(8,128)S(1)}, f32[32,5120]{1,0:T(8,128)S(1)}, u32[]{:S(2)}, u32[]{:S(2)}) %collective-permute-start.32) | collective-permute-done | bytes 655392 | tf_op jit(solution)/shard_map/ppermute | solution.py:465
  (84 shorter events, 20.8 us)
Async XLA Ops:
  0.7 18.2 %collective-permute-start = (f32[32,5120]{1,0:T(8,128)S(1)}, f32[32,5120]{1,0:T(8,128)S(1)}, u32[]{:S(2)}, u32[]{:S(2)}) collective-permute-start(f32[32,5120]{1,0:T(8,128)S(1)} %fetch.3), channel_id=1, source_target_pairs={{0,8},{8,0},{16,24},{24,16},{1,9},{9,1},{17,25},{25,17},{2,10},{10... | collective-permute-start | bytes 1966088 | tf_op jit(solution)/shard_map/ppermute | solution.py:458
  3.4 29.5 %collective-permute-start.7 = (f32[32,5120]{1,0:T(8,128)S(1)}, f32[32,5120]{1,0:T(8,128)S(1)}, u32[]{:S(2)}, u32[]{:S(2)}) collective-permute-start(f32[32,5120]{1,0:T(8,128)S(1)} %fetch.2.refs_0_), channel_id=1, source_target_pairs={{0,8},{8,0},{16,24},{24,16},{1,9},{9,1},{17,25},{25,17},{2,10},{10... | collective-permute-start | bytes 1966088 | tf_op jit(solution)/shard_map/ppermute | solution.py:458
  19.0 17.0 %collective-permute-start.1 = (f32[32,5120]{1,0:T(8,128)S(1)}, f32[32,5120]{1,0:T(8,128)S(1)}, u32[]{:S(2)}, u32[]{:S(2)}) collective-permute-start(f32[32,5120]{1,0:T(8,128)S(1)} %block.16), channel_id=1, source_target_pairs={{8,16},{16,8},{9,17},{17,9},{10,18},{18,10},{11,19},{19,11},{12,20... | collective-permute-start | bytes 1966088 | tf_op jit(solution)/shard_map/ppermute | solution.py:450
  21.0 26.0 %collective-permute-start.14 = (f32[32,5120]{1,0:T(8,128)S(1)}, f32[32,5120]{1,0:T(8,128)S(1)}, u32[]{:S(2)}, u32[]{:S(2)}) collective-permute-start(f32[32,5120]{1,0:T(8,128)S(1)} %block.27), channel_id=1, source_target_pairs={{0,8},{8,0},{16,24},{24,16},{1,9},{9,1},{17,25},{25,17},{2,10},{10... | collective-permute-start | bytes 1966088 | tf_op jit(solution)/shard_map/ppermute | solution.py:458
  33.0 17.0 %collective-permute-start.8 = (f32[32,5120]{1,0:T(8,128)S(1)}, f32[32,5120]{1,0:T(8,128)S(1)}, u32[]{:S(2)}, u32[]{:S(2)}) collective-permute-start(f32[32,5120]{1,0:T(8,128)S(1)} %block.22), channel_id=1, source_target_pairs={{8,16},{16,8},{9,17},{17,9},{10,18},{18,10},{11,19},{19,11},{12,20... | collective-permute-start | bytes 1966088 | tf_op jit(solution)/shard_map/ppermute | solution.py:450
  36.0 25.0 %collective-permute-start.2 = (f32[32,5120]{1,0:T(8,128)S(1)}, f32[32,5120]{1,0:T(8,128)S(1)}, u32[]{:S(2)}, u32[]{:S(2)}) collective-permute-start(f32[32,5120]{1,0:T(8,128)S(1)} %block.17), channel_id=1, source_target_pairs={{0,8},{8,0},{16,24},{24,16},{1,9},{9,1},{17,25},{25,17},{2,10},{10... | collective-permute-start | bytes 1966088 | tf_op jit(solution)/shard_map/ppermute | solution.py:458
  47.1 17.0 %collective-permute-start.15 = (f32[32,5120]{1,0:T(8,128)S(1)}, f32[32,5120]{1,0:T(8,128)S(1)}, u32[]{:S(2)}, u32[]{:S(2)}) collective-permute-start(f32[32,5120]{1,0:T(8,128)S(1)} %block.28), channel_id=1, source_target_pairs={{8,16},{16,8},{9,17},{17,9},{10,18},{18,10},{11,19},{19,11},{12,20... | collective-permute-start | bytes 1966088 | tf_op jit(solution)/shard_map/ppermute | solution.py:450
  50.1 25.0 %collective-permute-start.9 = (f32[32,5120]{1,0:T(8,128)S(1)}, f32[32,5120]{1,0:T(8,128)S(1)}, u32[]{:S(2)}, u32[]{:S(2)}) collective-permute-start(f32[32,5120]{1,0:T(8,128)S(1)} %block.23), channel_id=1, source_target_pairs={{0,8},{8,0},{16,24},{24,16},{1,9},{9,1},{17,25},{25,17},{2,10},{10... | collective-permute-start | bytes 1966088 | tf_op jit(solution)/shard_map/ppermute | solution.py:458
  61.1 17.0 %collective-permute-start.3 = (f32[32,5120]{1,0:T(8,128)S(1)}, f32[32,5120]{1,0:T(8,128)S(1)}, u32[]{:S(2)}, u32[]{:S(2)}) collective-permute-start(f32[32,5120]{1,0:T(8,128)S(1)} %block.18), channel_id=1, source_target_pairs={{8,16},{16,8},{9,17},{17,9},{10,18},{18,10},{11,19},{19,11},{12,20... | collective-permute-start | bytes 1966088 | tf_op jit(solution)/shard_map/ppermute | solution.py:450
  64.1 25.0 %collective-permute-start.16 = (f32[32,5120]{1,0:T(8,128)S(1)}, f32[32,5120]{1,0:T(8,128)S(1)}, u32[]{:S(2)}, u32[]{:S(2)}) collective-permute-start(f32[32,5120]{1,0:T(8,128)S(1)} %block.29), channel_id=1, source_target_pairs={{0,8},{8,0},{16,24},{24,16},{1,9},{9,1},{17,25},{25,17},{2,10},{10... | collective-permute-start | bytes 1966088 | tf_op jit(solution)/shard_map/ppermute | solution.py:458
  75.1 17.0 %collective-permute-start.10 = (f32[32,5120]{1,0:T(8,128)S(1)}, f32[32,5120]{1,0:T(8,128)S(1)}, u32[]{:S(2)}, u32[]{:S(2)}) collective-permute-start(f32[32,5120]{1,0:T(8,128)S(1)} %block.24), channel_id=1, source_target_pairs={{8,16},{16,8},{9,17},{17,9},{10,18},{18,10},{11,19},{19,11},{12,20... | collective-permute-start | bytes 1966088 | tf_op jit(solution)/shard_map/ppermute | solution.py:450
  78.1 25.0 %collective-permute-start.4 = (f32[32,5120]{1,0:T(8,128)S(1)}, f32[32,5120]{1,0:T(8,128)S(1)}, u32[]{:S(2)}, u32[]{:S(2)}) collective-permute-start(f32[32,5120]{1,0:T(8,128)S(1)} %block.19), channel_id=1, source_target_pairs={{0,8},{8,0},{16,24},{24,16},{1,9},{9,1},{17,25},{25,17},{2,10},{10... | collective-permute-start | bytes 1966088 | tf_op jit(solution)/shard_map/ppermute | solution.py:458
  89.2 17.0 %collective-permute-start.17 = (f32[32,5120]{1,0:T(8,128)S(1)}, f32[32,5120]{1,0:T(8,128)S(1)}, u32[]{:S(2)}, u32[]{:S(2)}) collective-permute-start(f32[32,5120]{1,0:T(8,128)S(1)} %block.30), channel_id=1, source_target_pairs={{8,16},{16,8},{9,17},{17,9},{10,18},{18,10},{11,19},{19,11},{12,20... | collective-permute-start | bytes 1966088 | tf_op jit(solution)/shard_map/ppermute | solution.py:450
  92.2 25.0 %collective-permute-start.11 = (f32[32,5120]{1,0:T(8,128)S(1)}, f32[32,5120]{1,0:T(8,128)S(1)}, u32[]{:S(2)}, u32[]{:S(2)}) collective-permute-start(f32[32,5120]{1,0:T(8,128)S(1)} %block.25), channel_id=1, source_target_pairs={{0,8},{8,0},{16,24},{24,16},{1,9},{9,1},{17,25},{25,17},{2,10},{10... | collective-permute-start | bytes 1966088 | tf_op jit(solution)/shard_map/ppermute | solution.py:458
  103.2 17.0 %collective-permute-start.5 = (f32[32,5120]{1,0:T(8,128)S(1)}, f32[32,5120]{1,0:T(8,128)S(1)}, u32[]{:S(2)}, u32[]{:S(2)}) collective-permute-start(f32[32,5120]{1,0:T(8,128)S(1)} %block.20), channel_id=1, source_target_pairs={{8,16},{16,8},{9,17},{17,9},{10,18},{18,10},{11,19},{19,11},{12,20... | collective-permute-start | bytes 1966088 | tf_op jit(solution)/shard_map/ppermute | solution.py:450
  106.2 25.0 %collective-permute-start.18 = (f32[32,5120]{1,0:T(8,128)S(1)}, f32[32,5120]{1,0:T(8,128)S(1)}, u32[]{:S(2)}, u32[]{:S(2)}) collective-permute-start(f32[32,5120]{1,0:T(8,128)S(1)} %block.31), channel_id=1, source_target_pairs={{0,8},{8,0},{16,24},{24,16},{1,9},{9,1},{17,25},{25,17},{2,10},{10... | collective-permute-start | bytes 1966088 | tf_op jit(solution)/shard_map/ppermute | solution.py:458
  117.3 30.6 %collective-permute-start.12 = (f32[32,5120]{1,0:T(8,128)S(1)}, f32[32,5120]{1,0:T(8,128)S(1)}, u32[]{:S(2)}, u32[]{:S(2)}) collective-permute-start(f32[32,5120]{1,0:T(8,128)S(1)} %block.26), channel_id=1, source_target_pairs={{8,16},{16,8},{9,17},{17,9},{10,18},{18,10},{11,19},{19,11},{12,20... | collective-permute-start | bytes 1966088 | tf_op jit(solution)/shard_map/ppermute | solution.py:450
  120.3 27.6 %collective-permute-start.6 = (f32[32,5120]{1,0:T(8,128)S(1)}, f32[32,5120]{1,0:T(8,128)S(1)}, u32[]{:S(2)}, u32[]{:S(2)}) collective-permute-start(f32[32,5120]{1,0:T(8,128)S(1)} %block.21), channel_id=1, source_target_pairs={{0,8},{8,0},{16,24},{24,16},{1,9},{9,1},{17,25},{25,17},{2,10},{10... | collective-permute-start | bytes 1966088 | tf_op jit(solution)/shard_map/ppermute | solution.py:458
  120.5 1.2 collective-permute-start.23
  120.8 1.4 collective-permute-start.24
  121.8 9.7 %collective-permute-start.22 = (f32[32,128]{1,0:T(8,128)S(1)}, f32[32,128]{1,0:T(8,128)S(1)}, u32[]{:S(2)}, u32[]{:S(2)}) collective-permute-start(f32[32,128]{1,0:T(8,128)S(1)} %get-tuple-element.61.refs_0_), channel_id=1, source_target_pairs={{0,1},{1,0},{2,3},{3,2},{4,5},{5,4},{6,7},{7,6},{8,9},{9,8},{10,11... | collective-permute-start | bytes 49160 | tf_op jit(solution)/shard_map/ppermute | solution.py:37
  122.2 10.5 %collective-permute-start.21 = (f32[32,128]{1,0:T(8,128)S(1)}, f32[32,128]{1,0:T(8,128)S(1)}, u32[]{:S(2)}, u32[]{:S(2)}) collective-permute-start(f32[32,128]{1,0:T(8,128)S(1)} %get-tuple-element.58.refs_0_), channel_id=1, source_target_pairs={{0,1},{1,0},{2,3},{3,2},{4,5},{5,4},{6,7},{7,6},{8,9},{9,8},{10,11... | collective-permute-start | bytes 49160 | tf_op jit(solution)/shard_map/ppermute | solution.py:37
  131.3 1.7 collective-permute-start.20
  131.5 1.6 collective-permute-start.19
  133.3 12.9 %collective-permute-start.25 = (f32[1,10624]{1,0:T(1,128)S(1)}, f32[1,10624]{1,0:T(1,128)S(1)}, u32[]{:S(2)}, u32[]{:S(2)}) collective-permute-start(f32[1,10624]{1,0:T(1,128)S(1)} %get-tuple-element.75.refs_2_.refs_0_), channel_id=1, source_target_pairs={{0,8},{24,16},{1,9},{25,17},{2,10},{26,18},{3,11},{27,19},{4,12},{... | collective-permute-start | bytes 127496 | tf_op jit(solution)/shard_map/ppermute | solution.py:461
  134.7 33.3 %collective-permute-start.30 = (f32[32,5120]{1,0:T(8,128)S(1)}, f32[32,5120]{1,0:T(8,128)S(1)}, u32[]{:S(2)}, u32[]{:S(2)}) collective-permute-start(f32[32,5120]{1,0:T(8,128)S(1)} %pass.2.refs_0_), channel_id=1, source_target_pairs={{0,8},{24,16},{1,9},{25,17},{2,10},{26,18},{3,11},{27,19},{4,12},{... | collective-permute-start | bytes 1966088 | tf_op jit(solution)/shard_map/ppermute | solution.py:464
  146.3 27.2 %collective-permute-start.32 = (f32[32,5120]{1,0:T(8,128)S(1)}, f32[32,5120]{1,0:T(8,128)S(1)}, u32[]{:S(2)}, u32[]{:S(2)}) collective-permute-start(f32[32,5120]{1,0:T(8,128)S(1)} %pass.3), channel_id=1, source_target_pairs={{0,8},{24,16},{1,9},{25,17},{2,10},{26,18},{3,11},{27,19},{4,12},{... | collective-permute-start | bytes 1966088 | tf_op jit(solution)/shard_map/ppermute | solution.py:465
  148.1 1.2 collective-permute-start.13
  149.5 4.1 %collective-permute-start.26 = (f32[1,10368]{1,0:T(1,128)S(1)}, f32[1,10368]{1,0:T(1,128)S(1)}, u32[]{:S(2)}, u32[]{:S(2)}) collective-permute-start(f32[1,10368]{1,0:T(1,128)S(1)} %get-tuple-element.76), channel_id=1, source_target_pairs={{0,2},{2,0},{4,6},{6,4},{1,3},{3,1},{5,7},{7,5},{8,10},{10,8},{12,... | collective-permute-start | bytes 124424 | tf_op jit(solution)/shard_map/ppermute | solution.py:30
  153.6 4.1 %collective-permute-start.27 = (f32[1,10368]{1,0:T(1,128)S(1)}, f32[1,10368]{1,0:T(1,128)S(1)}, u32[]{:S(2)}, u32[]{:S(2)}) collective-permute-start(f32[1,10368]{1,0:T(1,128)S(1)} %add.9), channel_id=1, source_target_pairs={{0,4},{2,6},{4,0},{6,2},{1,5},{3,7},{5,1},{7,3},{8,12},{10,14},{12... | collective-permute-start | bytes 124424 | tf_op jit(solution)/shard_map/ppermute | solution.py:30
  157.8 5.9 %collective-permute-start.28 = (f32[1,10368]{1,0:T(1,128)S(1)}, f32[1,10368]{1,0:T(1,128)S(1)}, u32[]{:S(2)}, u32[]{:S(2)}) collective-permute-start(f32[1,10368]{1,0:T(1,128)S(1)} %add.10), channel_id=1, source_target_pairs={{8,16},{16,8},{9,17},{17,9},{10,18},{18,10},{11,19},{19,11},{12,20... | collective-permute-start | bytes 124424 | tf_op jit(solution)/shard_map/ppermute | solution.py:468
  163.7 3.0 %collective-permute-start.29 = (f32[1,10368]{1,0:T(1,128)S(1)}, f32[1,10368]{1,0:T(1,128)S(1)}, u32[]{:S(2)}, u32[]{:S(2)}) collective-permute-start(f32[1,10368]{1,0:T(1,128)S(1)} %add.11.sums_ref), channel_id=1, source_target_pairs={{8,0},{16,24},{9,1},{17,25},{10,2},{18,26},{11,3},{19,27},{12,4},{... | collective-permute-start | bytes 124424 | tf_op jit(solution)/shard_map/ppermute | solution.py:469
  (4 other events, 44.5 us)

commit v6 on v5

--- a/solution.py
+++ b/solution.py
@@ -170,10 +170,55 @@
     return row == lax.broadcasted_iota(jnp.int32, (rows, lanes), 1)
 
 
+def half_of(side, cols, k):
+    return pl.ds(pl.multiple_of(side * (cols // 2) + k * lanes, lanes), lanes)
+
+
+def other_half(sums, cols):
+    def body(sums_ref, out_ref):
+        side = 1 - lax.rem(lax.axis_index("row"), 2)
+        for k in range(cols // 2 // lanes):
+            out_ref[:, pl.ds(k * lanes, lanes)] = sums_ref[:, half_of(side, cols, k)]
+            out_ref[:, pl.ds(cols // 2 + k * lanes, lanes)] = sums_ref[:, half_of(side + 2, cols, k)]
+
+    return pl.pallas_call(
+        body,
+        out_shape=f32(1, cols),
+        in_specs=[ON_CHIP],
+        out_specs=ON_CHIP,
+        compiler_params=limits,
+        cost_estimate=cost(cols, 1, 8),
+        name="half",
+    )(sums)
+
+
+def joined_half(sums, received, cols):
+    width = sums.shape[1] - cols
+
+    def body(sums_ref, received_ref, out_ref):
+        side = lax.rem(lax.axis_index("row"), 2)
+        for k in range(cols // 2 // lanes):
+            at = pl.ds(k * lanes, lanes)
+            out_ref[:, at] = sums_ref[:, half_of(side, cols, k)] + received_ref[:, at]
+            at = pl.ds(cols // 2 + k * lanes, lanes)
+            out_ref[:, at] = sums_ref[:, half_of(side + 2, cols, k)] + received_ref[:, at]
+        out_ref[:, cols:width] = sums_ref[:, 2 * cols : cols + width]
+
+    return pl.pallas_call(
+        body,
+        out_shape=f32(1, width),
+        in_specs=[ON_CHIP] * 2,
+        out_specs=ON_CHIP,
+        compiler_params=limits,
+        cost_estimate=cost(cols, 1, 12),
+        name="joined",
+    )(sums, received)
+
+
 def unpack_rows(sums, cols, count, rows):
     def body(sums_ref, *outs):
         for k, out in enumerate(outs):
-            values = sums_ref[:, pl.ds(2 * cols + (k + 1) * lanes, lanes)]
+            values = sums_ref[:, pl.ds(cols + (k + 1) * lanes, lanes)]
             column = jnp.sum(jnp.where(diagonal(rows), values, 0.0), axis=1, keepdims=True)
             out[...] = jnp.broadcast_to(column, (rows, lanes))
 
@@ -188,7 +233,7 @@
     )(sums)
 
 
-def scale_block(gradient, table, counted, row_parts, old_rows, col_part, held, carried, hidden_width):
+def scale_block(gradient, table, counted, row_parts, old_rows, col_part, held, halves, carried, hidden_width):
     rows, cols = gradient.shape
 
     def body(grad_ref, col_ref, old_ref, *refs):
@@ -212,7 +257,7 @@
 
         put(pl.ds(2 * cols, lanes), jnp.sum(row, axis=0, keepdims=True))
         for k in range(len(carried)):
-            values = refs[len(row_parts) + len(held) + k][...]
+            values = refs[len(row_parts) + len(held) + len(halves) + k][...]
             at = pl.ds(2 * cols + (k + 1) * lanes, lanes)
             sums_out[:, at] = jnp.sum(jnp.where(diagonal(rows), values, 0.0), axis=0, keepdims=True)
         for k in range(cols // lanes):
@@ -220,16 +265,22 @@
             values = grad_ref[:, at]
             put(at, col_ref[:, at])
             put(pl.ds(cols + k * lanes, lanes), jnp.sum(values * values * inverse, axis=0, keepdims=True))
+        for half in refs[len(row_parts) + len(held) : len(row_parts) + len(held) + len(halves)]:
+            side = lax.rem(lax.axis_index("row"), 2)
+            for k in range(cols // 2 // lanes):
+                sums_out[:, half_of(side, cols, k)] += half[:, pl.ds(k * lanes, lanes)]
+                sums_out[:, half_of(side + 2, cols, k)] += half[:, pl.ds(cols // 2 + k * lanes, lanes)]
+            sums_out[:, pl.ds(2 * cols, lanes)] += half[:, pl.ds(cols, lanes)]
 
     return pl.pallas_call(
         body,
         out_shape=(f32(rows, lanes), f32(1, 2 * cols + (1 + len(carried)) * lanes)),
-        in_specs=[ON_CHIP] * (3 + len(row_parts) + len(held) + len(carried)),
+        in_specs=[ON_CHIP] * (3 + len(row_parts) + len(held) + len(halves) + len(carried)),
         out_specs=(ON_CHIP, ON_CHIP),
         compiler_params=limits,
         cost_estimate=cost(rows * cols, 4, 4),
         name="scale",
-    )(gradient, col_part, old_rows, *row_parts, *held, *carried)
+    )(gradient, col_part, old_rows, *row_parts, *held, *halves, *carried)
 
 
 def column_factor(sums, extra, old_cols, matrix_rows):
@@ -440,7 +491,7 @@
         finished[slot] = gradient
         carried = [new_row[3], new_row[4]] if slot == 8 else []
         new_row[slot], total = scale_block(
-            gradient, table, counted, row_parts, old_rows, col_part, [*sums[-1:], *extra], carried, hidden_width
+            gradient, table, counted, row_parts, old_rows, col_part, sums[-1:], list(extra), carried, hidden_width
         )
         sums.append(total)
 
@@ -458,7 +509,10 @@
         P[slot] = lax.ppermute(operand, "dp", swap)
         if 3 <= slot <= 8:
             settle(slot)
-    early = lax.ppermute(sums[-1], "dp", outward)
+    cols = grad.shape[1]
+    side = lax.axis_size("row")
+    received = lax.ppermute(other_half(sums[-1], cols), "row", [(i, i ^ 1) for i in range(side)])
+    early = lax.ppermute(joined_half(sums[-1], received, cols), "dp", outward)
     late_rows = unpack_rows(early, grad.shape[1], 2, rows)
     operand = pass_on(finished[3], [sums[-1]])
     P[10] = lax.ppermute(operand, "dp", outward)
@@ -496,7 +550,7 @@
         grad_piece, row_part, col_part = finish_block(grad, table, [rights[slot], lefts[slot]], rows)
         row_parts = [row_part] + other_parts(row_part, "col")
         row_piece, sums = scale_block(
-            grad_piece, table, [1] * replicas, row_parts, old_rows, col_part, held, [], hidden_width
+            grad_piece, table, [1] * replicas, row_parts, old_rows, col_part, held, [], [], hidden_width
         )
         held = [sums]
         gradient.append(grad_piece)
@@ -518,7 +572,8 @@
     weights = params.reshape(owned_rows, local_cols)
     old_rows = jnp.broadcast_to(row_second.reshape(slab_rows, 1), (slab_rows, lanes))
     old_cols = col_second.reshape(1, local_cols)
-    line = short_line if replicas == 4 and pieces == 4 else long_line
+    short = replicas == 4 and pieces == 4 and lax.axis_size("row") % 2 == 0 and local_cols % (2 * lanes) == 0
+    line = short_line if short else long_line
     total, extra, choices = line(grad, old_rows, hidden_width, pieces, rows)
     new_col, col_scale, update_part, row_mean = column_factor(total, extra, old_cols, matrix_rows)
     updates = [update_part] + other_parts(update_part, "col")

time: 175 us -> 174 us (level)
  waiting for transfers between devices: 130 us -> 128 us
    ppermute x1 -> x2, waiting for transfers between devices: 10.3 us -> 8.16 us  [the longest x1 5.87 us: short_line(): early = lax.ppermute(joined_half(sums[-1], received, cols), 'dp', outward)]
  transfers between devices with their start and end apart: 33 -> 34, of which waited for: 26 -> 27; matrix products, arithmetic and copies ran while one was open for 0% -> 0% of each run, Pallas kernels for 5% -> 5%
where the time goes in v6:
time: 174 us
  waiting for transfers between devices  128 us (74%)
  starting transfers between devices  34.3 us (20%)
  Pallas kernels  10.2 us (6%)
    ppermute x10, waiting for transfers between devices, short_line(): P[slot] = lax.ppermute(operand, 'dp', swap)  97 us
    ppermute x8, starting transfers between devices, short_line(): M[slot] = lax.ppermute(operand, 'dp', middle)  15.4 us
    ppermute x8, waiting for transfers between devices, short_line(): M[slot] = lax.ppermute(operand, 'dp', middle)  7.08 us
    ppermute x1, waiting for transfers between devices, short_line(): early = lax.ppermute(joined_half(sums[-1], received, cols), 'dp', outward)  5.87 us
    ppermute x10, starting transfers between devices, short_line(): P[slot] = lax.ppermute(operand, 'dp', swap)  5.08 us
    ppermute x2, waiting for transfers between devices, axis_sum(): values = values + lax.ppermute(values, axis, pairs)  5 us
    ppermute x1, waiting for transfers between devices, short_line(): total = total + lax.ppermute(total, 'dp', middle)  3.97 us
  transfers between devices with their start and end apart: 34, of which 27 were waited for; matrix products, arithmetic and copies ran while one was open for 0% of the time, Pallas kernels for 5%

profile of v6, /device:TPU:16, one launch (start us, length us, event | category | flops | bytes accessed | tf_op | source)
XLA Modules:
  0.0 174.0 jit_solution(7180102510825036672)
XLA Ops:
  0.7 2.6 %collective-permute-start = (f32[32,5120]{1,0:T(8,128)S(1)}, f32[32,5120]{1,0:T(8,128)S(1)}, u32[]{:S(2)}, u32[]{:S(2)}) collective-permute-start(f32[32,5120]{1,0:T(8,128)S(1)} %fetch.3), channel_id=1, source_target_pairs={{0,8},{8,0},{16,24},{24,16},{1,9},{9,1},{17,25},{25,17},{2,10},{10... | collective-permute-start | bytes 1966088 | tf_op jit(solution)/shard_map/ppermute | solution.py:509
  4.5 2.5 %stage.1.grad_ref = bf16[512,5120]{1,0:T(8,128)(2,1)S(1)} custom-call(bf16[512,5120]{1,0:T(8,128)(2,1)} %bitcast.9, f32[32,5120]{1,0:T(8,128)S(1)} %fetch.2.refs_0_), custom_call_target="tpu_custom_call" | custom-call | bytes 5242880 | tf_op jit(solution)/shard_map/stage/pallas_call | solution.py:76
  7.0 11.9 %collective-permute-done.refs_0_ = f32[32,5120]{1,0:T(8,128)S(1)} collective-permute-done((f32[32,5120]{1,0:T(8,128)S(1)}, f32[32,5120]{1,0:T(8,128)S(1)}, u32[]{:S(2)}, u32[]{:S(2)}) %collective-permute-start) | collective-permute-done | bytes 655392 | tf_op jit(solution)/shard_map/ppermute | solution.py:509
  19.0 1.9 %collective-permute-start.1 = (f32[32,5120]{1,0:T(8,128)S(1)}, f32[32,5120]{1,0:T(8,128)S(1)}, u32[]{:S(2)}, u32[]{:S(2)}) collective-permute-start(f32[32,5120]{1,0:T(8,128)S(1)} %block.16), channel_id=1, source_target_pairs={{8,16},{16,8},{9,17},{17,9},{10,18},{18,10},{11,19},{19,11},{12,20... | collective-permute-start | bytes 1966088 | tf_op jit(solution)/shard_map/ppermute | solution.py:501
  21.9 11.1 %collective-permute-done.7.refs_0_ = f32[32,5120]{1,0:T(8,128)S(1)} collective-permute-done((f32[32,5120]{1,0:T(8,128)S(1)}, f32[32,5120]{1,0:T(8,128)S(1)}, u32[]{:S(2)}, u32[]{:S(2)}) %collective-permute-start.7) | collective-permute-done | bytes 655392 | tf_op jit(solution)/shard_map/ppermute | solution.py:509
  33.0 1.9 %collective-permute-start.8 = (f32[32,5120]{1,0:T(8,128)S(1)}, f32[32,5120]{1,0:T(8,128)S(1)}, u32[]{:S(2)}, u32[]{:S(2)}) collective-permute-start(f32[32,5120]{1,0:T(8,128)S(1)} %block.22), channel_id=1, source_target_pairs={{8,16},{16,8},{9,17},{17,9},{10,18},{18,10},{11,19},{19,11},{12,20... | collective-permute-start | bytes 1966088 | tf_op jit(solution)/shard_map/ppermute | solution.py:501
  36.1 10.9 %collective-permute-done.14.refs_0_ = f32[32,5120]{1,0:T(8,128)S(1)} collective-permute-done((f32[32,5120]{1,0:T(8,128)S(1)}, f32[32,5120]{1,0:T(8,128)S(1)}, u32[]{:S(2)}, u32[]{:S(2)}) %collective-permute-start.14) | collective-permute-done | bytes 655392 | tf_op jit(solution)/shard_map/ppermute | solution.py:509
  47.1 1.9 %collective-permute-start.15 = (f32[32,5120]{1,0:T(8,128)S(1)}, f32[32,5120]{1,0:T(8,128)S(1)}, u32[]{:S(2)}, u32[]{:S(2)}) collective-permute-start(f32[32,5120]{1,0:T(8,128)S(1)} %block.28), channel_id=1, source_target_pairs={{8,16},{16,8},{9,17},{17,9},{10,18},{18,10},{11,19},{19,11},{12,20... | collective-permute-start | bytes 1966088 | tf_op jit(solution)/shard_map/ppermute | solution.py:501
  50.1 10.9 %collective-permute-done.2.refs_0_ = f32[32,5120]{1,0:T(8,128)S(1)} collective-permute-done((f32[32,5120]{1,0:T(8,128)S(1)}, f32[32,5120]{1,0:T(8,128)S(1)}, u32[]{:S(2)}, u32[]{:S(2)}) %collective-permute-start.2) | collective-permute-done | bytes 655392 | tf_op jit(solution)/shard_map/ppermute | solution.py:509
  61.1 1.9 %collective-permute-start.3 = (f32[32,5120]{1,0:T(8,128)S(1)}, f32[32,5120]{1,0:T(8,128)S(1)}, u32[]{:S(2)}, u32[]{:S(2)}) collective-permute-start(f32[32,5120]{1,0:T(8,128)S(1)} %block.18), channel_id=1, source_target_pairs={{8,16},{16,8},{9,17},{17,9},{10,18},{18,10},{11,19},{19,11},{12,20... | collective-permute-start | bytes 1966088 | tf_op jit(solution)/shard_map/ppermute | solution.py:501
  64.2 10.9 %collective-permute-done.9.refs_0_ = f32[32,5120]{1,0:T(8,128)S(1)} collective-permute-done((f32[32,5120]{1,0:T(8,128)S(1)}, f32[32,5120]{1,0:T(8,128)S(1)}, u32[]{:S(2)}, u32[]{:S(2)}) %collective-permute-start.9) | collective-permute-done | bytes 655392 | tf_op jit(solution)/shard_map/ppermute | solution.py:509
  75.1 1.9 %collective-permute-start.10 = (f32[32,5120]{1,0:T(8,128)S(1)}, f32[32,5120]{1,0:T(8,128)S(1)}, u32[]{:S(2)}, u32[]{:S(2)}) collective-permute-start(f32[32,5120]{1,0:T(8,128)S(1)} %block.24), channel_id=1, source_target_pairs={{8,16},{16,8},{9,17},{17,9},{10,18},{18,10},{11,19},{19,11},{12,20... | collective-permute-start | bytes 1966088 | tf_op jit(solution)/shard_map/ppermute | solution.py:501
  78.2 10.9 %collective-permute-done.16.refs_0_ = f32[32,5120]{1,0:T(8,128)S(1)} collective-permute-done((f32[32,5120]{1,0:T(8,128)S(1)}, f32[32,5120]{1,0:T(8,128)S(1)}, u32[]{:S(2)}, u32[]{:S(2)}) %collective-permute-start.16) | collective-permute-done | bytes 655392 | tf_op jit(solution)/shard_map/ppermute | solution.py:509
  89.2 1.9 %collective-permute-start.17 = (f32[32,5120]{1,0:T(8,128)S(1)}, f32[32,5120]{1,0:T(8,128)S(1)}, u32[]{:S(2)}, u32[]{:S(2)}) collective-permute-start(f32[32,5120]{1,0:T(8,128)S(1)} %block.30), channel_id=1, source_target_pairs={{8,16},{16,8},{9,17},{17,9},{10,18},{18,10},{11,19},{19,11},{12,20... | collective-permute-start | bytes 1966088 | tf_op jit(solution)/shard_map/ppermute | solution.py:501
  92.3 10.9 %collective-permute-done.4.refs_0_ = f32[32,5120]{1,0:T(8,128)S(1)} collective-permute-done((f32[32,5120]{1,0:T(8,128)S(1)}, f32[32,5120]{1,0:T(8,128)S(1)}, u32[]{:S(2)}, u32[]{:S(2)}) %collective-permute-start.4) | collective-permute-done | bytes 655392 | tf_op jit(solution)/shard_map/ppermute | solution.py:509
  103.2 1.9 %collective-permute-start.5 = (f32[32,5120]{1,0:T(8,128)S(1)}, f32[32,5120]{1,0:T(8,128)S(1)}, u32[]{:S(2)}, u32[]{:S(2)}) collective-permute-start(f32[32,5120]{1,0:T(8,128)S(1)} %block.20), channel_id=1, source_target_pairs={{8,16},{16,8},{9,17},{17,9},{10,18},{18,10},{11,19},{19,11},{12,20... | collective-permute-start | bytes 1966088 | tf_op jit(solution)/shard_map/ppermute | solution.py:501
  106.3 10.9 %collective-permute-done.11.refs_0_ = f32[32,5120]{1,0:T(8,128)S(1)} collective-permute-done((f32[32,5120]{1,0:T(8,128)S(1)}, f32[32,5120]{1,0:T(8,128)S(1)}, u32[]{:S(2)}, u32[]{:S(2)}) %collective-permute-start.11) | collective-permute-done | bytes 655392 | tf_op jit(solution)/shard_map/ppermute | solution.py:509
  117.3 1.9 %collective-permute-start.12 = (f32[32,5120]{1,0:T(8,128)S(1)}, f32[32,5120]{1,0:T(8,128)S(1)}, u32[]{:S(2)}, u32[]{:S(2)}) collective-permute-start(f32[32,5120]{1,0:T(8,128)S(1)} %block.26), channel_id=1, source_target_pairs={{8,16},{16,8},{9,17},{17,9},{10,18},{18,10},{11,19},{19,11},{12,20... | collective-permute-start | bytes 1966088 | tf_op jit(solution)/shard_map/ppermute | solution.py:501
  122.7 8.6 %collective-permute-done.18.refs_0_ = f32[32,5120]{1,0:T(8,128)S(1)} collective-permute-done((f32[32,5120]{1,0:T(8,128)S(1)}, f32[32,5120]{1,0:T(8,128)S(1)}, u32[]{:S(2)}, u32[]{:S(2)}) %collective-permute-start.18) | collective-permute-done | bytes 655392 | tf_op jit(solution)/shard_map/ppermute | solution.py:509
  133.4 1.6 collective-permute-start.25
  134.9 2.3 %collective-permute-done.25.received_ref = f32[1,5120]{1,0:T(1,128)S(1)} collective-permute-done((f32[1,5120]{1,0:T(1,128)S(1)}, f32[1,5120]{1,0:T(1,128)S(1)}, u32[]{:S(2)}, u32[]{:S(2)}) %collective-permute-start.25) | collective-permute-done | bytes 20512 | tf_op jit(solution)/shard_map/ppermute | solution.py:514
  139.9 5.9 %collective-permute-done.26.refs_3_.sums_ref.refs_1_ = f32[1,5504]{1,0:T(1,128)S(1)} collective-permute-done((f32[1,5504]{1,0:T(1,128)S(1)}, f32[1,5504]{1,0:T(1,128)S(1)}, u32[]{:S(2)}, u32[]{:S(2)}) %collective-permute-start.26) | collective-permute-done | bytes 22048 | tf_op jit(solution)/shard_map/ppermute | solution.py:515
  145.8 1.6 collective-permute-start.33
  149.1 1.6 collective-permute-start.27
  150.7 2.5 %collective-permute-done.27 = f32[1,10368]{1,0:T(1,128)S(1)} collective-permute-done((f32[1,10368]{1,0:T(1,128)S(1)}, f32[1,10368]{1,0:T(1,128)S(1)}, u32[]{:S(2)}, u32[]{:S(2)}) %collective-permute-start.27) | collective-permute-done | bytes 41504 | tf_op jit(solution)/shard_map/ppermute | solution.py:30
  153.2 1.6 collective-permute-start.28
  154.8 2.5 %collective-permute-done.28 = f32[1,10368]{1,0:T(1,128)S(1)} collective-permute-done((f32[1,10368]{1,0:T(1,128)S(1)}, f32[1,10368]{1,0:T(1,128)S(1)}, u32[]{:S(2)}, u32[]{:S(2)}) %collective-permute-start.28) | collective-permute-done | bytes 41504 | tf_op jit(solution)/shard_map/ppermute | solution.py:30
  157.4 1.9 %collective-permute-start.29 = (f32[1,10368]{1,0:T(1,128)S(1)}, f32[1,10368]{1,0:T(1,128)S(1)}, u32[]{:S(2)}, u32[]{:S(2)}) collective-permute-start(f32[1,10368]{1,0:T(1,128)S(1)} %add.10), channel_id=1, source_target_pairs={{8,16},{16,8},{9,17},{17,9},{10,18},{18,10},{11,19},{19,11},{12,20... | collective-permute-start | bytes 124424 | tf_op jit(solution)/shard_map/ppermute | solution.py:522
  159.3 4.0 %collective-permute-done.29 = f32[1,10368]{1,0:T(1,128)S(1)} collective-permute-done((f32[1,10368]{1,0:T(1,128)S(1)}, f32[1,10368]{1,0:T(1,128)S(1)}, u32[]{:S(2)}, u32[]{:S(2)}) %collective-permute-start.29) | collective-permute-done | bytes 41504 | tf_op jit(solution)/shard_map/ppermute | solution.py:522
  164.6 1.7 collective-permute-done.30.refs_0_
  168.0 1.7 %apply.1 = (f32[128,5120]{1,0:T(8,128)}, f32[1,5120]{1,0:T(1,128)S(1)}, f32[32,128]{1,0:T(8,128)S(1)}) custom-call(f32[128,5120]{1,0:T(8,128)S(1)} %bitcast.5, f32[1,5120]{1,0:T(1,128)S(1)} %get-tuple-element.77.col_ref, f32[1,128]{1,0:T(1,128)S(1)} %get-tuple-element.78.mean_ref, f32[32,5120]{1,0:T(8,128)S(1)} %get-tuple-element.59.grad_ref.refs_0_, ...), custom_call_target="tpu_custom_call" | custom-call | flops 1966080 | bytes 5898240 | tf_op jit(solution)/shard_map/apply/pallas_call | solution.py:379
  169.8 3.3 %collective-permute-done.33.refs_1_ = f32[32,5120]{1,0:T(8,128)S(1)} collective-permute-done((f32[32,5120]{1,0:T(8,128)S(1)}, f32[32,5120]{1,0:T(8,128)S(1)}, u32[]{:S(2)}, u32[]{:S(2)}) %collective-permute-start.33) | collective-permute-done | bytes 655392 | tf_op jit(solution)/shard_map/ppermute | solution.py:519
  (88 shorter events, 23.5 us)
Async XLA Ops:
  0.7 18.2 %collective-permute-start = (f32[32,5120]{1,0:T(8,128)S(1)}, f32[32,5120]{1,0:T(8,128)S(1)}, u32[]{:S(2)}, u32[]{:S(2)}) collective-permute-start(f32[32,5120]{1,0:T(8,128)S(1)} %fetch.3), channel_id=1, source_target_pairs={{0,8},{8,0},{16,24},{24,16},{1,9},{9,1},{17,25},{25,17},{2,10},{10... | collective-permute-start | bytes 1966088 | tf_op jit(solution)/shard_map/ppermute | solution.py:509
  3.4 29.5 %collective-permute-start.7 = (f32[32,5120]{1,0:T(8,128)S(1)}, f32[32,5120]{1,0:T(8,128)S(1)}, u32[]{:S(2)}, u32[]{:S(2)}) collective-permute-start(f32[32,5120]{1,0:T(8,128)S(1)} %fetch.2.refs_0_), channel_id=1, source_target_pairs={{0,8},{8,0},{16,24},{24,16},{1,9},{9,1},{17,25},{25,17},{2,10},{10... | collective-permute-start | bytes 1966088 | tf_op jit(solution)/shard_map/ppermute | solution.py:509
  19.0 17.0 %collective-permute-start.1 = (f32[32,5120]{1,0:T(8,128)S(1)}, f32[32,5120]{1,0:T(8,128)S(1)}, u32[]{:S(2)}, u32[]{:S(2)}) collective-permute-start(f32[32,5120]{1,0:T(8,128)S(1)} %block.16), channel_id=1, source_target_pairs={{8,16},{16,8},{9,17},{17,9},{10,18},{18,10},{11,19},{19,11},{12,20... | collective-permute-start | bytes 1966088 | tf_op jit(solution)/shard_map/ppermute | solution.py:501
  21.0 26.0 %collective-permute-start.14 = (f32[32,5120]{1,0:T(8,128)S(1)}, f32[32,5120]{1,0:T(8,128)S(1)}, u32[]{:S(2)}, u32[]{:S(2)}) collective-permute-start(f32[32,5120]{1,0:T(8,128)S(1)} %block.27), channel_id=1, source_target_pairs={{0,8},{8,0},{16,24},{24,16},{1,9},{9,1},{17,25},{25,17},{2,10},{10... | collective-permute-start | bytes 1966088 | tf_op jit(solution)/shard_map/ppermute | solution.py:509
  33.0 17.0 %collective-permute-start.8 = (f32[32,5120]{1,0:T(8,128)S(1)}, f32[32,5120]{1,0:T(8,128)S(1)}, u32[]{:S(2)}, u32[]{:S(2)}) collective-permute-start(f32[32,5120]{1,0:T(8,128)S(1)} %block.22), channel_id=1, source_target_pairs={{8,16},{16,8},{9,17},{17,9},{10,18},{18,10},{11,19},{19,11},{12,20... | collective-permute-start | bytes 1966088 | tf_op jit(solution)/shard_map/ppermute | solution.py:501
  36.0 25.0 %collective-permute-start.2 = (f32[32,5120]{1,0:T(8,128)S(1)}, f32[32,5120]{1,0:T(8,128)S(1)}, u32[]{:S(2)}, u32[]{:S(2)}) collective-permute-start(f32[32,5120]{1,0:T(8,128)S(1)} %block.17), channel_id=1, source_target_pairs={{0,8},{8,0},{16,24},{24,16},{1,9},{9,1},{17,25},{25,17},{2,10},{10... | collective-permute-start | bytes 1966088 | tf_op jit(solution)/shard_map/ppermute | solution.py:509
  47.1 17.0 %collective-permute-start.15 = (f32[32,5120]{1,0:T(8,128)S(1)}, f32[32,5120]{1,0:T(8,128)S(1)}, u32[]{:S(2)}, u32[]{:S(2)}) collective-permute-start(f32[32,5120]{1,0:T(8,128)S(1)} %block.28), channel_id=1, source_target_pairs={{8,16},{16,8},{9,17},{17,9},{10,18},{18,10},{11,19},{19,11},{12,20... | collective-permute-start | bytes 1966088 | tf_op jit(solution)/shard_map/ppermute | solution.py:501
  50.1 25.0 %collective-permute-start.9 = (f32[32,5120]{1,0:T(8,128)S(1)}, f32[32,5120]{1,0:T(8,128)S(1)}, u32[]{:S(2)}, u32[]{:S(2)}) collective-permute-start(f32[32,5120]{1,0:T(8,128)S(1)} %block.23), channel_id=1, source_target_pairs={{0,8},{8,0},{16,24},{24,16},{1,9},{9,1},{17,25},{25,17},{2,10},{10... | collective-permute-start | bytes 1966088 | tf_op jit(solution)/shard_map/ppermute | solution.py:509
  61.1 17.0 %collective-permute-start.3 = (f32[32,5120]{1,0:T(8,128)S(1)}, f32[32,5120]{1,0:T(8,128)S(1)}, u32[]{:S(2)}, u32[]{:S(2)}) collective-permute-start(f32[32,5120]{1,0:T(8,128)S(1)} %block.18), channel_id=1, source_target_pairs={{8,16},{16,8},{9,17},{17,9},{10,18},{18,10},{11,19},{19,11},{12,20... | collective-permute-start | bytes 1966088 | tf_op jit(solution)/shard_map/ppermute | solution.py:501
  64.1 25.0 %collective-permute-start.16 = (f32[32,5120]{1,0:T(8,128)S(1)}, f32[32,5120]{1,0:T(8,128)S(1)}, u32[]{:S(2)}, u32[]{:S(2)}) collective-permute-start(f32[32,5120]{1,0:T(8,128)S(1)} %block.29), channel_id=1, source_target_pairs={{0,8},{8,0},{16,24},{24,16},{1,9},{9,1},{17,25},{25,17},{2,10},{10... | collective-permute-start | bytes 1966088 | tf_op jit(solution)/shard_map/ppermute | solution.py:509
  75.1 17.0 %collective-permute-start.10 = (f32[32,5120]{1,0:T(8,128)S(1)}, f32[32,5120]{1,0:T(8,128)S(1)}, u32[]{:S(2)}, u32[]{:S(2)}) collective-permute-start(f32[32,5120]{1,0:T(8,128)S(1)} %block.24), channel_id=1, source_target_pairs={{8,16},{16,8},{9,17},{17,9},{10,18},{18,10},{11,19},{19,11},{12,20... | collective-permute-start | bytes 1966088 | tf_op jit(solution)/shard_map/ppermute | solution.py:501
  78.1 25.0 %collective-permute-start.4 = (f32[32,5120]{1,0:T(8,128)S(1)}, f32[32,5120]{1,0:T(8,128)S(1)}, u32[]{:S(2)}, u32[]{:S(2)}) collective-permute-start(f32[32,5120]{1,0:T(8,128)S(1)} %block.19), channel_id=1, source_target_pairs={{0,8},{8,0},{16,24},{24,16},{1,9},{9,1},{17,25},{25,17},{2,10},{10... | collective-permute-start | bytes 1966088 | tf_op jit(solution)/shard_map/ppermute | solution.py:509
  89.2 17.0 %collective-permute-start.17 = (f32[32,5120]{1,0:T(8,128)S(1)}, f32[32,5120]{1,0:T(8,128)S(1)}, u32[]{:S(2)}, u32[]{:S(2)}) collective-permute-start(f32[32,5120]{1,0:T(8,128)S(1)} %block.30), channel_id=1, source_target_pairs={{8,16},{16,8},{9,17},{17,9},{10,18},{18,10},{11,19},{19,11},{12,20... | collective-permute-start | bytes 1966088 | tf_op jit(solution)/shard_map/ppermute | solution.py:501
  92.2 25.0 %collective-permute-start.11 = (f32[32,5120]{1,0:T(8,128)S(1)}, f32[32,5120]{1,0:T(8,128)S(1)}, u32[]{:S(2)}, u32[]{:S(2)}) collective-permute-start(f32[32,5120]{1,0:T(8,128)S(1)} %block.25), channel_id=1, source_target_pairs={{0,8},{8,0},{16,24},{24,16},{1,9},{9,1},{17,25},{25,17},{2,10},{10... | collective-permute-start | bytes 1966088 | tf_op jit(solution)/shard_map/ppermute | solution.py:509
  103.2 17.0 %collective-permute-start.5 = (f32[32,5120]{1,0:T(8,128)S(1)}, f32[32,5120]{1,0:T(8,128)S(1)}, u32[]{:S(2)}, u32[]{:S(2)}) collective-permute-start(f32[32,5120]{1,0:T(8,128)S(1)} %block.20), channel_id=1, source_target_pairs={{8,16},{16,8},{9,17},{17,9},{10,18},{18,10},{11,19},{19,11},{12,20... | collective-permute-start | bytes 1966088 | tf_op jit(solution)/shard_map/ppermute | solution.py:501
  106.2 25.0 %collective-permute-start.18 = (f32[32,5120]{1,0:T(8,128)S(1)}, f32[32,5120]{1,0:T(8,128)S(1)}, u32[]{:S(2)}, u32[]{:S(2)}) collective-permute-start(f32[32,5120]{1,0:T(8,128)S(1)} %block.31), channel_id=1, source_target_pairs={{0,8},{8,0},{16,24},{24,16},{1,9},{9,1},{17,25},{25,17},{2,10},{10... | collective-permute-start | bytes 1966088 | tf_op jit(solution)/shard_map/ppermute | solution.py:509
  117.3 30.1 %collective-permute-start.12 = (f32[32,5120]{1,0:T(8,128)S(1)}, f32[32,5120]{1,0:T(8,128)S(1)}, u32[]{:S(2)}, u32[]{:S(2)}) collective-permute-start(f32[32,5120]{1,0:T(8,128)S(1)} %block.26), channel_id=1, source_target_pairs={{8,16},{16,8},{9,17},{17,9},{10,18},{18,10},{11,19},{19,11},{12,20... | collective-permute-start | bytes 1966088 | tf_op jit(solution)/shard_map/ppermute | solution.py:501
  120.3 27.1 %collective-permute-start.6 = (f32[32,5120]{1,0:T(8,128)S(1)}, f32[32,5120]{1,0:T(8,128)S(1)}, u32[]{:S(2)}, u32[]{:S(2)}) collective-permute-start(f32[32,5120]{1,0:T(8,128)S(1)} %block.21), channel_id=1, source_target_pairs={{0,8},{8,0},{16,24},{24,16},{1,9},{9,1},{17,25},{25,17},{2,10},{10... | collective-permute-start | bytes 1966088 | tf_op jit(solution)/shard_map/ppermute | solution.py:509
  120.5 1.2 collective-permute-start.23
  120.8 1.4 collective-permute-start.24
  121.8 9.7 %collective-permute-start.22 = (f32[32,128]{1,0:T(8,128)S(1)}, f32[32,128]{1,0:T(8,128)S(1)}, u32[]{:S(2)}, u32[]{:S(2)}) collective-permute-start(f32[32,128]{1,0:T(8,128)S(1)} %get-tuple-element.61.refs_0_), channel_id=1, source_target_pairs={{0,1},{1,0},{2,3},{3,2},{4,5},{5,4},{6,7},{7,6},{8,9},{9,8},{10,11... | collective-permute-start | bytes 49160 | tf_op jit(solution)/shard_map/ppermute | solution.py:37
  122.2 10.5 %collective-permute-start.21 = (f32[32,128]{1,0:T(8,128)S(1)}, f32[32,128]{1,0:T(8,128)S(1)}, u32[]{:S(2)}, u32[]{:S(2)}) collective-permute-start(f32[32,128]{1,0:T(8,128)S(1)} %get-tuple-element.58.refs_0_), channel_id=1, source_target_pairs={{0,1},{1,0},{2,3},{3,2},{4,5},{5,4},{6,7},{7,6},{8,9},{9,8},{10,11... | collective-permute-start | bytes 49160 | tf_op jit(solution)/shard_map/ppermute | solution.py:37
  131.3 1.7 collective-permute-start.20
  131.5 1.6 collective-permute-start.19
  133.4 3.8 %collective-permute-start.25 = (f32[1,5120]{1,0:T(1,128)S(1)}, f32[1,5120]{1,0:T(1,128)S(1)}, u32[]{:S(2)}, u32[]{:S(2)}) collective-permute-start(f32[1,5120]{1,0:T(1,128)S(1)} %half.1), channel_id=1, source_target_pairs={{0,2},{2,0},{4,6},{6,4},{1,3},{3,1},{5,7},{7,5},{8,10},{10,8},{12,... | collective-permute-start | bytes 61448 | tf_op jit(solution)/shard_map/ppermute | solution.py:514
  137.3 8.5 %collective-permute-start.26 = (f32[1,5504]{1,0:T(1,128)S(1)}, f32[1,5504]{1,0:T(1,128)S(1)}, u32[]{:S(2)}, u32[]{:S(2)}) collective-permute-start(f32[1,5504]{1,0:T(1,128)S(1)} %joined.1), channel_id=1, source_target_pairs={{0,8},{24,16},{1,9},{25,17},{2,10},{26,18},{3,11},{27,19},{4,12},{... | collective-permute-start | bytes 66056 | tf_op jit(solution)/shard_map/ppermute | solution.py:515
  138.6 28.9 %collective-permute-start.31 = (f32[32,5120]{1,0:T(8,128)S(1)}, f32[32,5120]{1,0:T(8,128)S(1)}, u32[]{:S(2)}, u32[]{:S(2)}) collective-permute-start(f32[32,5120]{1,0:T(8,128)S(1)} %pass.2.refs_0_), channel_id=1, source_target_pairs={{0,8},{24,16},{1,9},{25,17},{2,10},{26,18},{3,11},{27,19},{4,12},{... | collective-permute-start | bytes 1966088 | tf_op jit(solution)/shard_map/ppermute | solution.py:518
  145.8 27.2 %collective-permute-start.33 = (f32[32,5120]{1,0:T(8,128)S(1)}, f32[32,5120]{1,0:T(8,128)S(1)}, u32[]{:S(2)}, u32[]{:S(2)}) collective-permute-start(f32[32,5120]{1,0:T(8,128)S(1)} %pass.3), channel_id=1, source_target_pairs={{0,8},{24,16},{1,9},{25,17},{2,10},{26,18},{3,11},{27,19},{4,12},{... | collective-permute-start | bytes 1966088 | tf_op jit(solution)/shard_map/ppermute | solution.py:519
  149.1 4.1 %collective-permute-start.27 = (f32[1,10368]{1,0:T(1,128)S(1)}, f32[1,10368]{1,0:T(1,128)S(1)}, u32[]{:S(2)}, u32[]{:S(2)}) collective-permute-start(f32[1,10368]{1,0:T(1,128)S(1)} %get-tuple-element.76), channel_id=1, source_target_pairs={{0,2},{2,0},{4,6},{6,4},{1,3},{3,1},{5,7},{7,5},{8,10},{10,8},{12,... | collective-permute-start | bytes 124424 | tf_op jit(solution)/shard_map/ppermute | solution.py:30
  153.2 4.1 %collective-permute-start.28 = (f32[1,10368]{1,0:T(1,128)S(1)}, f32[1,10368]{1,0:T(1,128)S(1)}, u32[]{:S(2)}, u32[]{:S(2)}) collective-permute-start(f32[1,10368]{1,0:T(1,128)S(1)} %add.9), channel_id=1, source_target_pairs={{0,4},{2,6},{4,0},{6,2},{1,5},{3,7},{5,1},{7,3},{8,12},{10,14},{12... | collective-permute-start | bytes 124424 | tf_op jit(solution)/shard_map/ppermute | solution.py:30
  157.4 5.9 %collective-permute-start.29 = (f32[1,10368]{1,0:T(1,128)S(1)}, f32[1,10368]{1,0:T(1,128)S(1)}, u32[]{:S(2)}, u32[]{:S(2)}) collective-permute-start(f32[1,10368]{1,0:T(1,128)S(1)} %add.10), channel_id=1, source_target_pairs={{8,16},{16,8},{9,17},{17,9},{10,18},{18,10},{11,19},{19,11},{12,20... | collective-permute-start | bytes 124424 | tf_op jit(solution)/shard_map/ppermute | solution.py:522
  163.3 3.0 %collective-permute-start.30 = (f32[1,10368]{1,0:T(1,128)S(1)}, f32[1,10368]{1,0:T(1,128)S(1)}, u32[]{:S(2)}, u32[]{:S(2)}) collective-permute-start(f32[1,10368]{1,0:T(1,128)S(1)} %add.11.sums_ref), channel_id=1, source_target_pairs={{8,0},{16,24},{9,1},{17,25},{10,2},{18,26},{11,3},{19,27},{12,4},{... | collective-permute-start | bytes 124424 | tf_op jit(solution)/shard_map/ppermute | solution.py:523
  (5 other events, 45.8 us)

commit v7 on v6

--- a/solution.py
+++ b/solution.py
@@ -505,8 +505,9 @@
             operand = fetch_block(grad, table, [1, 0, 0, 1], rows)
             staged = stage_gradient(grad, [operand])
         else:
-            operand = block_sum(staged, table, arrived, [P[0]] if slot == 2 else [], rows)
-        P[slot] = lax.ppermute(operand, "dp", swap)
+            tokens = [P[0]] if slot == 2 else sums[-2:-1]
+            operand = block_sum(staged, table, arrived, tokens, rows)
+        P[slot] = lax.ppermute(operand, "dp", outward if slot in (1, 2) else swap)
         if 3 <= slot <= 8:
             settle(slot)
     cols = grad.shape[1]

time: 174 us -> 174 us (level)
    ppermute x8, waiting for transfers between devices: 2.02 us -> 7.52 us  [other_parts(): lax.ppermute(values, axis, [(i, (i + k) % size) for i in range(size)])]
    ppermute x8, waiting for transfers between devices: 7.08 us -> 2.59 us  [short_line(): M[slot] = lax.ppermute(operand, 'dp', middle)]
  transfers between devices with their start and end apart: 34 -> 34, of which waited for: 27 -> 26; matrix products, arithmetic and copies ran while one was open for 0% -> 0% of each run, Pallas kernels for 5% -> 5%
where the time goes in v7:
time: 174 us
  waiting for transfers between devices  129 us (74%)
  starting transfers between devices  33.6 us (19%)
  Pallas kernels  10.4 us (6%)
    ppermute x10, waiting for transfers between devices, short_line(): P[slot] = lax.ppermute(operand, 'dp', outward if slot in (1, 2) else swap)  96 us
    ppermute x8, starting transfers between devices, short_line(): M[slot] = lax.ppermute(operand, 'dp', middle)  15.4 us
    ppermute x8, waiting for transfers between devices, other_parts(): lax.ppermute(values, axis, [(i, (i + k) % size) for i in range(size)])  7.52 us
    ppermute x1, waiting for transfers between devices, short_line(): early = lax.ppermute(joined_half(sums[-1], received, cols), 'dp', outward)  6.29 us
    ppermute x10, starting transfers between devices, short_line(): P[slot] = lax.ppermute(operand, 'dp', outward if slot in (1, 2) else swap)  5.69 us
    ppermute x2, waiting for transfers between devices, axis_sum(): values = values + lax.ppermute(values, axis, pairs)  5 us
    ppermute x1, waiting for transfers between devices, short_line(): total = total + lax.ppermute(total, 'dp', middle)  3.97 us
  transfers between devices with their start and end apart: 34, of which 26 were waited for; matrix products, arithmetic and copies ran while one was open for 0% of the time, Pallas kernels for 5%

profile of v7, /device:TPU:16, one launch (start us, length us, event | category | flops | bytes accessed | tf_op | source)
XLA Modules:
  0.0 174.0 jit_solution(13591144831281527810)
XLA Ops:
  0.7 2.6 %collective-permute-start = (f32[32,5120]{1,0:T(8,128)S(1)}, f32[32,5120]{1,0:T(8,128)S(1)}, u32[]{:S(2)}, u32[]{:S(2)}) collective-permute-start(f32[32,5120]{1,0:T(8,128)S(1)} %fetch.3), channel_id=1, source_target_pairs={{0,8},{8,0},{16,24},{24,16},{1,9},{9,1},{17,25},{25,17},{2,10},{10... | collective-permute-start | bytes 1966088 | tf_op jit(solution)/shard_map/ppermute | solution.py:510
  4.7 2.5 %stage.1.grad_ref = bf16[512,5120]{1,0:T(8,128)(2,1)S(1)} custom-call(bf16[512,5120]{1,0:T(8,128)(2,1)} %bitcast.9, f32[32,5120]{1,0:T(8,128)S(1)} %fetch.2.refs_0_), custom_call_target="tpu_custom_call" | custom-call | bytes 5242880 | tf_op jit(solution)/shard_map/stage/pallas_call | solution.py:76
  7.2 11.7 %collective-permute-done.refs_0_ = f32[32,5120]{1,0:T(8,128)S(1)} collective-permute-done((f32[32,5120]{1,0:T(8,128)S(1)}, f32[32,5120]{1,0:T(8,128)S(1)}, u32[]{:S(2)}, u32[]{:S(2)}) %collective-permute-start) | collective-permute-done | bytes 655392 | tf_op jit(solution)/shard_map/ppermute | solution.py:510
  19.0 1.9 %collective-permute-start.1 = (f32[32,5120]{1,0:T(8,128)S(1)}, f32[32,5120]{1,0:T(8,128)S(1)}, u32[]{:S(2)}, u32[]{:S(2)}) collective-permute-start(f32[32,5120]{1,0:T(8,128)S(1)} %block.16), channel_id=1, source_target_pairs={{8,16},{16,8},{9,17},{17,9},{10,18},{18,10},{11,19},{19,11},{12,20... | collective-permute-start | bytes 1966088 | tf_op jit(solution)/shard_map/ppermute | solution.py:501
  22.3 10.7 %collective-permute-done.4.refs_0_ = f32[32,5120]{1,0:T(8,128)S(1)} collective-permute-done((f32[32,5120]{1,0:T(8,128)S(1)}, f32[32,5120]{1,0:T(8,128)S(1)}, u32[]{:S(2)}, u32[]{:S(2)}) %collective-permute-start.4) | collective-permute-done | bytes 655392 | tf_op jit(solution)/shard_map/ppermute | solution.py:510
  33.0 1.9 %collective-permute-start.5 = (f32[32,5120]{1,0:T(8,128)S(1)}, f32[32,5120]{1,0:T(8,128)S(1)}, u32[]{:S(2)}, u32[]{:S(2)}) collective-permute-start(f32[32,5120]{1,0:T(8,128)S(1)} %block.19), channel_id=1, source_target_pairs={{8,16},{16,8},{9,17},{17,9},{10,18},{18,10},{11,19},{19,11},{12,20... | collective-permute-start | bytes 1966088 | tf_op jit(solution)/shard_map/ppermute | solution.py:501
  36.1 10.9 %collective-permute-done.12.refs_0_ = f32[32,5120]{1,0:T(8,128)S(1)} collective-permute-done((f32[32,5120]{1,0:T(8,128)S(1)}, f32[32,5120]{1,0:T(8,128)S(1)}, u32[]{:S(2)}, u32[]{:S(2)}) %collective-permute-start.12) | collective-permute-done | bytes 655392 | tf_op jit(solution)/shard_map/ppermute | solution.py:510
  47.1 1.9 %collective-permute-start.13 = (f32[32,5120]{1,0:T(8,128)S(1)}, f32[32,5120]{1,0:T(8,128)S(1)}, u32[]{:S(2)}, u32[]{:S(2)}) collective-permute-start(f32[32,5120]{1,0:T(8,128)S(1)} %block.25), channel_id=1, source_target_pairs={{8,16},{16,8},{9,17},{17,9},{10,18},{18,10},{11,19},{19,11},{12,20... | collective-permute-start | bytes 1966088 | tf_op jit(solution)/shard_map/ppermute | solution.py:501
  50.1 10.9 %collective-permute-done.2.refs_0_ = f32[32,5120]{1,0:T(8,128)S(1)} collective-permute-done((f32[32,5120]{1,0:T(8,128)S(1)}, f32[32,5120]{1,0:T(8,128)S(1)}, u32[]{:S(2)}, u32[]{:S(2)}) %collective-permute-start.2) | collective-permute-done | bytes 655392 | tf_op jit(solution)/shard_map/ppermute | solution.py:510
  61.1 1.9 %collective-permute-start.3 = (f32[32,5120]{1,0:T(8,128)S(1)}, f32[32,5120]{1,0:T(8,128)S(1)}, u32[]{:S(2)}, u32[]{:S(2)}) collective-permute-start(f32[32,5120]{1,0:T(8,128)S(1)} %block.18), channel_id=1, source_target_pairs={{8,16},{16,8},{9,17},{17,9},{10,18},{18,10},{11,19},{19,11},{12,20... | collective-permute-start | bytes 1966088 | tf_op jit(solution)/shard_map/ppermute | solution.py:501
  65.0 10.1 %collective-permute-done.6.refs_0_ = f32[32,5120]{1,0:T(8,128)S(1)} collective-permute-done((f32[32,5120]{1,0:T(8,128)S(1)}, f32[32,5120]{1,0:T(8,128)S(1)}, u32[]{:S(2)}, u32[]{:S(2)}) %collective-permute-start.6) | collective-permute-done | bytes 655392 | tf_op jit(solution)/shard_map/ppermute | solution.py:510
  75.1 1.9 %collective-permute-start.11 = (f32[32,5120]{1,0:T(8,128)S(1)}, f32[32,5120]{1,0:T(8,128)S(1)}, u32[]{:S(2)}, u32[]{:S(2)}) collective-permute-start(f32[32,5120]{1,0:T(8,128)S(1)} %block.23), channel_id=1, source_target_pairs={{8,16},{16,8},{9,17},{17,9},{10,18},{18,10},{11,19},{19,11},{12,20... | collective-permute-start | bytes 1966088 | tf_op jit(solution)/shard_map/ppermute | solution.py:501
  78.9 10.3 %collective-permute-done.14.refs_0_ = f32[32,5120]{1,0:T(8,128)S(1)} collective-permute-done((f32[32,5120]{1,0:T(8,128)S(1)}, f32[32,5120]{1,0:T(8,128)S(1)}, u32[]{:S(2)}, u32[]{:S(2)}) %collective-permute-start.14) | collective-permute-done | bytes 655392 | tf_op jit(solution)/shard_map/ppermute | solution.py:510
  89.2 1.9 %collective-permute-start.22 = (f32[32,5120]{1,0:T(8,128)S(1)}, f32[32,5120]{1,0:T(8,128)S(1)}, u32[]{:S(2)}, u32[]{:S(2)}) collective-permute-start(f32[32,5120]{1,0:T(8,128)S(1)} %block.30), channel_id=1, source_target_pairs={{8,16},{16,8},{9,17},{17,9},{10,18},{18,10},{11,19},{19,11},{12,20... | collective-permute-start | bytes 1966088 | tf_op jit(solution)/shard_map/ppermute | solution.py:501
  92.9 10.3 %collective-permute-done.9.refs_0_ = f32[32,5120]{1,0:T(8,128)S(1)} collective-permute-done((f32[32,5120]{1,0:T(8,128)S(1)}, f32[32,5120]{1,0:T(8,128)S(1)}, u32[]{:S(2)}, u32[]{:S(2)}) %collective-permute-start.9) | collective-permute-done | bytes 655392 | tf_op jit(solution)/shard_map/ppermute | solution.py:510
  103.2 1.9 %collective-permute-start.10 = (f32[32,5120]{1,0:T(8,128)S(1)}, f32[32,5120]{1,0:T(8,128)S(1)}, u32[]{:S(2)}, u32[]{:S(2)}) collective-permute-start(f32[32,5120]{1,0:T(8,128)S(1)} %block.22), channel_id=1, source_target_pairs={{8,16},{16,8},{9,17},{17,9},{10,18},{18,10},{11,19},{19,11},{12,20... | collective-permute-start | bytes 1966088 | tf_op jit(solution)/shard_map/ppermute | solution.py:501
  106.9 10.3 %collective-permute-done.16.refs_0_ = f32[32,5120]{1,0:T(8,128)S(1)} collective-permute-done((f32[32,5120]{1,0:T(8,128)S(1)}, f32[32,5120]{1,0:T(8,128)S(1)}, u32[]{:S(2)}, u32[]{:S(2)}) %collective-permute-start.16) | collective-permute-done | bytes 655392 | tf_op jit(solution)/shard_map/ppermute | solution.py:510
  117.6 1.9 %collective-permute-start.20 = (f32[32,5120]{1,0:T(8,128)S(1)}, f32[32,5120]{1,0:T(8,128)S(1)}, u32[]{:S(2)}, u32[]{:S(2)}) collective-permute-start(f32[32,5120]{1,0:T(8,128)S(1)} %block.29), channel_id=1, source_target_pairs={{8,16},{16,8},{9,17},{17,9},{10,18},{18,10},{11,19},{19,11},{12,20... | collective-permute-start | bytes 1966088 | tf_op jit(solution)/shard_map/ppermute | solution.py:501
  120.4 10.9 %collective-permute-done.23.refs_0_ = f32[32,5120]{1,0:T(8,128)S(1)} collective-permute-done((f32[32,5120]{1,0:T(8,128)S(1)}, f32[32,5120]{1,0:T(8,128)S(1)}, u32[]{:S(2)}, u32[]{:S(2)}) %collective-permute-start.23) | collective-permute-done | bytes 655392 | tf_op jit(solution)/shard_map/ppermute | solution.py:510
  132.9 1.6 collective-permute-start.25
  134.5 2.3 %collective-permute-done.25.received_ref = f32[1,5120]{1,0:T(1,128)S(1)} collective-permute-done((f32[1,5120]{1,0:T(1,128)S(1)}, f32[1,5120]{1,0:T(1,128)S(1)}, u32[]{:S(2)}, u32[]{:S(2)}) %collective-permute-start.25) | collective-permute-done | bytes 20512 | tf_op jit(solution)/shard_map/ppermute | solution.py:515
  139.5 6.3 %collective-permute-done.26.refs_3_.sums_ref.refs_1_ = f32[1,5504]{1,0:T(1,128)S(1)} collective-permute-done((f32[1,5504]{1,0:T(1,128)S(1)}, f32[1,5504]{1,0:T(1,128)S(1)}, u32[]{:S(2)}, u32[]{:S(2)}) %collective-permute-start.26) | collective-permute-done | bytes 22048 | tf_op jit(solution)/shard_map/ppermute | solution.py:516
  145.8 1.6 collective-permute-start.33
  149.1 1.6 collective-permute-start.27
  150.7 2.5 %collective-permute-done.27 = f32[1,10368]{1,0:T(1,128)S(1)} collective-permute-done((f32[1,10368]{1,0:T(1,128)S(1)}, f32[1,10368]{1,0:T(1,128)S(1)}, u32[]{:S(2)}, u32[]{:S(2)}) %collective-permute-start.27) | collective-permute-done | bytes 41504 | tf_op jit(solution)/shard_map/ppermute | solution.py:30
  153.2 1.6 collective-permute-start.28
  154.8 2.5 %collective-permute-done.28 = f32[1,10368]{1,0:T(1,128)S(1)} collective-permute-done((f32[1,10368]{1,0:T(1,128)S(1)}, f32[1,10368]{1,0:T(1,128)S(1)}, u32[]{:S(2)}, u32[]{:S(2)}) %collective-permute-start.28) | collective-permute-done | bytes 41504 | tf_op jit(solution)/shard_map/ppermute | solution.py:30
  157.4 1.9 %collective-permute-start.29 = (f32[1,10368]{1,0:T(1,128)S(1)}, f32[1,10368]{1,0:T(1,128)S(1)}, u32[]{:S(2)}, u32[]{:S(2)}) collective-permute-start(f32[1,10368]{1,0:T(1,128)S(1)} %add.10), channel_id=1, source_target_pairs={{8,16},{16,8},{9,17},{17,9},{10,18},{18,10},{11,19},{19,11},{12,20... | collective-permute-start | bytes 124424 | tf_op jit(solution)/shard_map/ppermute | solution.py:523
  159.3 4.0 %collective-permute-done.29 = f32[1,10368]{1,0:T(1,128)S(1)} collective-permute-done((f32[1,10368]{1,0:T(1,128)S(1)}, f32[1,10368]{1,0:T(1,128)S(1)}, u32[]{:S(2)}, u32[]{:S(2)}) %collective-permute-start.29) | collective-permute-done | bytes 41504 | tf_op jit(solution)/shard_map/ppermute | solution.py:523
  164.6 1.7 collective-permute-done.30.refs_0_
  168.0 1.7 %apply.1 = (f32[128,5120]{1,0:T(8,128)}, f32[1,5120]{1,0:T(1,128)S(1)}, f32[32,128]{1,0:T(8,128)S(1)}) custom-call(f32[128,5120]{1,0:T(8,128)S(1)} %bitcast.5, f32[1,5120]{1,0:T(1,128)S(1)} %get-tuple-element.77.col_ref, f32[1,128]{1,0:T(1,128)S(1)} %get-tuple-element.78.mean_ref, f32[32,5120]{1,0:T(8,128)S(1)} %get-tuple-element.55.grad_ref.refs_0_, ...), custom_call_target="tpu_custom_call" | custom-call | flops 1966080 | bytes 5898240 | tf_op jit(solution)/shard_map/apply/pallas_call | solution.py:379
  169.8 3.3 %collective-permute-done.33.refs_1_ = f32[32,5120]{1,0:T(8,128)S(1)} collective-permute-done((f32[32,5120]{1,0:T(8,128)S(1)}, f32[32,5120]{1,0:T(8,128)S(1)}, u32[]{:S(2)}, u32[]{:S(2)}) %collective-permute-start.33) | collective-permute-done | bytes 655392 | tf_op jit(solution)/shard_map/ppermute | solution.py:520
  (88 shorter events, 24.0 us)
Async XLA Ops:
  0.7 18.2 %collective-permute-start = (f32[32,5120]{1,0:T(8,128)S(1)}, f32[32,5120]{1,0:T(8,128)S(1)}, u32[]{:S(2)}, u32[]{:S(2)}) collective-permute-start(f32[32,5120]{1,0:T(8,128)S(1)} %fetch.3), channel_id=1, source_target_pairs={{0,8},{8,0},{16,24},{24,16},{1,9},{9,1},{17,25},{25,17},{2,10},{10... | collective-permute-start | bytes 1966088 | tf_op jit(solution)/shard_map/ppermute | solution.py:510
  3.4 29.5 %collective-permute-start.4 = (f32[32,5120]{1,0:T(8,128)S(1)}, f32[32,5120]{1,0:T(8,128)S(1)}, u32[]{:S(2)}, u32[]{:S(2)}) collective-permute-start(f32[32,5120]{1,0:T(8,128)S(1)} %fetch.2.refs_0_), channel_id=1, source_target_pairs={{0,8},{24,16},{1,9},{25,17},{2,10},{26,18},{3,11},{27,19},{4,12},{... | collective-permute-start | bytes 1966088 | tf_op jit(solution)/shard_map/ppermute | solution.py:510
  19.0 17.0 %collective-permute-start.1 = (f32[32,5120]{1,0:T(8,128)S(1)}, f32[32,5120]{1,0:T(8,128)S(1)}, u32[]{:S(2)}, u32[]{:S(2)}) collective-permute-start(f32[32,5120]{1,0:T(8,128)S(1)} %block.16), channel_id=1, source_target_pairs={{8,16},{16,8},{9,17},{17,9},{10,18},{18,10},{11,19},{19,11},{12,20... | collective-permute-start | bytes 1966088 | tf_op jit(solution)/shard_map/ppermute | solution.py:501
  21.0 26.0 %collective-permute-start.12 = (f32[32,5120]{1,0:T(8,128)S(1)}, f32[32,5120]{1,0:T(8,128)S(1)}, u32[]{:S(2)}, u32[]{:S(2)}) collective-permute-start(f32[32,5120]{1,0:T(8,128)S(1)} %block.24), channel_id=1, source_target_pairs={{0,8},{24,16},{1,9},{25,17},{2,10},{26,18},{3,11},{27,19},{4,12},{... | collective-permute-start | bytes 1966088 | tf_op jit(solution)/shard_map/ppermute | solution.py:510
  33.0 17.0 %collective-permute-start.5 = (f32[32,5120]{1,0:T(8,128)S(1)}, f32[32,5120]{1,0:T(8,128)S(1)}, u32[]{:S(2)}, u32[]{:S(2)}) collective-permute-start(f32[32,5120]{1,0:T(8,128)S(1)} %block.19), channel_id=1, source_target_pairs={{8,16},{16,8},{9,17},{17,9},{10,18},{18,10},{11,19},{19,11},{12,20... | collective-permute-start | bytes 1966088 | tf_op jit(solution)/shard_map/ppermute | solution.py:501
  36.0 25.0 %collective-permute-start.2 = (f32[32,5120]{1,0:T(8,128)S(1)}, f32[32,5120]{1,0:T(8,128)S(1)}, u32[]{:S(2)}, u32[]{:S(2)}) collective-permute-start(f32[32,5120]{1,0:T(8,128)S(1)} %block.17), channel_id=1, source_target_pairs={{0,8},{8,0},{16,24},{24,16},{1,9},{9,1},{17,25},{25,17},{2,10},{10... | collective-permute-start | bytes 1966088 | tf_op jit(solution)/shard_map/ppermute | solution.py:510
  47.1 17.7 %collective-permute-start.13 = (f32[32,5120]{1,0:T(8,128)S(1)}, f32[32,5120]{1,0:T(8,128)S(1)}, u32[]{:S(2)}, u32[]{:S(2)}) collective-permute-start(f32[32,5120]{1,0:T(8,128)S(1)} %block.25), channel_id=1, source_target_pairs={{8,16},{16,8},{9,17},{17,9},{10,18},{18,10},{11,19},{19,11},{12,20... | collective-permute-start | bytes 1966088 | tf_op jit(solution)/shard_map/ppermute | solution.py:501
  50.1 25.0 %collective-permute-start.6 = (f32[32,5120]{1,0:T(8,128)S(1)}, f32[32,5120]{1,0:T(8,128)S(1)}, u32[]{:S(2)}, u32[]{:S(2)}) collective-permute-start(f32[32,5120]{1,0:T(8,128)S(1)} %block.20), channel_id=1, source_target_pairs={{0,8},{8,0},{16,24},{24,16},{1,9},{9,1},{17,25},{25,17},{2,10},{10... | collective-permute-start | bytes 1966088 | tf_op jit(solution)/shard_map/ppermute | solution.py:510
  61.1 17.6 %collective-permute-start.3 = (f32[32,5120]{1,0:T(8,128)S(1)}, f32[32,5120]{1,0:T(8,128)S(1)}, u32[]{:S(2)}, u32[]{:S(2)}) collective-permute-start(f32[32,5120]{1,0:T(8,128)S(1)} %block.18), channel_id=1, source_target_pairs={{8,16},{16,8},{9,17},{17,9},{10,18},{18,10},{11,19},{19,11},{12,20... | collective-permute-start | bytes 1966088 | tf_op jit(solution)/shard_map/ppermute | solution.py:501
  64.9 24.3 %collective-permute-start.14 = (f32[32,5120]{1,0:T(8,128)S(1)}, f32[32,5120]{1,0:T(8,128)S(1)}, u32[]{:S(2)}, u32[]{:S(2)}) collective-permute-start(f32[32,5120]{1,0:T(8,128)S(1)} %block.26), channel_id=1, source_target_pairs={{0,8},{8,0},{16,24},{24,16},{1,9},{9,1},{17,25},{25,17},{2,10},{10... | collective-permute-start | bytes 1966088 | tf_op jit(solution)/shard_map/ppermute | solution.py:510
  75.1 17.6 %collective-permute-start.11 = (f32[32,5120]{1,0:T(8,128)S(1)}, f32[32,5120]{1,0:T(8,128)S(1)}, u32[]{:S(2)}, u32[]{:S(2)}) collective-permute-start(f32[32,5120]{1,0:T(8,128)S(1)} %block.23), channel_id=1, source_target_pairs={{8,16},{16,8},{9,17},{17,9},{10,18},{18,10},{11,19},{19,11},{12,20... | collective-permute-start | bytes 1966088 | tf_op jit(solution)/shard_map/ppermute | solution.py:501
  77.3 1.2 collective-permute-start.7
  78.8 24.4 %collective-permute-start.9 = (f32[32,5120]{1,0:T(8,128)S(1)}, f32[32,5120]{1,0:T(8,128)S(1)}, u32[]{:S(2)}, u32[]{:S(2)}) collective-permute-start(f32[32,5120]{1,0:T(8,128)S(1)} %block.21), channel_id=1, source_target_pairs={{0,8},{8,0},{16,24},{24,16},{1,9},{9,1},{17,25},{25,17},{2,10},{10... | collective-permute-start | bytes 1966088 | tf_op jit(solution)/shard_map/ppermute | solution.py:510
  89.2 17.6 %collective-permute-start.22 = (f32[32,5120]{1,0:T(8,128)S(1)}, f32[32,5120]{1,0:T(8,128)S(1)}, u32[]{:S(2)}, u32[]{:S(2)}) collective-permute-start(f32[32,5120]{1,0:T(8,128)S(1)} %block.30), channel_id=1, source_target_pairs={{8,16},{16,8},{9,17},{17,9},{10,18},{18,10},{11,19},{19,11},{12,20... | collective-permute-start | bytes 1966088 | tf_op jit(solution)/shard_map/ppermute | solution.py:501
  91.3 1.2 collective-permute-start.15
  92.8 24.4 %collective-permute-start.16 = (f32[32,5120]{1,0:T(8,128)S(1)}, f32[32,5120]{1,0:T(8,128)S(1)}, u32[]{:S(2)}, u32[]{:S(2)}) collective-permute-start(f32[32,5120]{1,0:T(8,128)S(1)} %block.27), channel_id=1, source_target_pairs={{0,8},{8,0},{16,24},{24,16},{1,9},{9,1},{17,25},{25,17},{2,10},{10... | collective-permute-start | bytes 1966088 | tf_op jit(solution)/shard_map/ppermute | solution.py:510
  103.2 17.0 %collective-permute-start.10 = (f32[32,5120]{1,0:T(8,128)S(1)}, f32[32,5120]{1,0:T(8,128)S(1)}, u32[]{:S(2)}, u32[]{:S(2)}) collective-permute-start(f32[32,5120]{1,0:T(8,128)S(1)} %block.22), channel_id=1, source_target_pairs={{8,16},{16,8},{9,17},{17,9},{10,18},{18,10},{11,19},{19,11},{12,20... | collective-permute-start | bytes 1966088 | tf_op jit(solution)/shard_map/ppermute | solution.py:501
  105.3 1.2 collective-permute-start.18
  106.9 24.4 %collective-permute-start.23 = (f32[32,5120]{1,0:T(8,128)S(1)}, f32[32,5120]{1,0:T(8,128)S(1)}, u32[]{:S(2)}, u32[]{:S(2)}) collective-permute-start(f32[32,5120]{1,0:T(8,128)S(1)} %block.31), channel_id=1, source_target_pairs={{0,8},{8,0},{16,24},{24,16},{1,9},{9,1},{17,25},{25,17},{2,10},{10... | collective-permute-start | bytes 1966088 | tf_op jit(solution)/shard_map/ppermute | solution.py:510
  117.4 2.1 %collective-permute-start.17 = (f32[32,128]{1,0:T(8,128)S(1)}, f32[32,128]{1,0:T(8,128)S(1)}, u32[]{:S(2)}, u32[]{:S(2)}) collective-permute-start(f32[32,128]{1,0:T(8,128)S(1)} %get-tuple-element.61.refs_0_), channel_id=1, source_target_pairs={{0,1},{1,0},{2,3},{3,2},{4,5},{5,4},{6,7},{7,6},{8,9},{9,8},{10,11... | collective-permute-start | bytes 49160 | tf_op jit(solution)/shard_map/ppermute | solution.py:37
  117.6 29.9 %collective-permute-start.20 = (f32[32,5120]{1,0:T(8,128)S(1)}, f32[32,5120]{1,0:T(8,128)S(1)}, u32[]{:S(2)}, u32[]{:S(2)}) collective-permute-start(f32[32,5120]{1,0:T(8,128)S(1)} %block.29), channel_id=1, source_target_pairs={{8,16},{16,8},{9,17},{17,9},{10,18},{18,10},{11,19},{19,11},{12,20... | collective-permute-start | bytes 1966088 | tf_op jit(solution)/shard_map/ppermute | solution.py:501
  120.3 27.1 %collective-permute-start.19 = (f32[32,5120]{1,0:T(8,128)S(1)}, f32[32,5120]{1,0:T(8,128)S(1)}, u32[]{:S(2)}, u32[]{:S(2)}) collective-permute-start(f32[32,5120]{1,0:T(8,128)S(1)} %block.28), channel_id=1, source_target_pairs={{0,8},{8,0},{16,24},{24,16},{1,9},{9,1},{17,25},{25,17},{2,10},{10... | collective-permute-start | bytes 1966088 | tf_op jit(solution)/shard_map/ppermute | solution.py:510
  131.5 1.2 collective-permute-start.24
  132.9 3.8 %collective-permute-start.25 = (f32[1,5120]{1,0:T(1,128)S(1)}, f32[1,5120]{1,0:T(1,128)S(1)}, u32[]{:S(2)}, u32[]{:S(2)}) collective-permute-start(f32[1,5120]{1,0:T(1,128)S(1)} %half.1), channel_id=1, source_target_pairs={{0,2},{2,0},{4,6},{6,4},{1,3},{3,1},{5,7},{7,5},{8,10},{10,8},{12,... | collective-permute-start | bytes 61448 | tf_op jit(solution)/shard_map/ppermute | solution.py:515
  136.8 8.9 %collective-permute-start.26 = (f32[1,5504]{1,0:T(1,128)S(1)}, f32[1,5504]{1,0:T(1,128)S(1)}, u32[]{:S(2)}, u32[]{:S(2)}) collective-permute-start(f32[1,5504]{1,0:T(1,128)S(1)} %joined.1), channel_id=1, source_target_pairs={{0,8},{24,16},{1,9},{25,17},{2,10},{26,18},{3,11},{27,19},{4,12},{... | collective-permute-start | bytes 66056 | tf_op jit(solution)/shard_map/ppermute | solution.py:516
  138.2 29.3 %collective-permute-start.31 = (f32[32,5120]{1,0:T(8,128)S(1)}, f32[32,5120]{1,0:T(8,128)S(1)}, u32[]{:S(2)}, u32[]{:S(2)}) collective-permute-start(f32[32,5120]{1,0:T(8,128)S(1)} %pass.2.refs_0_), channel_id=1, source_target_pairs={{0,8},{24,16},{1,9},{25,17},{2,10},{26,18},{3,11},{27,19},{4,12},{... | collective-permute-start | bytes 1966088 | tf_op jit(solution)/shard_map/ppermute | solution.py:519
  145.8 27.2 %collective-permute-start.33 = (f32[32,5120]{1,0:T(8,128)S(1)}, f32[32,5120]{1,0:T(8,128)S(1)}, u32[]{:S(2)}, u32[]{:S(2)}) collective-permute-start(f32[32,5120]{1,0:T(8,128)S(1)} %pass.3), channel_id=1, source_target_pairs={{0,8},{24,16},{1,9},{25,17},{2,10},{26,18},{3,11},{27,19},{4,12},{... | collective-permute-start | bytes 1966088 | tf_op jit(solution)/shard_map/ppermute | solution.py:520
  147.6 1.2 collective-permute-start.21
  149.1 4.1 %collective-permute-start.27 = (f32[1,10368]{1,0:T(1,128)S(1)}, f32[1,10368]{1,0:T(1,128)S(1)}, u32[]{:S(2)}, u32[]{:S(2)}) collective-permute-start(f32[1,10368]{1,0:T(1,128)S(1)} %get-tuple-element.76), channel_id=1, source_target_pairs={{0,2},{2,0},{4,6},{6,4},{1,3},{3,1},{5,7},{7,5},{8,10},{10,8},{12,... | collective-permute-start | bytes 124424 | tf_op jit(solution)/shard_map/ppermute | solution.py:30
  153.2 4.1 %collective-permute-start.28 = (f32[1,10368]{1,0:T(1,128)S(1)}, f32[1,10368]{1,0:T(1,128)S(1)}, u32[]{:S(2)}, u32[]{:S(2)}) collective-permute-start(f32[1,10368]{1,0:T(1,128)S(1)} %add.9), channel_id=1, source_target_pairs={{0,4},{2,6},{4,0},{6,2},{1,5},{3,7},{5,1},{7,3},{8,12},{10,14},{12... | collective-permute-start | bytes 124424 | tf_op jit(solution)/shard_map/ppermute | solution.py:30
  157.4 5.9 %collective-permute-start.29 = (f32[1,10368]{1,0:T(1,128)S(1)}, f32[1,10368]{1,0:T(1,128)S(1)}, u32[]{:S(2)}, u32[]{:S(2)}) collective-permute-start(f32[1,10368]{1,0:T(1,128)S(1)} %add.10), channel_id=1, source_target_pairs={{8,16},{16,8},{9,17},{17,9},{10,18},{18,10},{11,19},{19,11},{12,20... | collective-permute-start | bytes 124424 | tf_op jit(solution)/shard_map/ppermute | solution.py:523
  163.3 3.0 %collective-permute-start.30 = (f32[1,10368]{1,0:T(1,128)S(1)}, f32[1,10368]{1,0:T(1,128)S(1)}, u32[]{:S(2)}, u32[]{:S(2)}) collective-permute-start(f32[1,10368]{1,0:T(1,128)S(1)} %add.11.sums_ref), channel_id=1, source_target_pairs={{8,0},{16,24},{9,1},{17,25},{10,2},{18,26},{11,3},{19,27},{12,4},{... | collective-permute-start | bytes 124424 | tf_op jit(solution)/shard_map/ppermute | solution.py:524
  (5 other events, 48.4 us)

commit v8 on v7

--- a/solution.py
+++ b/solution.py
@@ -507,7 +507,7 @@
         else:
             tokens = [P[0]] if slot == 2 else sums[-2:-1]
             operand = block_sum(staged, table, arrived, tokens, rows)
-        P[slot] = lax.ppermute(operand, "dp", outward if slot in (1, 2) else swap)
+        P[slot] = lax.ppermute(operand, "dp", outward if slot in (1, 2, 9) else swap)
         if 3 <= slot <= 8:
             settle(slot)
     cols = grad.shape[1]

time: 174 us -> 175 us (level)
  waiting for transfers between devices: 129 us -> 127 us
where the time goes in v8:
time: 175 us; the launch traced here: 174 us
  waiting for transfers between devices  127 us (73%)
  starting transfers between devices  34.8 us (20%)
  Pallas kernels  10.4 us (6%)
    ppermute x10, waiting for transfers between devices, short_line(): lax.ppermute(operand, 'dp', outward if slot in (1, 2, 9) else swap)  94.8 us
    ppermute x8, starting transfers between devices, short_line(): M[slot] = lax.ppermute(operand, 'dp', middle)  15.4 us
    ppermute x8, waiting for transfers between devices, other_parts(): lax.ppermute(values, axis, [(i, (i + k) % size) for i in range(size)])  7.52 us
    ppermute x10, starting transfers between devices, short_line(): lax.ppermute(operand, 'dp', outward if slot in (1, 2, 9) else swap)  6.92 us
    ppermute x1, waiting for transfers between devices, short_line(): early = lax.ppermute(joined_half(sums[-1], received, cols), 'dp', outward)  6.29 us
    ppermute x2, waiting for transfers between devices, axis_sum(): values = values + lax.ppermute(values, axis, pairs)  5 us
    ppermute x1, waiting for transfers between devices, short_line(): total = total + lax.ppermute(total, 'dp', middle)  3.97 us
  transfers between devices with their start and end apart: 34, of which 26 were waited for; matrix products, arithmetic and copies ran while one was open for 0% of the time, Pallas kernels for 5%

profile of v8, /device:TPU:16, one launch (start us, length us, event | category | flops | bytes accessed | tf_op | source)
XLA Modules:
  0.0 174.0 jit_solution(5172869284295977776)
XLA Ops:
  0.7 2.6 %collective-permute-start = (f32[32,5120]{1,0:T(8,128)S(1)}, f32[32,5120]{1,0:T(8,128)S(1)}, u32[]{:S(2)}, u32[]{:S(2)}) collective-permute-start(f32[32,5120]{1,0:T(8,128)S(1)} %fetch.3), channel_id=1, source_target_pairs={{0,8},{8,0},{16,24},{24,16},{1,9},{9,1},{17,25},{25,17},{2,10},{10... | collective-permute-start | bytes 1966088 | tf_op jit(solution)/shard_map/ppermute | solution.py:510
  4.7 2.5 %stage.1.grad_ref = bf16[512,5120]{1,0:T(8,128)(2,1)S(1)} custom-call(bf16[512,5120]{1,0:T(8,128)(2,1)} %bitcast.9, f32[32,5120]{1,0:T(8,128)S(1)} %fetch.2.refs_0_), custom_call_target="tpu_custom_call" | custom-call | bytes 5242880 | tf_op jit(solution)/shard_map/stage/pallas_call | solution.py:76
  7.2 11.7 %collective-permute-done.refs_0_ = f32[32,5120]{1,0:T(8,128)S(1)} collective-permute-done((f32[32,5120]{1,0:T(8,128)S(1)}, f32[32,5120]{1,0:T(8,128)S(1)}, u32[]{:S(2)}, u32[]{:S(2)}) %collective-permute-start) | collective-permute-done | bytes 655392 | tf_op jit(solution)/shard_map/ppermute | solution.py:510
  19.0 1.9 %collective-permute-start.1 = (f32[32,5120]{1,0:T(8,128)S(1)}, f32[32,5120]{1,0:T(8,128)S(1)}, u32[]{:S(2)}, u32[]{:S(2)}) collective-permute-start(f32[32,5120]{1,0:T(8,128)S(1)} %block.16), channel_id=1, source_target_pairs={{8,16},{16,8},{9,17},{17,9},{10,18},{18,10},{11,19},{19,11},{12,20... | collective-permute-start | bytes 1966088 | tf_op jit(solution)/shard_map/ppermute | solution.py:501
  22.3 10.7 %collective-permute-done.4.refs_0_ = f32[32,5120]{1,0:T(8,128)S(1)} collective-permute-done((f32[32,5120]{1,0:T(8,128)S(1)}, f32[32,5120]{1,0:T(8,128)S(1)}, u32[]{:S(2)}, u32[]{:S(2)}) %collective-permute-start.4) | collective-permute-done | bytes 655392 | tf_op jit(solution)/shard_map/ppermute | solution.py:510
  33.0 1.9 %collective-permute-start.5 = (f32[32,5120]{1,0:T(8,128)S(1)}, f32[32,5120]{1,0:T(8,128)S(1)}, u32[]{:S(2)}, u32[]{:S(2)}) collective-permute-start(f32[32,5120]{1,0:T(8,128)S(1)} %block.19), channel_id=1, source_target_pairs={{8,16},{16,8},{9,17},{17,9},{10,18},{18,10},{11,19},{19,11},{12,20... | collective-permute-start | bytes 1966088 | tf_op jit(solution)/shard_map/ppermute | solution.py:501
  36.1 10.9 %collective-permute-done.12.refs_0_ = f32[32,5120]{1,0:T(8,128)S(1)} collective-permute-done((f32[32,5120]{1,0:T(8,128)S(1)}, f32[32,5120]{1,0:T(8,128)S(1)}, u32[]{:S(2)}, u32[]{:S(2)}) %collective-permute-start.12) | collective-permute-done | bytes 655392 | tf_op jit(solution)/shard_map/ppermute | solution.py:510
  47.1 1.9 %collective-permute-start.13 = (f32[32,5120]{1,0:T(8,128)S(1)}, f32[32,5120]{1,0:T(8,128)S(1)}, u32[]{:S(2)}, u32[]{:S(2)}) collective-permute-start(f32[32,5120]{1,0:T(8,128)S(1)} %block.25), channel_id=1, source_target_pairs={{8,16},{16,8},{9,17},{17,9},{10,18},{18,10},{11,19},{19,11},{12,20... | collective-permute-start | bytes 1966088 | tf_op jit(solution)/shard_map/ppermute | solution.py:501
  50.1 10.9 %collective-permute-done.2.refs_0_ = f32[32,5120]{1,0:T(8,128)S(1)} collective-permute-done((f32[32,5120]{1,0:T(8,128)S(1)}, f32[32,5120]{1,0:T(8,128)S(1)}, u32[]{:S(2)}, u32[]{:S(2)}) %collective-permute-start.2) | collective-permute-done | bytes 655392 | tf_op jit(solution)/shard_map/ppermute | solution.py:510
  61.1 1.9 %collective-permute-start.3 = (f32[32,5120]{1,0:T(8,128)S(1)}, f32[32,5120]{1,0:T(8,128)S(1)}, u32[]{:S(2)}, u32[]{:S(2)}) collective-permute-start(f32[32,5120]{1,0:T(8,128)S(1)} %block.18), channel_id=1, source_target_pairs={{8,16},{16,8},{9,17},{17,9},{10,18},{18,10},{11,19},{19,11},{12,20... | collective-permute-start | bytes 1966088 | tf_op jit(solution)/shard_map/ppermute | solution.py:501
  65.0 10.1 %collective-permute-done.6.refs_0_ = f32[32,5120]{1,0:T(8,128)S(1)} collective-permute-done((f32[32,5120]{1,0:T(8,128)S(1)}, f32[32,5120]{1,0:T(8,128)S(1)}, u32[]{:S(2)}, u32[]{:S(2)}) %collective-permute-start.6) | collective-permute-done | bytes 655392 | tf_op jit(solution)/shard_map/ppermute | solution.py:510
  75.1 1.9 %collective-permute-start.11 = (f32[32,5120]{1,0:T(8,128)S(1)}, f32[32,5120]{1,0:T(8,128)S(1)}, u32[]{:S(2)}, u32[]{:S(2)}) collective-permute-start(f32[32,5120]{1,0:T(8,128)S(1)} %block.23), channel_id=1, source_target_pairs={{8,16},{16,8},{9,17},{17,9},{10,18},{18,10},{11,19},{19,11},{12,20... | collective-permute-start | bytes 1966088 | tf_op jit(solution)/shard_map/ppermute | solution.py:501
  78.9 10.3 %collective-permute-done.14.refs_0_ = f32[32,5120]{1,0:T(8,128)S(1)} collective-permute-done((f32[32,5120]{1,0:T(8,128)S(1)}, f32[32,5120]{1,0:T(8,128)S(1)}, u32[]{:S(2)}, u32[]{:S(2)}) %collective-permute-start.14) | collective-permute-done | bytes 655392 | tf_op jit(solution)/shard_map/ppermute | solution.py:510
  89.2 1.9 %collective-permute-start.22 = (f32[32,5120]{1,0:T(8,128)S(1)}, f32[32,5120]{1,0:T(8,128)S(1)}, u32[]{:S(2)}, u32[]{:S(2)}) collective-permute-start(f32[32,5120]{1,0:T(8,128)S(1)} %block.30), channel_id=1, source_target_pairs={{8,16},{16,8},{9,17},{17,9},{10,18},{18,10},{11,19},{19,11},{12,20... | collective-permute-start | bytes 1966088 | tf_op jit(solution)/shard_map/ppermute | solution.py:501
  92.9 10.3 %collective-permute-done.9.refs_0_ = f32[32,5120]{1,0:T(8,128)S(1)} collective-permute-done((f32[32,5120]{1,0:T(8,128)S(1)}, f32[32,5120]{1,0:T(8,128)S(1)}, u32[]{:S(2)}, u32[]{:S(2)}) %collective-permute-start.9) | collective-permute-done | bytes 655392 | tf_op jit(solution)/shard_map/ppermute | solution.py:510
  103.2 1.9 %collective-permute-start.10 = (f32[32,5120]{1,0:T(8,128)S(1)}, f32[32,5120]{1,0:T(8,128)S(1)}, u32[]{:S(2)}, u32[]{:S(2)}) collective-permute-start(f32[32,5120]{1,0:T(8,128)S(1)} %block.22), channel_id=1, source_target_pairs={{8,16},{16,8},{9,17},{17,9},{10,18},{18,10},{11,19},{19,11},{12,20... | collective-permute-start | bytes 1966088 | tf_op jit(solution)/shard_map/ppermute | solution.py:501
  106.9 10.3 %collective-permute-done.16.refs_0_ = f32[32,5120]{1,0:T(8,128)S(1)} collective-permute-done((f32[32,5120]{1,0:T(8,128)S(1)}, f32[32,5120]{1,0:T(8,128)S(1)}, u32[]{:S(2)}, u32[]{:S(2)}) %collective-permute-start.16) | collective-permute-done | bytes 655392 | tf_op jit(solution)/shard_map/ppermute | solution.py:510
  117.6 1.9 %collective-permute-start.20 = (f32[32,5120]{1,0:T(8,128)S(1)}, f32[32,5120]{1,0:T(8,128)S(1)}, u32[]{:S(2)}, u32[]{:S(2)}) collective-permute-start(f32[32,5120]{1,0:T(8,128)S(1)} %block.29), channel_id=1, source_target_pairs={{8,16},{16,8},{9,17},{17,9},{10,18},{18,10},{11,19},{19,11},{12,20... | collective-permute-start | bytes 1966088 | tf_op jit(solution)/shard_map/ppermute | solution.py:501
  121.6 9.7 %collective-permute-done.23.refs_0_ = f32[32,5120]{1,0:T(8,128)S(1)} collective-permute-done((f32[32,5120]{1,0:T(8,128)S(1)}, f32[32,5120]{1,0:T(8,128)S(1)}, u32[]{:S(2)}, u32[]{:S(2)}) %collective-permute-start.23) | collective-permute-done | bytes 655392 | tf_op jit(solution)/shard_map/ppermute | solution.py:510
  132.9 1.6 collective-permute-start.25
  134.5 2.3 %collective-permute-done.25.received_ref = f32[1,5120]{1,0:T(1,128)S(1)} collective-permute-done((f32[1,5120]{1,0:T(1,128)S(1)}, f32[1,5120]{1,0:T(1,128)S(1)}, u32[]{:S(2)}, u32[]{:S(2)}) %collective-permute-start.25) | collective-permute-done | bytes 20512 | tf_op jit(solution)/shard_map/ppermute | solution.py:515
  139.5 6.3 %collective-permute-done.26.refs_3_.sums_ref.refs_1_ = f32[1,5504]{1,0:T(1,128)S(1)} collective-permute-done((f32[1,5504]{1,0:T(1,128)S(1)}, f32[1,5504]{1,0:T(1,128)S(1)}, u32[]{:S(2)}, u32[]{:S(2)}) %collective-permute-start.26) | collective-permute-done | bytes 22048 | tf_op jit(solution)/shard_map/ppermute | solution.py:516
  145.8 1.6 collective-permute-start.33
  149.1 1.6 collective-permute-start.27
  150.7 2.5 %collective-permute-done.27 = f32[1,10368]{1,0:T(1,128)S(1)} collective-permute-done((f32[1,10368]{1,0:T(1,128)S(1)}, f32[1,10368]{1,0:T(1,128)S(1)}, u32[]{:S(2)}, u32[]{:S(2)}) %collective-permute-start.27) | collective-permute-done | bytes 41504 | tf_op jit(solution)/shard_map/ppermute | solution.py:30
  153.2 1.6 collective-permute-start.28
  154.8 2.5 %collective-permute-done.28 = f32[1,10368]{1,0:T(1,128)S(1)} collective-permute-done((f32[1,10368]{1,0:T(1,128)S(1)}, f32[1,10368]{1,0:T(1,128)S(1)}, u32[]{:S(2)}, u32[]{:S(2)}) %collective-permute-start.28) | collective-permute-done | bytes 41504 | tf_op jit(solution)/shard_map/ppermute | solution.py:30
  157.4 1.9 %collective-permute-start.29 = (f32[1,10368]{1,0:T(1,128)S(1)}, f32[1,10368]{1,0:T(1,128)S(1)}, u32[]{:S(2)}, u32[]{:S(2)}) collective-permute-start(f32[1,10368]{1,0:T(1,128)S(1)} %add.10), channel_id=1, source_target_pairs={{8,16},{16,8},{9,17},{17,9},{10,18},{18,10},{11,19},{19,11},{12,20... | collective-permute-start | bytes 124424 | tf_op jit(solution)/shard_map/ppermute | solution.py:523
  159.3 4.0 %collective-permute-done.29 = f32[1,10368]{1,0:T(1,128)S(1)} collective-permute-done((f32[1,10368]{1,0:T(1,128)S(1)}, f32[1,10368]{1,0:T(1,128)S(1)}, u32[]{:S(2)}, u32[]{:S(2)}) %collective-permute-start.29) | collective-permute-done | bytes 41504 | tf_op jit(solution)/shard_map/ppermute | solution.py:523
  164.6 1.7 collective-permute-done.30.refs_0_
  168.0 1.7 %apply.1 = (f32[128,5120]{1,0:T(8,128)}, f32[1,5120]{1,0:T(1,128)S(1)}, f32[32,128]{1,0:T(8,128)S(1)}) custom-call(f32[128,5120]{1,0:T(8,128)S(1)} %bitcast.5, f32[1,5120]{1,0:T(1,128)S(1)} %get-tuple-element.77.col_ref, f32[1,128]{1,0:T(1,128)S(1)} %get-tuple-element.78.mean_ref, f32[32,5120]{1,0:T(8,128)S(1)} %get-tuple-element.55.grad_ref.refs_0_, ...), custom_call_target="tpu_custom_call" | custom-call | flops 1966080 | bytes 5898240 | tf_op jit(solution)/shard_map/apply/pallas_call | solution.py:379
  169.8 3.3 %collective-permute-done.33.refs_1_ = f32[32,5120]{1,0:T(8,128)S(1)} collective-permute-done((f32[32,5120]{1,0:T(8,128)S(1)}, f32[32,5120]{1,0:T(8,128)S(1)}, u32[]{:S(2)}, u32[]{:S(2)}) %collective-permute-start.33) | collective-permute-done | bytes 655392 | tf_op jit(solution)/shard_map/ppermute | solution.py:520
  (88 shorter events, 25.2 us)
Async XLA Ops:
  0.7 18.2 %collective-permute-start = (f32[32,5120]{1,0:T(8,128)S(1)}, f32[32,5120]{1,0:T(8,128)S(1)}, u32[]{:S(2)}, u32[]{:S(2)}) collective-permute-start(f32[32,5120]{1,0:T(8,128)S(1)} %fetch.3), channel_id=1, source_target_pairs={{0,8},{8,0},{16,24},{24,16},{1,9},{9,1},{17,25},{25,17},{2,10},{10... | collective-permute-start | bytes 1966088 | tf_op jit(solution)/shard_map/ppermute | solution.py:510
  3.4 29.5 %collective-permute-start.4 = (f32[32,5120]{1,0:T(8,128)S(1)}, f32[32,5120]{1,0:T(8,128)S(1)}, u32[]{:S(2)}, u32[]{:S(2)}) collective-permute-start(f32[32,5120]{1,0:T(8,128)S(1)} %fetch.2.refs_0_), channel_id=1, source_target_pairs={{0,8},{24,16},{1,9},{25,17},{2,10},{26,18},{3,11},{27,19},{4,12},{... | collective-permute-start | bytes 1966088 | tf_op jit(solution)/shard_map/ppermute | solution.py:510
  19.0 17.0 %collective-permute-start.1 = (f32[32,5120]{1,0:T(8,128)S(1)}, f32[32,5120]{1,0:T(8,128)S(1)}, u32[]{:S(2)}, u32[]{:S(2)}) collective-permute-start(f32[32,5120]{1,0:T(8,128)S(1)} %block.16), channel_id=1, source_target_pairs={{8,16},{16,8},{9,17},{17,9},{10,18},{18,10},{11,19},{19,11},{12,20... | collective-permute-start | bytes 1966088 | tf_op jit(solution)/shard_map/ppermute | solution.py:501
  21.0 26.0 %collective-permute-start.12 = (f32[32,5120]{1,0:T(8,128)S(1)}, f32[32,5120]{1,0:T(8,128)S(1)}, u32[]{:S(2)}, u32[]{:S(2)}) collective-permute-start(f32[32,5120]{1,0:T(8,128)S(1)} %block.24), channel_id=1, source_target_pairs={{0,8},{24,16},{1,9},{25,17},{2,10},{26,18},{3,11},{27,19},{4,12},{... | collective-permute-start | bytes 1966088 | tf_op jit(solution)/shard_map/ppermute | solution.py:510
  33.0 17.0 %collective-permute-start.5 = (f32[32,5120]{1,0:T(8,128)S(1)}, f32[32,5120]{1,0:T(8,128)S(1)}, u32[]{:S(2)}, u32[]{:S(2)}) collective-permute-start(f32[32,5120]{1,0:T(8,128)S(1)} %block.19), channel_id=1, source_target_pairs={{8,16},{16,8},{9,17},{17,9},{10,18},{18,10},{11,19},{19,11},{12,20... | collective-permute-start | bytes 1966088 | tf_op jit(solution)/shard_map/ppermute | solution.py:501
  36.0 25.0 %collective-permute-start.2 = (f32[32,5120]{1,0:T(8,128)S(1)}, f32[32,5120]{1,0:T(8,128)S(1)}, u32[]{:S(2)}, u32[]{:S(2)}) collective-permute-start(f32[32,5120]{1,0:T(8,128)S(1)} %block.17), channel_id=1, source_target_pairs={{0,8},{8,0},{16,24},{24,16},{1,9},{9,1},{17,25},{25,17},{2,10},{10... | collective-permute-start | bytes 1966088 | tf_op jit(solution)/shard_map/ppermute | solution.py:510
  47.1 17.7 %collective-permute-start.13 = (f32[32,5120]{1,0:T(8,128)S(1)}, f32[32,5120]{1,0:T(8,128)S(1)}, u32[]{:S(2)}, u32[]{:S(2)}) collective-permute-start(f32[32,5120]{1,0:T(8,128)S(1)} %block.25), channel_id=1, source_target_pairs={{8,16},{16,8},{9,17},{17,9},{10,18},{18,10},{11,19},{19,11},{12,20... | collective-permute-start | bytes 1966088 | tf_op jit(solution)/shard_map/ppermute | solution.py:501
  50.1 25.0 %collective-permute-start.6 = (f32[32,5120]{1,0:T(8,128)S(1)}, f32[32,5120]{1,0:T(8,128)S(1)}, u32[]{:S(2)}, u32[]{:S(2)}) collective-permute-start(f32[32,5120]{1,0:T(8,128)S(1)} %block.20), channel_id=1, source_target_pairs={{0,8},{8,0},{16,24},{24,16},{1,9},{9,1},{17,25},{25,17},{2,10},{10... | collective-permute-start | bytes 1966088 | tf_op jit(solution)/shard_map/ppermute | solution.py:510
  61.1 17.6 %collective-permute-start.3 = (f32[32,5120]{1,0:T(8,128)S(1)}, f32[32,5120]{1,0:T(8,128)S(1)}, u32[]{:S(2)}, u32[]{:S(2)}) collective-permute-start(f32[32,5120]{1,0:T(8,128)S(1)} %block.18), channel_id=1, source_target_pairs={{8,16},{16,8},{9,17},{17,9},{10,18},{18,10},{11,19},{19,11},{12,20... | collective-permute-start | bytes 1966088 | tf_op jit(solution)/shard_map/ppermute | solution.py:501
  64.9 24.3 %collective-permute-start.14 = (f32[32,5120]{1,0:T(8,128)S(1)}, f32[32,5120]{1,0:T(8,128)S(1)}, u32[]{:S(2)}, u32[]{:S(2)}) collective-permute-start(f32[32,5120]{1,0:T(8,128)S(1)} %block.26), channel_id=1, source_target_pairs={{0,8},{8,0},{16,24},{24,16},{1,9},{9,1},{17,25},{25,17},{2,10},{10... | collective-permute-start | bytes 1966088 | tf_op jit(solution)/shard_map/ppermute | solution.py:510
  75.1 17.6 %collective-permute-start.11 = (f32[32,5120]{1,0:T(8,128)S(1)}, f32[32,5120]{1,0:T(8,128)S(1)}, u32[]{:S(2)}, u32[]{:S(2)}) collective-permute-start(f32[32,5120]{1,0:T(8,128)S(1)} %block.23), channel_id=1, source_target_pairs={{8,16},{16,8},{9,17},{17,9},{10,18},{18,10},{11,19},{19,11},{12,20... | collective-permute-start | bytes 1966088 | tf_op jit(solution)/shard_map/ppermute | solution.py:501
  77.3 1.2 collective-permute-start.7
  78.8 24.4 %collective-permute-start.9 = (f32[32,5120]{1,0:T(8,128)S(1)}, f32[32,5120]{1,0:T(8,128)S(1)}, u32[]{:S(2)}, u32[]{:S(2)}) collective-permute-start(f32[32,5120]{1,0:T(8,128)S(1)} %block.21), channel_id=1, source_target_pairs={{0,8},{8,0},{16,24},{24,16},{1,9},{9,1},{17,25},{25,17},{2,10},{10... | collective-permute-start | bytes 1966088 | tf_op jit(solution)/shard_map/ppermute | solution.py:510
  89.2 17.6 %collective-permute-start.22 = (f32[32,5120]{1,0:T(8,128)S(1)}, f32[32,5120]{1,0:T(8,128)S(1)}, u32[]{:S(2)}, u32[]{:S(2)}) collective-permute-start(f32[32,5120]{1,0:T(8,128)S(1)} %block.30), channel_id=1, source_target_pairs={{8,16},{16,8},{9,17},{17,9},{10,18},{18,10},{11,19},{19,11},{12,20... | collective-permute-start | bytes 1966088 | tf_op jit(solution)/shard_map/ppermute | solution.py:501
  91.3 1.2 collective-permute-start.15
  92.8 24.4 %collective-permute-start.16 = (f32[32,5120]{1,0:T(8,128)S(1)}, f32[32,5120]{1,0:T(8,128)S(1)}, u32[]{:S(2)}, u32[]{:S(2)}) collective-permute-start(f32[32,5120]{1,0:T(8,128)S(1)} %block.27), channel_id=1, source_target_pairs={{0,8},{8,0},{16,24},{24,16},{1,9},{9,1},{17,25},{25,17},{2,10},{10... | collective-permute-start | bytes 1966088 | tf_op jit(solution)/shard_map/ppermute | solution.py:510
  103.2 17.0 %collective-permute-start.10 = (f32[32,5120]{1,0:T(8,128)S(1)}, f32[32,5120]{1,0:T(8,128)S(1)}, u32[]{:S(2)}, u32[]{:S(2)}) collective-permute-start(f32[32,5120]{1,0:T(8,128)S(1)} %block.22), channel_id=1, source_target_pairs={{8,16},{16,8},{9,17},{17,9},{10,18},{18,10},{11,19},{19,11},{12,20... | collective-permute-start | bytes 1966088 | tf_op jit(solution)/shard_map/ppermute | solution.py:501
  105.3 1.2 collective-permute-start.18
  106.9 24.4 %collective-permute-start.23 = (f32[32,5120]{1,0:T(8,128)S(1)}, f32[32,5120]{1,0:T(8,128)S(1)}, u32[]{:S(2)}, u32[]{:S(2)}) collective-permute-start(f32[32,5120]{1,0:T(8,128)S(1)} %block.31), channel_id=1, source_target_pairs={{0,8},{8,0},{16,24},{24,16},{1,9},{9,1},{17,25},{25,17},{2,10},{10... | collective-permute-start | bytes 1966088 | tf_op jit(solution)/shard_map/ppermute | solution.py:510
  117.4 2.1 %collective-permute-start.17 = (f32[32,128]{1,0:T(8,128)S(1)}, f32[32,128]{1,0:T(8,128)S(1)}, u32[]{:S(2)}, u32[]{:S(2)}) collective-permute-start(f32[32,128]{1,0:T(8,128)S(1)} %get-tuple-element.61.refs_0_), channel_id=1, source_target_pairs={{0,1},{1,0},{2,3},{3,2},{4,5},{5,4},{6,7},{7,6},{8,9},{9,8},{10,11... | collective-permute-start | bytes 49160 | tf_op jit(solution)/shard_map/ppermute | solution.py:37
  117.6 29.9 %collective-permute-start.20 = (f32[32,5120]{1,0:T(8,128)S(1)}, f32[32,5120]{1,0:T(8,128)S(1)}, u32[]{:S(2)}, u32[]{:S(2)}) collective-permute-start(f32[32,5120]{1,0:T(8,128)S(1)} %block.29), channel_id=1, source_target_pairs={{8,16},{16,8},{9,17},{17,9},{10,18},{18,10},{11,19},{19,11},{12,20... | collective-permute-start | bytes 1966088 | tf_op jit(solution)/shard_map/ppermute | solution.py:501
  120.3 27.1 %collective-permute-start.19 = (f32[32,5120]{1,0:T(8,128)S(1)}, f32[32,5120]{1,0:T(8,128)S(1)}, u32[]{:S(2)}, u32[]{:S(2)}) collective-permute-start(f32[32,5120]{1,0:T(8,128)S(1)} %block.28), channel_id=1, source_target_pairs={{0,8},{24,16},{1,9},{25,17},{2,10},{26,18},{3,11},{27,19},{4,12},{... | collective-permute-start | bytes 1966088 | tf_op jit(solution)/shard_map/ppermute | solution.py:510
  131.5 1.2 collective-permute-start.24
  132.9 3.8 %collective-permute-start.25 = (f32[1,5120]{1,0:T(1,128)S(1)}, f32[1,5120]{1,0:T(1,128)S(1)}, u32[]{:S(2)}, u32[]{:S(2)}) collective-permute-start(f32[1,5120]{1,0:T(1,128)S(1)} %half.1), channel_id=1, source_target_pairs={{0,2},{2,0},{4,6},{6,4},{1,3},{3,1},{5,7},{7,5},{8,10},{10,8},{12,... | collective-permute-start | bytes 61448 | tf_op jit(solution)/shard_map/ppermute | solution.py:515
  136.8 8.9 %collective-permute-start.26 = (f32[1,5504]{1,0:T(1,128)S(1)}, f32[1,5504]{1,0:T(1,128)S(1)}, u32[]{:S(2)}, u32[]{:S(2)}) collective-permute-start(f32[1,5504]{1,0:T(1,128)S(1)} %joined.1), channel_id=1, source_target_pairs={{0,8},{24,16},{1,9},{25,17},{2,10},{26,18},{3,11},{27,19},{4,12},{... | collective-permute-start | bytes 66056 | tf_op jit(solution)/shard_map/ppermute | solution.py:516
  138.2 29.3 %collective-permute-start.31 = (f32[32,5120]{1,0:T(8,128)S(1)}, f32[32,5120]{1,0:T(8,128)S(1)}, u32[]{:S(2)}, u32[]{:S(2)}) collective-permute-start(f32[32,5120]{1,0:T(8,128)S(1)} %pass.2.refs_0_), channel_id=1, source_target_pairs={{0,8},{24,16},{1,9},{25,17},{2,10},{26,18},{3,11},{27,19},{4,12},{... | collective-permute-start | bytes 1966088 | tf_op jit(solution)/shard_map/ppermute | solution.py:519
  145.8 27.2 %collective-permute-start.33 = (f32[32,5120]{1,0:T(8,128)S(1)}, f32[32,5120]{1,0:T(8,128)S(1)}, u32[]{:S(2)}, u32[]{:S(2)}) collective-permute-start(f32[32,5120]{1,0:T(8,128)S(1)} %pass.3), channel_id=1, source_target_pairs={{0,8},{24,16},{1,9},{25,17},{2,10},{26,18},{3,11},{27,19},{4,12},{... | collective-permute-start | bytes 1966088 | tf_op jit(solution)/shard_map/ppermute | solution.py:520
  147.6 1.2 collective-permute-start.21
  149.1 4.1 %collective-permute-start.27 = (f32[1,10368]{1,0:T(1,128)S(1)}, f32[1,10368]{1,0:T(1,128)S(1)}, u32[]{:S(2)}, u32[]{:S(2)}) collective-permute-start(f32[1,10368]{1,0:T(1,128)S(1)} %get-tuple-element.76), channel_id=1, source_target_pairs={{0,2},{2,0},{4,6},{6,4},{1,3},{3,1},{5,7},{7,5},{8,10},{10,8},{12,... | collective-permute-start | bytes 124424 | tf_op jit(solution)/shard_map/ppermute | solution.py:30
  153.2 4.1 %collective-permute-start.28 = (f32[1,10368]{1,0:T(1,128)S(1)}, f32[1,10368]{1,0:T(1,128)S(1)}, u32[]{:S(2)}, u32[]{:S(2)}) collective-permute-start(f32[1,10368]{1,0:T(1,128)S(1)} %add.9), channel_id=1, source_target_pairs={{0,4},{2,6},{4,0},{6,2},{1,5},{3,7},{5,1},{7,3},{8,12},{10,14},{12... | collective-permute-start | bytes 124424 | tf_op jit(solution)/shard_map/ppermute | solution.py:30
  157.4 5.9 %collective-permute-start.29 = (f32[1,10368]{1,0:T(1,128)S(1)}, f32[1,10368]{1,0:T(1,128)S(1)}, u32[]{:S(2)}, u32[]{:S(2)}) collective-permute-start(f32[1,10368]{1,0:T(1,128)S(1)} %add.10), channel_id=1, source_target_pairs={{8,16},{16,8},{9,17},{17,9},{10,18},{18,10},{11,19},{19,11},{12,20... | collective-permute-start | bytes 124424 | tf_op jit(solution)/shard_map/ppermute | solution.py:523
  163.3 3.0 %collective-permute-start.30 = (f32[1,10368]{1,0:T(1,128)S(1)}, f32[1,10368]{1,0:T(1,128)S(1)}, u32[]{:S(2)}, u32[]{:S(2)}) collective-permute-start(f32[1,10368]{1,0:T(1,128)S(1)} %add.11.sums_ref), channel_id=1, source_target_pairs={{8,0},{16,24},{9,1},{17,25},{10,2},{18,26},{11,3},{19,27},{12,4},{... | collective-permute-start | bytes 124424 | tf_op jit(solution)/shard_map/ppermute | solution.py:524
  (5 other events, 48.4 us)
